TPU v7x, 32 devices: a whole 2x2x4 slice. The times are simulated.
32 devices in a mesh: dp: 8 (over z, y), shard: 4 (over x, core).
Axes of the slice: x: 2, y: 2, z: 4, core: 2. Of those that a mesh axis runs over, the one named last changes fastest.
Arguments:
- hidden_acts: bfloat16 [8, 128, 8192], P('dp', None, 'shard'), may hold values from -6 to 6
- out_grad: bfloat16 [8, 128, 1024], P('dp'), may hold values from -0.0546875 to 0.0546875
- token_ids: int32 [8, 128], P('dp'), may hold values from 0 to 255999, as said below
- trigger: int32 [8, 512], P('dp', 'shard'), may hold values 0 or 1
- stale: bfloat16 [8, 8192, 1024], P('dp', 'shard'), may hold values from -0.5 to 0.5
- aggregate_prev: float32 [4, 2048, 1024], P('shard', 'dp'), may hold values from -12 to 12
Outputs:
- aggregate: float32 [4, 2048, 1024], P('shard', 'dp')
- update: float32 [4, 2048, 1024], P('shard', 'dp')
- triggered: float32 [], replicated
Inputs may be any that keep to these rules, and one draw needn't show every extreme that they name: `token_ids`: id 0 marks padding and stands only after all of a worker's other tokens; at least half of each worker's 128 tokens are not padding.
All inputs are finite; a program needn't handle non-finite values. No bound on the sum of `trigger` on one device may be relied on, other than what follows from the above.
Results may differ from a plain program's by a relative error of at most 0.00051.
Values may be sent and summed in bfloat16 or wider, within the bound.
No kernel may reach another device: no remote copies, remote signals or barrier semaphores. Data moves between devices by JAX's collectives and lax.ppermute only.
A program may use at most 64 MiB of HBM per device.

v0:
```python
import jax
import jax.numpy as jnp
from jax import lax
from jax.sharding import PartitionSpec as P

COLS = 1024
HID = 8192
BLOCK = 16


clip_ratio = 0.25
epsilon = 1e-06


def add_sources(received):
    return jnp.sum(received, axis=0, dtype=jnp.float32)


def local(hidden_acts, out_grad, token_ids, trigger, stale, aggregate_prev):
    real_mask = (token_ids[0] != 0).astype(jnp.bfloat16)
    masked = out_grad[0] * real_mask[:, None]
    hidden = hidden_acts[0]
    stale_rows = stale[0]
    row_flags = jnp.repeat(trigger[0], BLOCK).astype(jnp.float32)[:, None]
    owners = lax.axis_size("dp")
    own_rows = aggregate_prev.shape[1]
    width = stale_rows.shape[1]
    local_count = jnp.sum(trigger.astype(jnp.float32))
    triggered = lax.psum(local_count, ("dp", "shard"))
    gradient = lax.dot_general(
        hidden, masked, (((0,), (0,)), ((), ())), preferred_element_type=jnp.float32
    )
    delta = (
        (row_flags * (gradient - stale_rows.astype(jnp.float32)))
        .astype(jnp.bfloat16)
        .reshape(owners, own_rows, width)
    )
    received = lax.all_to_all(delta, "dp", split_axis=0, concat_axis=0, tiled=True)
    summed = add_sources(received)
    aggregate = aggregate_prev[0] + summed
    squares = jnp.sum(aggregate * aggregate)
    square_total = lax.psum(squares, ("dp", "shard"))
    limit = clip_ratio * jnp.sqrt(jnp.asarray(HID * COLS, jnp.float32))
    clip_factor = jnp.minimum(1.0, limit / jnp.sqrt(square_total + epsilon))
    return (aggregate[None], (aggregate * clip_factor)[None], triggered)


def solution(mesh):
    return jax.shard_map(
        local,
        mesh=mesh,
        in_specs=(
            P("dp", None, "shard"),
            P("dp", None, None),
            P("dp", None),
            P("dp", "shard"),
            P("dp", "shard", None),
            P("shard", "dp", None),
        ),
        out_specs=(P("shard", "dp", None), P("shard", "dp", None), P()),
        check_vma=False,
    )
```

profile of v0, /device:TPU:12, one launch (start us, length us, event | category | flops | bytes accessed | tf_op | source)
XLA Modules:
  0.0 163.7 jit_solution(7264303181198848266)
XLA Ops:
  0.6 0.0 copy-start
  0.6 0.0 copy-start.4
  0.7 0.0 copy-start.3
  0.7 0.0 copy-start.2
  0.7 6.6 %copy.11 = bf16[1,2048,1024]{1,2,0:T(8,128)(2,1)} copy(bf16[1,2048,1024]{2,1,0:T(8,128)(2,1)} %param.10) | data formatting | bytes 8388608 | tf_op args[4]
  7.2 0.0 copy-done.4
  7.3 0.1 broadcast_in_dim.2
  7.3 0.1 convert_element_type.39
  7.4 0.0 copy-done.3
  7.4 0.0 copy-done
  7.4 0.0 copy-done.2
  7.5 3.5 %fusion.1 = bf16[2048,1024]{0,1:T(8,128)(2,1)S(1)} fusion(bf16[1,2048,1024]{1,2,0:T(8,128)(2,1)} %copy.11, f32[2048]{0:T(1024)S(1)} %convert_element_type.39, bf16[1,128,2048]{2,1,0:T(8,128)(2,1)S(1)} %copy-done, bf16[1,128,1024]{2,1,0:T(8,128)(2,1)S(1)} %copy-done.2, bf16[128]{0:T(256)(128)(2,1)S(1)} %fusion.8), kind=kOutput, calls=%fused_computation.2 | convolution fusion | flops 545390592 | bytes 9183488 | tf_op jit(solution)/shard_map/dot_general | solution.py:30
  11.0 2.2 %copy.21 = bf16[128,8,8,256]{3,2,0,1:T(8,128)(2,1)} copy(bf16[128,8,8,256]{3,2,1,0:T(8,128)(2,1)S(1)} %bitcast.29) | data formatting | bytes 8388608 | tf_op jit(solution)/shard_map/reshape | solution.py:36
  13.2 0.0 copy-start.1
  13.2 6.4 %all-to-all-start = ((bf16[8,256,1024]{1,2,0:T(8,128)(2,1)}), bf16[8,256,1024]{1,2,0:T(8,128)(2,1)}, u32[]{:S(2)}, u32[]{:S(2)}) async-start(bf16[8,256,1024]{1,2,0:T(8,128)(2,1)} %bitcast.28), calls=%async_computation | async-start | bytes 8388608 | tf_op jit(solution)/shard_map/all_to_all | solution.py:38
  19.6 0.0 copy-done.1
  19.6 0.3 copy.14
  19.9 0.6 convert_reduce_fusion.1
  20.5 89.0 %all-to-all-done = bf16[8,256,1024]{1,2,0:T(8,128)(2,1)} async-done(((bf16[8,256,1024]{1,2,0:T(8,128)(2,1)}), bf16[8,256,1024]{1,2,0:T(8,128)(2,1)}, u32[]{:S(2)}, u32[]{:S(2)}) %all-to-all-start) | async-done | bytes 4194336 | tf_op jit(solution)/shard_map/all_to_all | solution.py:38
  109.5 2.9 %convert_reduce_fusion = f32[256,1024]{0,1:T(8,128)S(1)} fusion(bf16[8,256,1024]{1,2,0:T(8,128)(2,1)} %all-to-all-done), kind=kLoop, calls=%fused_computation.3 | loop fusion | flops 3932160 | bytes 5242880 | tf_op jit(solution)/shard_map/reduce_sum | solution.py:16
  112.4 0.9 fusion.3
  113.3 43.2 %all-reduce = (f32[]{:T(128)}, f32[]{:T(128)}) all-reduce(f32[]{:T(128)} %fusion.3, f32[]{:T(128)} %convert_reduce_fusion.1), channel_id=1, replica_groups=mesh['dp'=8,'shard'=4] {'dp','shard'}, use_global_device_ids=true, to_apply=%region_2.0 | all-reduce | flops 2 | bytes 16 | tf_op jit(solution)/shard_map/psum | solution.py:42
  157.2 1.5 broadcast_multiply_fusion
  158.7 2.5 %copy.16 = f32[1,256,1024]{2,1,0:T(8,128)} copy(f32[1,256,1024]{1,2,0:T(8,128)} %get-tuple-element.9) | data formatting | bytes 2097152
  161.2 2.5 %copy.17 = f32[1,256,1024]{2,1,0:T(8,128)} copy(f32[1,256,1024]{1,2,0:T(8,128)} %get-tuple-element.8) | data formatting | bytes 2097152
  (2 shorter events, 0.0 us)
Async XLA Ops:
  0.6 6.8 %copy-start = (bf16[1,128,2048]{2,1,0:T(8,128)(2,1)S(1)}, bf16[1,128,2048]{2,1,0:T(8,128)(2,1)}, u32[]{:S(2)}) copy-start(bf16[1,128,2048]{2,1,0:T(8,128)(2,1)} %param.6) | copy-start | bytes 1572868
  0.6 6.6 %copy-start.4 = (s32[1,128]{1,0:T(1,128)S(1)}, s32[1,128]{1,0:T(1,128)}, u32[]{:S(2)}) copy-start(s32[1,128]{1,0:T(1,128)} %param.9) | copy-start | bytes 1540
  0.7 6.8 %copy-start.3 = (s32[1,128]{1,0:T(1,128)S(1)}, s32[1,128]{1,0:T(1,128)}, u32[]{:S(2)}) copy-start(s32[1,128]{1,0:T(1,128)} %param.8) | copy-start | bytes 1540
  0.7 6.8 %copy-start.2 = (bf16[1,128,1024]{2,1,0:T(8,128)(2,1)S(1)}, bf16[1,128,1024]{2,1,0:T(8,128)(2,1)}, u32[]{:S(2)}) copy-start(bf16[1,128,1024]{2,1,0:T(8,128)(2,1)} %param.7) | copy-start | bytes 786436
  13.2 6.4 %copy-start.1 = (f32[1,256,1024]{2,1,0:T(8,128)S(1)}, f32[1,256,1024]{2,1,0:T(8,128)}, u32[]{:S(2)}) copy-start(f32[1,256,1024]{2,1,0:T(8,128)} %param.11) | copy-start | bytes 3145732
  13.2 96.3 %all-to-all-start = ((bf16[8,256,1024]{1,2,0:T(8,128)(2,1)}), bf16[8,256,1024]{1,2,0:T(8,128)(2,1)}, u32[]{:S(2)}, u32[]{:S(2)}) async-start(bf16[8,256,1024]{1,2,0:T(8,128)(2,1)} %bitcast.28), calls=%async_computation | async-start | bytes 8388608 | tf_op jit(solution)/shard_map/all_to_all | solution.py:38
where the time goes:
time: 164 us
  waiting for transfers between devices  89 us (54%)
  blocking collectives  43.2 us (26%)
  local copies, waits for them, and re-layouts  14.4 us (9%)
  starting transfers between devices  6.36 us (4%)
  other arithmetic  5.87 us (4%)
  matrix products  3.54 us (2%)
    all_to_all x1, waiting for transfers between devices, local(): lax.all_to_all(delta, 'dp', split_axis=0, concat_axis=0, tiled=True)  89 us
    psum x1, blocking collectives, local(): square_total = lax.psum(squares, ('dp', 'shard'))  43.2 us
    unnamed x14, local copies, waits for them, and re-layouts  12 us
    all_to_all x1, starting transfers between devices, local(): lax.all_to_all(delta, 'dp', split_axis=0, concat_axis=0, tiled=True)  6.36 us
    dot_general x1, matrix products, local(): lax.dot_general(hidden, masked, (((0,), (0,)), ((), ())), preferred_eleme...  3.54 us
  transfers between devices with their start and end apart: 1, of which 1 were waited for; matrix products, arithmetic and copies ran while one was open for 1% of the time, Pallas kernels for 0%

commit v1 on v0

v1 whole, which is shorter than its diff:
```python
import jax
import jax.numpy as jnp
from jax import lax
from jax.experimental import pallas as pl
from jax.experimental.pallas import tpu as pltpu
from jax.sharding import PartitionSpec as P

COLS = 1024
HID = 8192
BLOCK = 16
clip_ratio = 0.25
epsilon = 1e-06
MIB = 1 << 20
STAGES = 3
ROUNDING = 4.8e-4
F32, BF16 = jnp.float32, jnp.bfloat16
VMEM = pl.BlockSpec(memory_space=pltpu.VMEM)
SMEM = pl.BlockSpec(memory_space=pltpu.SMEM)
HBM = pl.BlockSpec(memory_space=pltpu.HBM)

A0, A1, A, B = (0, 7), (7, 6), (0, 13), (13, 3)
RAW = (
    ("y6a", 1, ((6, A0),)),
    ("y4a", 1, ((4, A0),)),
    ("zb0", 2, ((5, B), (4, B))),
    ("y6b", 1, ((6, A1),)),
    ("zb1", 2, ((1, B), (0, B))),
    ("y4b", 1, ((4, A1),)),
    ("y2a", 1, ((2, A0),)),
    ("y2b", 1, ((2, A1),)),
    ("y0", 1, ((0, A),)),
)
OWN = ((6, A0), (5, B), (4, A0), (4, B), (6, A1), (4, A1), (1, B), (2, A0), (2, A1), (0, A), (0, B))
SUMS = (
    ("near0", 2, (6, A0), (("y6a", 0),), 0),
    ("pairb5", 1, (5, B), (("zb0", 0),), 0),
    ("quad0", 4, (4, A0), (("y4a", 0), ("near0", 0)), 1),
    ("near1", 2, (6, A1), (("y6b", 0),), 0),
    ("pairb1", 1, (1, B), (("zb1", 0),), 2),
    ("quadb", 4, (4, B), (("zb0", 1), ("pairb5", 0)), 1),
    ("quad1", 4, (4, A1), (("y4b", 0), ("near1", 0)), 1),
    ("last0", 2, (2, A0), (("y2a", 0),), 2),
    ("last1", 2, (2, A1), (("y2b", 0),), 2),
)
FINAL = (
    (A0, (0, A), 0, (("y0", 0), ("last0", 0), ("quad0", 0))),
    (A1, (0, A), 7, (("y0", 7), ("last1", 0), ("quad1", 0))),
    (B, (0, B), 0, (("zb1", 3), ("pairb1", 0), ("quadb", 0))),
)


def fold(x):
    sq = x * x
    total = jnp.zeros((8, 128), F32)
    for c in range(0, x.shape[1], 128):
        for r in range(0, x.shape[0], 8):
            total = total + sq[r : r + 8, c : c + 128]
    return total


def deltas(me, trig, tok, acts, og, stale, messages, chunk, limit):
    tokens, width = og.shape[1], og.shape[2]
    unit = chunk // 16
    pieces = [(i, m, r) for i, message in enumerate(messages) for m, r in message]
    masks = list(dict.fromkeys(m for _, m, _ in pieces))
    heights = [sum(r[1] for _, r in message) * unit for message in messages]
    total = sum(heights)
    n_out = len(messages)

    def kernel(me_ref, trig_ref, tok_ref, acts_hbm, og_hbm, stale_hbm, *refs):
        outs = refs[:n_out]
        acts_buf, og_buf, stale_buf, sem = refs[n_out:]
        start = {m: pl.multiple_of((me_ref[0] ^ m) * chunk, chunk) for m in masks}
        og_copy = pltpu.make_async_copy(og_hbm.at[0], og_buf, sem.at[0])
        act_copies, stale_copies = {}, []
        for j, m in enumerate(masks):
            act_copies[m] = pltpu.make_async_copy(
                acts_hbm.at[0, :, pl.ds(start[m], chunk)], acts_buf.at[j], sem.at[1 + j]
            )
        at = 0
        for j, (_, m, (first, count)) in enumerate(pieces):
            rows = pl.ds(pl.multiple_of(start[m] + first * unit, unit), count * unit)
            stale_copies.append(
                pltpu.make_async_copy(
                    stale_hbm.at[0, rows, :], stale_buf.at[pl.ds(at, count * unit), :], sem.at[1 + len(masks) + j]
                )
            )
            at += count * unit
        act_copies[masks[0]].start()
        og_copy.start()
        begun = {masks[0]}
        for j, (_, m, _) in enumerate(pieces):
            if m not in begun:
                act_copies[m].start()
                begun.add(m)
            stale_copies[j].start()
        real = (tok_ref[...] != 0).astype(BF16)
        weights = {}
        at, offset, last = 0, 0, -1
        for j, (i, m, (first, count)) in enumerate(pieces):
            offset = 0 if i != last else offset
            last = i
            if m not in weights:
                act_copies[m].wait()
                weights[m] = acts_buf[masks.index(m)].T * real
            if j == 0:
                og_copy.wait()
            part = weights[m][first * unit : (first + count) * unit]
            gradient = jnp.dot(part, og_buf[...], preferred_element_type=F32)
            stale_copies[j].wait()
            for b in range(0, count * unit, BLOCK):
                flag = trig_ref[(start[m] + first * unit + b) // BLOCK].astype(F32)
                old = stale_buf[at + b : at + b + BLOCK, :].astype(F32)
                outs[i][offset + b : offset + b + BLOCK, :] = (flag * (gradient[b : b + BLOCK] - old)).astype(BF16)
            at += count * unit
            offset += count * unit

    return pl.pallas_call(
        kernel,
        out_shape=tuple(jax.ShapeDtypeStruct((h, width), BF16) for h in heights),
        in_specs=[SMEM, SMEM, VMEM] + [HBM] * 3,
        out_specs=tuple(VMEM for _ in messages),
        scratch_shapes=[
            pltpu.VMEM((len(masks), tokens, chunk), BF16),
            pltpu.VMEM((tokens, width), BF16),
            pltpu.VMEM((total, width), BF16),
            pltpu.SemaphoreType.DMA((1 + len(masks) + len(pieces),)),
        ],
        cost_estimate=pl.CostEstimate(
            flops=2 * tokens * total * width, bytes_accessed=total * width * 4, transcendentals=0
        ),
        compiler_params=pltpu.CompilerParams(vmem_limit_bytes=limit),
    )(me, trig, tok, acts, og, stale)


def add_round(parts, rows):
    width = parts[0][0].shape[1]

    def kernel(*refs):
        out, lost = refs[-2:]
        energy = jnp.zeros((8, 128), F32)
        for r in range(0, rows, BLOCK):
            total = jnp.zeros((BLOCK, width), F32)
            for ref, (_, at) in zip(refs, parts):
                total = total + ref[at + r : at + r + BLOCK, :].astype(F32)
            rounded = total.astype(BF16)
            out[r : r + BLOCK, :] = rounded
            energy = energy + fold(total - rounded.astype(F32))
        lost[...] = energy

    return pl.pallas_call(
        kernel,
        out_shape=(jax.ShapeDtypeStruct((rows, width), BF16), jax.ShapeDtypeStruct((8, 128), F32)),
        in_specs=[VMEM] * len(parts),
        out_specs=(VMEM, VMEM),
        cost_estimate=pl.CostEstimate(flops=rows * width * 6, bytes_accessed=rows * width * 6, transcendentals=0),
        compiler_params=pltpu.CompilerParams(vmem_limit_bytes=12 * MIB),
    )(*[x for x, _ in parts])


def finish(prev, groups, lost, trig):
    arrays = {id(x): x for _, addends in groups for x, _ in addends}
    keys = list(arrays)
    flat = [x for group in lost for x in group]
    n_arrays, n_lost = len(keys), len(flat)

    def kernel(trig_ref, prev_ref, *refs):
        lost_refs = list(refs[n_arrays : n_arrays + n_lost])
        agg, kept, sums, sem = refs[n_arrays + n_lost :]
        total = jnp.zeros((8, 128), F32)
        copies = []
        for g, ((first, rows), addends) in enumerate(groups):
            for r in range(0, rows, BLOCK):
                a = prev_ref[0, first + r : first + r + BLOCK, :]
                for x, at in addends:
                    a = a + refs[keys.index(id(x))][at + r : at + r + BLOCK, :].astype(F32)
                kept[0, first + r : first + r + BLOCK, :] = a
                total = total + fold(a)
            span = pl.ds(first, rows)
            copies.append(pltpu.make_async_copy(kept.at[:, span], agg.at[:, span], sem.at[g]))
            copies[-1].start()
        hits = trig_ref[...].astype(F32)
        row = lax.broadcasted_iota(jnp.int32, (8, 128), 0)
        lane = lax.broadcasted_iota(jnp.int32, (8, 128), 1)
        stacked = jnp.where(row == 0, jnp.sum(total, axis=0, keepdims=True), jnp.where(row == 1, hits, 0.0))
        for i, group in enumerate(lost):
            tile = sum(lost_refs.pop(0)[...] for _ in group)
            stacked = jnp.where(row == 2 + i, jnp.sum(tile, axis=0, keepdims=True), stacked)
        values = jnp.sum(stacked, axis=1, keepdims=True)
        line = jnp.sum(jnp.where(row == lane, values, 0.0), axis=0, keepdims=True)
        sums[...] = jnp.broadcast_to(line[None], sums.shape)
        for c in copies:
            c.wait()

    n = lax.axis_size("dp") * lax.axis_size("shard")
    whole = jax.ShapeDtypeStruct(prev.shape, F32)
    return pl.pallas_call(
        kernel,
        out_shape=(whole, whole, jax.ShapeDtypeStruct((n, 1, 128), F32)),
        in_specs=[VMEM] * (2 + n_arrays + n_lost),
        out_specs=(HBM, VMEM, VMEM),
        scratch_shapes=[pltpu.SemaphoreType.DMA((len(groups),))],
        compiler_params=pltpu.CompilerParams(vmem_limit_bytes=12 * MIB),
        name="finish",
    )(trig, prev, *arrays.values(), *flat)


def scale(agg, gathered):
    devices = gathered.shape[0]
    pieces = 4
    rows = agg.shape[1] // pieces

    def kernel(agg_ref, all_ref, out, hits, bad, buf, sem):
        table = all_ref[:, 0, :]
        s = jnp.sum(table, axis=0, keepdims=True)
        lane = lax.broadcasted_iota(jnp.int32, (1, 128), 1)
        pick = lambda x, where: jnp.sum(jnp.where(where, x, 0.0), axis=1, keepdims=True)
        square_total = pick(s, lane == 0)
        limit = clip_ratio * jnp.sqrt(jnp.full((1, 1), HID * COLS, F32))
        factor = jnp.minimum(1.0, limit / jnp.sqrt(square_total + epsilon))
        copies = []
        for p in range(pieces):
            span = pl.ds(p * rows, rows)
            buf[0, p * rows : (p + 1) * rows, :] = agg_ref[0, p * rows : (p + 1) * rows, :] * factor
            copies.append(pltpu.make_async_copy(buf.at[:, span], out.at[:, span], sem.at[p]))
            copies[-1].start()
        most = jnp.max(table, axis=0, keepdims=True)
        hits[...] = pick(s, lane == 1)
        roundings = (lane >= 2) & (lane < 2 + STAGES)
        room = (ROUNDING * ROUNDING / STAGES) * square_total
        over = (pick(s, roundings) > room) | (devices * pick(most, roundings) > 2.0 * room)
        bad[...] = over.astype(jnp.int32)
        for c in copies:
            c.wait()

    one = lambda t: jax.ShapeDtypeStruct((1, 1), t)
    return pl.pallas_call(
        kernel,
        out_shape=(jax.ShapeDtypeStruct(agg.shape, F32), one(F32), one(jnp.int32)),
        in_specs=[VMEM, VMEM],
        out_specs=(HBM, VMEM, VMEM),
        scratch_shapes=[pltpu.VMEM(agg.shape, F32), pltpu.SemaphoreType.DMA((pieces,))],
        compiler_params=pltpu.CompilerParams(vmem_limit_bytes=8 * MIB),
        name="scale",
    )(agg, gathered)


def local(*args):
    return step(*args)


def step(hidden_acts, out_grad, token_ids, trigger, stale, aggregate_prev):
    n = lax.axis_size("dp")
    chunk = aggregate_prev.shape[1]
    unit = chunk // 16
    me = lax.axis_index("dp").astype(jnp.int32).reshape(1)
    args = (me, trigger[0], token_ids, hidden_acts, out_grad, stale)

    def swap(x, mask):
        return lax.ppermute(x, "dp", [(i, i ^ mask) for i in range(n)])

    outgoing = [[(m ^ bit, rows) for m, rows in parts] for _, bit, parts in RAW]
    made = list(deltas(*args, outgoing[:1], chunk, 60 * 1024 * 1024))
    made += deltas(*args, outgoing[1:], chunk, 16 * MIB)
    got = {label: swap(x, bit) for (label, bit, _), x in zip(RAW, made)}
    own = dict(zip(OWN, deltas(*args, [[key] for key in OWN], chunk, 16 * MIB)))
    lost = [[] for _ in range(STAGES)]
    for label, bit, mine, others, group in SUMS:
        parts = [(own[mine], 0)] + [(got[name], k * mine[1][1] * unit) for name, k in others]
        total, energy = add_round(parts, mine[1][1] * unit)
        lost[group].append(energy)
        got[label] = swap(total, bit)
    groups = []
    for (first, count), mine, at, others in FINAL:
        addends = [(own[mine], at * unit)] + [(got[name], k * unit) for name, k in others]
        groups.append(((first * unit, count * unit), addends))
    agg, kept, sums = finish(aggregate_prev, groups, lost, trigger)
    everyone = lax.all_to_all(sums, ("dp", "shard"), 0, 0, tiled=True)
    update, hits, bad = scale(kept, everyone)

    def again(state):
        mine = deltas(*args, [[(m, (0, 16))] for m in range(n)], chunk, 24 * MIB)
        came = [mine[0]] + [lax.ppermute(mine[m], "dp", [(i, i ^ m) for i in range(n)]) for m in range(1, n)]
        new_agg, new_kept, new_sums = finish(aggregate_prev, [((0, chunk), [(x, 0) for x in came])], [], trigger)
        new_update, _, _ = scale(new_kept, lax.all_to_all(new_sums, ("dp", "shard"), 0, 0, tiled=True))
        return jnp.zeros((), jnp.int32), new_agg, new_update

    _, agg, update = lax.while_loop(lambda state: state[0] > 0, again, (bad[0, 0], agg, update))
    return agg, update, hits[0, 0]


def exact(hidden_acts, out_grad, token_ids, trigger, stale, aggregate_prev):
    masked = out_grad[0] * (token_ids[0] != 0).astype(BF16)[:, None]
    row_flags = jnp.repeat(trigger[0], BLOCK).astype(F32)[:, None]
    triggered = lax.psum(jnp.sum(trigger.astype(F32)), ("dp", "shard"))
    gradient = lax.dot_general(hidden_acts[0], masked, (((0,), (0,)), ((), ())), preferred_element_type=F32)
    delta = (row_flags * (gradient - stale[0].astype(F32))).astype(BF16)
    delta = delta.reshape(lax.axis_size("dp"), aggregate_prev.shape[1], stale.shape[2])
    received = lax.all_to_all(delta, "dp", split_axis=0, concat_axis=0, tiled=True)
    aggregate = aggregate_prev[0] + jnp.sum(received, axis=0, dtype=F32)
    square_total = lax.psum(jnp.sum(aggregate * aggregate), ("dp", "shard"))
    limit = clip_ratio * jnp.sqrt(jnp.asarray(HID * COLS, F32))
    factor = jnp.minimum(1.0, limit / jnp.sqrt(square_total + epsilon))
    return aggregate[None], (aggregate * factor)[None], triggered


def solution(mesh):
    staged = mesh.shape["dp"] == 8
    return jax.shard_map(
        local if staged else exact,
        mesh=mesh,
        in_specs=(
            P("dp", None, "shard"),
            P("dp", None, None),
            P("dp", None),
            P("dp", "shard"),
            P("dp", "shard", None),
            P("shard", "dp", None),
        ),
        out_specs=(P("shard", "dp", None), P("shard", "dp", None), P()),
        check_vma=False,
    )
```

time: 164 us -> 83.8 us (0.51)
  the two profiles are of different devices: /device:TPU:12 before, /device:TPU:0 now
where the time goes in v1:
time: 83.8 us; the launch traced here: 83.5 us
  waiting for transfers between devices  32.5 us (39%)
  starting transfers between devices  23.3 us (28%)
  Pallas kernels  15.2 us (18%)
  blocking collectives  11.1 us (13%)
    ppermute x18, waiting for transfers between devices, swap(): return lax.ppermute(x, 'dp', [(i, i ^ mask) for i in range(n)])  32.5 us
    ppermute x18, starting transfers between devices, swap(): return lax.ppermute(x, 'dp', [(i, i ^ mask) for i in range(n)])  23.3 us
    pallas_call x3, Pallas kernels, deltas(): pl.pallas_call(kernel, out_shape=tuple((jax.ShapeDtypeStruct((h, width),...  11.2 us
    all_to_all x1, blocking collectives, step(): everyone = lax.all_to_all(sums, ('dp', 'shard'), 0, 0, tiled=True)  11.1 us
  transfers between devices with their start and end apart: 18, of which 8 were waited for; matrix products, arithmetic and copies ran while one was open for 0% of the time, Pallas kernels for 9%

profile of v1, /device:TPU:0, one launch (start us, length us, event | category | flops | bytes accessed | tf_op | source)
XLA Modules:
  0.0 83.5 jit_solution(10333363686878916305)
XLA Ops:
  0.7 4.6 %shard_map.86 = (bf16[112,1024]{1,0:T(8,128)(2,1)S(1)}, bf16[96,1024]{1,0:T(8,128)(2,1)S(1)}, bf16[96,1024]{1,0:T(8,128)(2,1)S(1)}, bf16[96,1024]{1,0:T(8,128)(2...) custom-call(s32[1]{0:T(128)} %bitcast.me_ref, ...), custom_call_target="tpu_custom_call" | custom-call | flops 239075328 | bytes 3735552 | tf_op jit(solution)/shard_map/pallas_call | solution.py:118
  5.3 3.1 %collective-permute-start.22 = (bf16[96,1024]{1,0:T(8,128)(2,1)S(1)}, bf16[96,1024]{1,0:T(8,128)(2,1)S(1)}, u32[]{:S(2)}, u32[]{:S(2)}) collective-permute-start(bf16[96,1024]{1,0:T(8,128)(2,1)S(1)} %get-tuple-element.137), channel_id=1, source_target_pairs={{0,8},{4,12},{8,0},{12,4},{16,24},{20,28},{24,16},{28,20},{1,9},{5... | collective-permute-start | bytes 589832 | tf_op jit(solution)/shard_map/ppermute | solution.py:260
  8.4 2.3 %shard_map.88 = bf16[112,1024]{1,0:T(8,128)(2,1)} custom-call(s32[1]{0:T(128)} %bitcast.me_ref, s32[128]{0:T(128)S(1)} %bitcast.5, s32[1,128]{1,0:T(1,128)S(1)} %copy-done.4, bf16[1,128,2048]{2,1,0:T(8,128)(2,1)S(1)} %copy-done.1, bf16[1,128,1024]{2,1,0:T(8,128)(2,1)S(1)} %copy-done.2, bf16[1,2048,1024]{2,1,0:T(8,128)(2,1)} %stale_hbm.5), custom_call_target="tpu_custom_call" | custom-call | flops 29360128 | bytes 458752 | tf_op jit(solution)/shard_map/pallas_call | solution.py:118
  10.7 1.6 %collective-permute-start.11 = (bf16[112,1024]{1,0:T(8,128)(2,1)}, bf16[112,1024]{1,0:T(8,128)(2,1)S(1)}, u32[]{:S(2)}, u32[]{:S(2)}) collective-permute-start(bf16[112,1024]{1,0:T(8,128)(2,1)} %shard_map.88), channel_id=1, source_target_pairs={{0,4},{4,0},{8,12},{12,8},{16,20},{20,16},{24,28},{28,24},{1,5},{5... | collective-permute-start | bytes 688136 | tf_op jit(solution)/shard_map/ppermute | solution.py:260
  12.3 0.5 collective-permute-start.17
  12.8 1.5 %collective-permute-start.16 = (bf16[96,1024]{1,0:T(8,128)(2,1)S(1)}, bf16[96,1024]{1,0:T(8,128)(2,1)S(1)}, u32[]{:S(2)}, u32[]{:S(2)}) collective-permute-start(bf16[96,1024]{1,0:T(8,128)(2,1)S(1)} %get-tuple-element.127), channel_id=1, source_target_pairs={{0,4},{4,0},{8,12},{12,8},{16,20},{20,16},{24,28},{28,24},{1,5},{5... | collective-permute-start | bytes 589832 | tf_op jit(solution)/shard_map/ppermute | solution.py:260
  14.3 0.5 collective-permute-start.10
  14.8 0.0 collective-permute-done.22.refs_1_
  14.8 0.2 collective-permute-start.20
  15.0 4.3 %shard_map.85 = (bf16[112,1024]{1,0:T(8,128)(2,1)S(1)}, bf16[48,1024]{1,0:T(8,128)(2,1)S(1)}, bf16[112,1024]{1,0:T(8,128)(2,1)S(1)}, bf16[48,1024]{1,0:T(8,128)(...) custom-call(s32[1]{0:T(128)} %bitcast.me_ref, ...), custom_call_target="tpu_custom_call" | custom-call | flops 268435456 | bytes 4194304 | tf_op jit(solution)/shard_map/pallas_call | solution.py:118
  19.4 0.1 shard_map.95
  19.4 0.0 collective-permute-done.11.refs_1_
  19.5 0.1 shard_map.89
  19.6 1.8 %collective-permute-start.8 = (bf16[112,1024]{1,0:T(8,128)(2,1)S(1)}, bf16[112,1024]{1,0:T(8,128)(2,1)S(1)}, u32[]{:S(2)}, u32[]{:S(2)}) collective-permute-start(bf16[112,1024]{1,0:T(8,128)(2,1)S(1)} %get-tuple-element.116), channel_id=1, source_target_pairs={{0,4},{4,0},{8,12},{12,8},{16,20},{20,16},{24,28},{28,24},{1,5},{5... | collective-permute-start | bytes 688136 | tf_op jit(solution)/shard_map/ppermute | solution.py:260
  21.4 2.2 %collective-permute-done.17.refs_1_ = bf16[96,1024]{1,0:T(8,128)(2,1)S(1)} collective-permute-done((bf16[96,1024]{1,0:T(8,128)(2,1)S(1)}, bf16[96,1024]{1,0:T(8,128)(2,1)S(1)}, u32[]{:S(2)}, u32[]{:S(2)}) %collective-permute-start.17) | collective-permute-done | bytes 196640 | tf_op jit(solution)/shard_map/ppermute | solution.py:260
  23.7 0.0 collective-permute-start.12
  23.7 4.2 %collective-permute-done.16.refs_1_ = bf16[96,1024]{1,0:T(8,128)(2,1)S(1)} collective-permute-done((bf16[96,1024]{1,0:T(8,128)(2,1)S(1)}, bf16[96,1024]{1,0:T(8,128)(2,1)S(1)}, u32[]{:S(2)}, u32[]{:S(2)}) %collective-permute-start.16) | collective-permute-done | bytes 196640 | tf_op jit(solution)/shard_map/ppermute | solution.py:260
  27.9 1.5 %collective-permute-start.23 = (bf16[48,1024]{1,0:T(8,128)(2,1)S(1)}, bf16[48,1024]{1,0:T(8,128)(2,1)S(1)}, u32[]{:S(2)}, u32[]{:S(2)}) collective-permute-start(bf16[48,1024]{1,0:T(8,128)(2,1)S(1)} %get-tuple-element.139), channel_id=1, source_target_pairs={{0,4},{4,0},{8,12},{12,8},{16,20},{20,16},{24,28},{28,24},{1,5},{5... | collective-permute-start | bytes 294920 | tf_op jit(solution)/shard_map/ppermute | solution.py:260
  29.4 0.1 shard_map.92
  29.5 0.0 collective-permute-done.20.refs_1_.refs_7_
  29.5 0.6 collective-permute-start.14
  30.1 2.7 %collective-permute-done.10.refs_1_ = bf16[112,1024]{1,0:T(8,128)(2,1)S(1)} collective-permute-done((bf16[112,1024]{1,0:T(8,128)(2,1)S(1)}, bf16[112,1024]{1,0:T(8,128)(2,1)S(1)}, u32[]{:S(2)}, u32[]{:S(2)}) %collective-permute-start.10) | collective-permute-done | bytes 229408 | tf_op jit(solution)/shard_map/ppermute | solution.py:260
  32.8 1.5 %collective-permute-start.7 = (bf16[208,1024]{1,0:T(8,128)(2,1)S(1)}, bf16[208,1024]{1,0:T(8,128)(2,1)S(1)}, u32[]{:S(2)}, u32[]{:S(2)}) collective-permute-start(bf16[208,1024]{1,0:T(8,128)(2,1)S(1)} %get-tuple-element.114), channel_id=1, source_target_pairs={{0,4},{4,0},{8,12},{12,8},{16,20},{20,16},{24,28},{28,24},{1,5},{5... | collective-permute-start | bytes 1277960 | tf_op jit(solution)/shard_map/ppermute | solution.py:260
  34.3 5.5 %collective-permute-done.23.refs_2_ = bf16[48,1024]{1,0:T(8,128)(2,1)S(1)} collective-permute-done((bf16[48,1024]{1,0:T(8,128)(2,1)S(1)}, bf16[48,1024]{1,0:T(8,128)(2,1)S(1)}, u32[]{:S(2)}, u32[]{:S(2)}) %collective-permute-start.23) | collective-permute-done | bytes 98336 | tf_op jit(solution)/shard_map/ppermute | solution.py:260
  39.8 0.0 collective-permute-start.18
  39.9 0.1 shard_map.94
  39.9 0.1 shard_map.96
  40.0 2.0 %collective-permute-start.21 = (bf16[48,1024]{1,0:T(8,128)(2,1)S(1)}, bf16[48,1024]{1,0:T(8,128)(2,1)S(1)}, u32[]{:S(2)}, u32[]{:S(2)}) collective-permute-start(bf16[48,1024]{1,0:T(8,128)(2,1)S(1)} %get-tuple-element.135), channel_id=1, source_target_pairs={{0,4},{4,0},{8,12},{12,8},{16,20},{20,16},{24,28},{28,24},{1,5},{5... | collective-permute-start | bytes 294920 | tf_op jit(solution)/shard_map/ppermute | solution.py:260
  42.0 2.6 %collective-permute-start.24 = (bf16[48,1024]{1,0:T(8,128)(2,1)S(1)}, bf16[48,1024]{1,0:T(8,128)(2,1)S(1)}, u32[]{:S(2)}, u32[]{:S(2)}) collective-permute-start(bf16[48,1024]{1,0:T(8,128)(2,1)S(1)} %get-tuple-element.140), channel_id=1, source_target_pairs={{0,16},{4,20},{8,24},{12,28},{16,0},{20,4},{24,8},{28,12},{1,17},{... | collective-permute-start | bytes 294920 | tf_op jit(solution)/shard_map/ppermute | solution.py:260
  44.6 0.1 shard_map.87
  44.7 0.2 shard_map.90
  44.9 0.0 collective-permute-done.14.refs_1_
  44.9 1.6 %collective-permute-start.9 = (bf16[112,1024]{1,0:T(8,128)(2,1)S(1)}, bf16[112,1024]{1,0:T(8,128)(2,1)S(1)}, u32[]{:S(2)}, u32[]{:S(2)}) collective-permute-start(bf16[112,1024]{1,0:T(8,128)(2,1)S(1)} %get-tuple-element.117), channel_id=1, source_target_pairs={{0,8},{4,12},{8,0},{12,4},{16,24},{20,28},{24,16},{28,20},{1,9},{5... | collective-permute-start | bytes 688136 | tf_op jit(solution)/shard_map/ppermute | solution.py:260
  46.5 4.0 %collective-permute-done.18.refs_2_ = bf16[96,1024]{1,0:T(8,128)(2,1)S(1)} collective-permute-done((bf16[96,1024]{1,0:T(8,128)(2,1)S(1)}, bf16[96,1024]{1,0:T(8,128)(2,1)S(1)}, u32[]{:S(2)}, u32[]{:S(2)}) %collective-permute-start.18) | collective-permute-done | bytes 196640 | tf_op jit(solution)/shard_map/ppermute | solution.py:260
  50.5 1.1 %collective-permute-start.13 = (bf16[112,1024]{1,0:T(8,128)(2,1)S(1)}, bf16[112,1024]{1,0:T(8,128)(2,1)S(1)}, u32[]{:S(2)}, u32[]{:S(2)}) collective-permute-start(bf16[112,1024]{1,0:T(8,128)(2,1)S(1)} %get-tuple-element.122), channel_id=1, source_target_pairs={{0,16},{4,20},{8,24},{12,28},{16,0},{20,4},{24,8},{28,12},{1,17},{... | collective-permute-start | bytes 688136 | tf_op jit(solution)/shard_map/ppermute | solution.py:260
  51.6 0.1 shard_map.91
  51.7 0.1 shard_map.93
  51.9 2.0 %collective-permute-done.21.refs_8_ = bf16[48,1024]{1,0:T(8,128)(2,1)S(1)} collective-permute-done((bf16[48,1024]{1,0:T(8,128)(2,1)S(1)}, bf16[48,1024]{1,0:T(8,128)(2,1)S(1)}, u32[]{:S(2)}, u32[]{:S(2)}) %collective-permute-start.21) | collective-permute-done | bytes 98336 | tf_op jit(solution)/shard_map/ppermute | solution.py:260
  53.8 1.1 %collective-permute-start.15 = (bf16[96,1024]{1,0:T(8,128)(2,1)S(1)}, bf16[96,1024]{1,0:T(8,128)(2,1)S(1)}, u32[]{:S(2)}, u32[]{:S(2)}) collective-permute-start(bf16[96,1024]{1,0:T(8,128)(2,1)S(1)} %get-tuple-element.125), channel_id=1, source_target_pairs={{0,8},{4,12},{8,0},{12,4},{16,24},{20,28},{24,16},{28,20},{1,9},{5... | collective-permute-start | bytes 589832 | tf_op jit(solution)/shard_map/ppermute | solution.py:260
  54.9 0.0 collective-permute-done.24.refs_9_
  54.9 2.0 %collective-permute-start.19 = (bf16[96,1024]{1,0:T(8,128)(2,1)S(1)}, bf16[96,1024]{1,0:T(8,128)(2,1)S(1)}, u32[]{:S(2)}, u32[]{:S(2)}) collective-permute-start(bf16[96,1024]{1,0:T(8,128)(2,1)S(1)} %get-tuple-element.131), channel_id=1, source_target_pairs={{0,16},{4,20},{8,24},{12,28},{16,0},{20,4},{24,8},{28,12},{1,17},{... | collective-permute-start | bytes 589832 | tf_op jit(solution)/shard_map/ppermute | solution.py:260
  56.9 7.2 %collective-permute-done.15.refs_4_ = bf16[96,1024]{1,0:T(8,128)(2,1)S(1)} collective-permute-done((bf16[96,1024]{1,0:T(8,128)(2,1)S(1)}, bf16[96,1024]{1,0:T(8,128)(2,1)S(1)}, u32[]{:S(2)}, u32[]{:S(2)}) %collective-permute-start.15) | collective-permute-done | bytes 196640 | tf_op jit(solution)/shard_map/ppermute | solution.py:260
  64.1 0.0 collective-permute-done.7.refs_1_
  64.1 4.6 %collective-permute-done.19.refs_5_ = bf16[96,1024]{1,0:T(8,128)(2,1)S(1)} collective-permute-done((bf16[96,1024]{1,0:T(8,128)(2,1)S(1)}, bf16[96,1024]{1,0:T(8,128)(2,1)S(1)}, u32[]{:S(2)}, u32[]{:S(2)}) %collective-permute-start.19) | collective-permute-done | bytes 196640 | tf_op jit(solution)/shard_map/ppermute | solution.py:260
  68.8 1.4 %finish.3 = (f32[1,256,1024]{2,1,0:T(8,128)}, f32[1,256,1024]{2,1,0:T(8,128)S(1)}, f32[32,1,128]{2,1,0:T(1,128)S(1)}) custom-call(s32[1,128]{1,0:T(1,128)S(1)} %copy-done.3, f32[1,256,1024]{2,1,0:T(8,128)S(1)} %copy-done, bf16[208,1024]{1,0:T(8,128)(2,1)S(1)} %get-tuple-element.113.refs_0_, bf16[208,1024]{1,0:T(8,128)(2,1)S(1)} %collective-permute-done.7.refs_1_, ...), custom_call_target="tpu_custom_call" | custom-call | tf_op jit(solution)/shard_map/finish/pallas_call | solution.py:197
  70.1 11.1 %all_to_all.9.all_ref = f32[32,1,128]{2,1,0:T(1,128)S(1)} all-to-all(f32[32,1,128]{2,1,0:T(1,128)S(1)} %get-tuple-element.151), channel_id=1, replica_groups=mesh['dp'=8,'shard'=4] {'dp','shard'}, dimensions={0} | all-to-all | bytes 32768 | tf_op jit(solution)/shard_map/all_to_all | solution.py:278
  81.2 1.7 %scale.3 = (f32[1,256,1024]{2,1,0:T(8,128)}, f32[1,1]{1,0:T(1,128)}, s32[1,1]{1,0:T(1,128)}) custom-call(f32[1,256,1024]{2,1,0:T(8,128)S(1)} %get-tuple-element.150.agg_ref, f32[32,1,128]{2,1,0:T(1,128)S(1)} %all_to_all.9.all_ref), custom_call_target="tpu_custom_call" | custom-call | tf_op jit(solution)/shard_map/scale/pallas_call | solution.py:237
  82.9 0.6 while.11
  (14 shorter events, 0.0 us)
Async XLA Ops:
  0.6 7.8 %copy-start.3 = (s32[1,128]{1,0:T(1,128)S(1)}, s32[1,128]{1,0:T(1,128)}, u32[]{:S(2)}) copy-start(s32[1,128]{1,0:T(1,128)} %trig_ref.1) | copy-start | bytes 1540
  0.6 7.8 %copy-start.4 = (s32[1,128]{1,0:T(1,128)S(1)}, s32[1,128]{1,0:T(1,128)}, u32[]{:S(2)}) copy-start(s32[1,128]{1,0:T(1,128)} %tok_ref.5) | copy-start | bytes 1540
  0.7 7.7 %copy-start.1 = (bf16[1,128,2048]{2,1,0:T(8,128)(2,1)S(1)}, bf16[1,128,2048]{2,1,0:T(8,128)(2,1)}, u32[]{:S(2)}) copy-start(bf16[1,128,2048]{2,1,0:T(8,128)(2,1)} %acts_hbm.5) | copy-start | bytes 1572868
  0.7 7.7 %copy-start.2 = (bf16[1,128,1024]{2,1,0:T(8,128)(2,1)S(1)}, bf16[1,128,1024]{2,1,0:T(8,128)(2,1)}, u32[]{:S(2)}) copy-start(bf16[1,128,1024]{2,1,0:T(8,128)(2,1)} %og_hbm.5) | copy-start | bytes 786436
  5.3 9.5 %collective-permute-start.22 = (bf16[96,1024]{1,0:T(8,128)(2,1)S(1)}, bf16[96,1024]{1,0:T(8,128)(2,1)S(1)}, u32[]{:S(2)}, u32[]{:S(2)}) collective-permute-start(bf16[96,1024]{1,0:T(8,128)(2,1)S(1)} %get-tuple-element.137), channel_id=1, source_target_pairs={{0,8},{4,12},{8,0},{12,4},{16,24},{20,28},{24,16},{28,20},{1,9},{5... | collective-permute-start | bytes 589832 | tf_op jit(solution)/shard_map/ppermute | solution.py:260
  10.7 8.8 %collective-permute-start.11 = (bf16[112,1024]{1,0:T(8,128)(2,1)}, bf16[112,1024]{1,0:T(8,128)(2,1)S(1)}, u32[]{:S(2)}, u32[]{:S(2)}) collective-permute-start(bf16[112,1024]{1,0:T(8,128)(2,1)} %shard_map.88), channel_id=1, source_target_pairs={{0,4},{4,0},{8,12},{12,8},{16,20},{20,16},{24,28},{28,24},{1,5},{5... | collective-permute-start | bytes 688136 | tf_op jit(solution)/shard_map/ppermute | solution.py:260
  12.3 11.4 %collective-permute-start.17 = (bf16[96,1024]{1,0:T(8,128)(2,1)S(1)}, bf16[96,1024]{1,0:T(8,128)(2,1)S(1)}, u32[]{:S(2)}, u32[]{:S(2)}) collective-permute-start(bf16[96,1024]{1,0:T(8,128)(2,1)S(1)} %get-tuple-element.129), channel_id=1, source_target_pairs={{0,4},{4,0},{8,12},{12,8},{16,20},{20,16},{24,28},{28,24},{1,5},{5... | collective-permute-start | bytes 589832 | tf_op jit(solution)/shard_map/ppermute | solution.py:260
  12.8 15.1 %collective-permute-start.16 = (bf16[96,1024]{1,0:T(8,128)(2,1)S(1)}, bf16[96,1024]{1,0:T(8,128)(2,1)S(1)}, u32[]{:S(2)}, u32[]{:S(2)}) collective-permute-start(bf16[96,1024]{1,0:T(8,128)(2,1)S(1)} %get-tuple-element.127), channel_id=1, source_target_pairs={{0,4},{4,0},{8,12},{12,8},{16,20},{20,16},{24,28},{28,24},{1,5},{5... | collective-permute-start | bytes 589832 | tf_op jit(solution)/shard_map/ppermute | solution.py:260
  14.3 18.5 %collective-permute-start.10 = (bf16[112,1024]{1,0:T(8,128)(2,1)S(1)}, bf16[112,1024]{1,0:T(8,128)(2,1)S(1)}, u32[]{:S(2)}, u32[]{:S(2)}) collective-permute-start(bf16[112,1024]{1,0:T(8,128)(2,1)S(1)} %get-tuple-element.119), channel_id=1, source_target_pairs={{0,4},{4,0},{8,12},{12,8},{16,20},{20,16},{24,28},{28,24},{1,5},{5... | collective-permute-start | bytes 688136 | tf_op jit(solution)/shard_map/ppermute | solution.py:260
  14.8 53.9 %copy-start = (f32[1,256,1024]{2,1,0:T(8,128)S(1)}, f32[1,256,1024]{2,1,0:T(8,128)}, u32[]{:S(2)}) copy-start(f32[1,256,1024]{2,1,0:T(8,128)} %prev_ref.1) | copy-start | bytes 3145732
  14.8 14.7 %collective-permute-start.20 = (bf16[96,1024]{1,0:T(8,128)(2,1)S(1)}, bf16[96,1024]{1,0:T(8,128)(2,1)S(1)}, u32[]{:S(2)}, u32[]{:S(2)}) collective-permute-start(bf16[96,1024]{1,0:T(8,128)(2,1)S(1)} %get-tuple-element.133), channel_id=1, source_target_pairs={{0,8},{4,12},{8,0},{12,4},{16,24},{20,28},{24,16},{28,20},{1,9},{5... | collective-permute-start | bytes 589832 | tf_op jit(solution)/shard_map/ppermute | solution.py:260
  19.6 20.4 %collective-permute-start.8 = (bf16[112,1024]{1,0:T(8,128)(2,1)S(1)}, bf16[112,1024]{1,0:T(8,128)(2,1)S(1)}, u32[]{:S(2)}, u32[]{:S(2)}) collective-permute-start(bf16[112,1024]{1,0:T(8,128)(2,1)S(1)} %get-tuple-element.116), channel_id=1, source_target_pairs={{0,4},{4,0},{8,12},{12,8},{16,20},{20,16},{24,28},{28,24},{1,5},{5... | collective-permute-start | bytes 688136 | tf_op jit(solution)/shard_map/ppermute | solution.py:260
  23.7 18.3 %collective-permute-start.12 = (bf16[112,1024]{1,0:T(8,128)(2,1)S(1)}, bf16[112,1024]{1,0:T(8,128)(2,1)S(1)}, u32[]{:S(2)}, u32[]{:S(2)}) collective-permute-start(bf16[112,1024]{1,0:T(8,128)(2,1)S(1)} %get-tuple-element.121), channel_id=1, source_target_pairs={{0,8},{4,12},{8,0},{12,4},{16,24},{20,28},{24,16},{28,20},{1,9},{5... | collective-permute-start | bytes 688136 | tf_op jit(solution)/shard_map/ppermute | solution.py:260
  27.9 11.9 %collective-permute-start.23 = (bf16[48,1024]{1,0:T(8,128)(2,1)S(1)}, bf16[48,1024]{1,0:T(8,128)(2,1)S(1)}, u32[]{:S(2)}, u32[]{:S(2)}) collective-permute-start(bf16[48,1024]{1,0:T(8,128)(2,1)S(1)} %get-tuple-element.139), channel_id=1, source_target_pairs={{0,4},{4,0},{8,12},{12,8},{16,20},{20,16},{24,28},{28,24},{1,5},{5... | collective-permute-start | bytes 294920 | tf_op jit(solution)/shard_map/ppermute | solution.py:260
  29.5 15.4 %collective-permute-start.14 = (bf16[96,1024]{1,0:T(8,128)(2,1)S(1)}, bf16[96,1024]{1,0:T(8,128)(2,1)S(1)}, u32[]{:S(2)}, u32[]{:S(2)}) collective-permute-start(bf16[96,1024]{1,0:T(8,128)(2,1)S(1)} %get-tuple-element.124), channel_id=1, source_target_pairs={{0,4},{4,0},{8,12},{12,8},{16,20},{20,16},{24,28},{28,24},{1,5},{5... | collective-permute-start | bytes 589832 | tf_op jit(solution)/shard_map/ppermute | solution.py:260
  32.8 31.3 %collective-permute-start.7 = (bf16[208,1024]{1,0:T(8,128)(2,1)S(1)}, bf16[208,1024]{1,0:T(8,128)(2,1)S(1)}, u32[]{:S(2)}, u32[]{:S(2)}) collective-permute-start(bf16[208,1024]{1,0:T(8,128)(2,1)S(1)} %get-tuple-element.114), channel_id=1, source_target_pairs={{0,4},{4,0},{8,12},{12,8},{16,20},{20,16},{24,28},{28,24},{1,5},{5... | collective-permute-start | bytes 1277960 | tf_op jit(solution)/shard_map/ppermute | solution.py:260
  39.8 10.7 %collective-permute-start.18 = (bf16[96,1024]{1,0:T(8,128)(2,1)S(1)}, bf16[96,1024]{1,0:T(8,128)(2,1)S(1)}, u32[]{:S(2)}, u32[]{:S(2)}) collective-permute-start(bf16[96,1024]{1,0:T(8,128)(2,1)S(1)} %get-tuple-element.130), channel_id=1, source_target_pairs={{0,8},{4,12},{8,0},{12,4},{16,24},{20,28},{24,16},{28,20},{1,9},{5... | collective-permute-start | bytes 589832 | tf_op jit(solution)/shard_map/ppermute | solution.py:260
  40.0 13.8 %collective-permute-start.21 = (bf16[48,1024]{1,0:T(8,128)(2,1)S(1)}, bf16[48,1024]{1,0:T(8,128)(2,1)S(1)}, u32[]{:S(2)}, u32[]{:S(2)}) collective-permute-start(bf16[48,1024]{1,0:T(8,128)(2,1)S(1)} %get-tuple-element.135), channel_id=1, source_target_pairs={{0,4},{4,0},{8,12},{12,8},{16,20},{20,16},{24,28},{28,24},{1,5},{5... | collective-permute-start | bytes 294920 | tf_op jit(solution)/shard_map/ppermute | solution.py:260
  42.0 12.9 %collective-permute-start.24 = (bf16[48,1024]{1,0:T(8,128)(2,1)S(1)}, bf16[48,1024]{1,0:T(8,128)(2,1)S(1)}, u32[]{:S(2)}, u32[]{:S(2)}) collective-permute-start(bf16[48,1024]{1,0:T(8,128)(2,1)S(1)} %get-tuple-element.140), channel_id=1, source_target_pairs={{0,16},{4,20},{8,24},{12,28},{16,0},{20,4},{24,8},{28,12},{1,17},{... | collective-permute-start | bytes 294920 | tf_op jit(solution)/shard_map/ppermute | solution.py:260
  44.9 19.3 %collective-permute-start.9 = (bf16[112,1024]{1,0:T(8,128)(2,1)S(1)}, bf16[112,1024]{1,0:T(8,128)(2,1)S(1)}, u32[]{:S(2)}, u32[]{:S(2)}) collective-permute-start(bf16[112,1024]{1,0:T(8,128)(2,1)S(1)} %get-tuple-element.117), channel_id=1, source_target_pairs={{0,8},{4,12},{8,0},{12,4},{16,24},{20,28},{24,16},{28,20},{1,9},{5... | collective-permute-start | bytes 688136 | tf_op jit(solution)/shard_map/ppermute | solution.py:260
  50.5 18.2 %collective-permute-start.13 = (bf16[112,1024]{1,0:T(8,128)(2,1)S(1)}, bf16[112,1024]{1,0:T(8,128)(2,1)S(1)}, u32[]{:S(2)}, u32[]{:S(2)}) collective-permute-start(bf16[112,1024]{1,0:T(8,128)(2,1)S(1)} %get-tuple-element.122), channel_id=1, source_target_pairs={{0,16},{4,20},{8,24},{12,28},{16,0},{20,4},{24,8},{28,12},{1,17},{... | collective-permute-start | bytes 688136 | tf_op jit(solution)/shard_map/ppermute | solution.py:260
  53.8 10.3 %collective-permute-start.15 = (bf16[96,1024]{1,0:T(8,128)(2,1)S(1)}, bf16[96,1024]{1,0:T(8,128)(2,1)S(1)}, u32[]{:S(2)}, u32[]{:S(2)}) collective-permute-start(bf16[96,1024]{1,0:T(8,128)(2,1)S(1)} %get-tuple-element.125), channel_id=1, source_target_pairs={{0,8},{4,12},{8,0},{12,4},{16,24},{20,28},{24,16},{28,20},{1,9},{5... | collective-permute-start | bytes 589832 | tf_op jit(solution)/shard_map/ppermute | solution.py:260
  54.9 13.8 %collective-permute-start.19 = (bf16[96,1024]{1,0:T(8,128)(2,1)S(1)}, bf16[96,1024]{1,0:T(8,128)(2,1)S(1)}, u32[]{:S(2)}, u32[]{:S(2)}) collective-permute-start(bf16[96,1024]{1,0:T(8,128)(2,1)S(1)} %get-tuple-element.131), channel_id=1, source_target_pairs={{0,16},{4,20},{8,24},{12,28},{16,0},{20,4},{24,8},{28,12},{1,17},{... | collective-permute-start | bytes 589832 | tf_op jit(solution)/shard_map/ppermute | solution.py:260

commit v2 on v1

--- a/solution.py
+++ b/solution.py
@@ -11,6 +11,7 @@
 clip_ratio = 0.25
 epsilon = 1e-06
 MIB = 1 << 20
+PIECE = 64
 STAGES = 3
 ROUNDING = 4.8e-4
 F32, BF16 = jnp.float32, jnp.bfloat16
@@ -18,19 +19,22 @@
 SMEM = pl.BlockSpec(memory_space=pltpu.SMEM)
 HBM = pl.BlockSpec(memory_space=pltpu.HBM)
 
-A0, A1, A, B = (0, 7), (7, 6), (0, 13), (13, 3)
+A0, A1, B = (0, 6), (6, 7), (13, 3)
 RAW = (
     ("y6a", 1, ((6, A0),)),
+    ("zb0", 2, ((5, B), (4, B))),
     ("y4a", 1, ((4, A0),)),
-    ("zb0", 2, ((5, B), (4, B))),
     ("y6b", 1, ((6, A1),)),
     ("zb1", 2, ((1, B), (0, B))),
     ("y4b", 1, ((4, A1),)),
     ("y2a", 1, ((2, A0),)),
     ("y2b", 1, ((2, A1),)),
-    ("y0", 1, ((0, A),)),
+    ("y0b", 1, ((0, A1),)),
+    ("y0a", 1, ((0, A0),)),
 )
-OWN = ((6, A0), (5, B), (4, A0), (4, B), (6, A1), (4, A1), (1, B), (2, A0), (2, A1), (0, A), (0, B))
+FIRST = 3
+OWN_EARLY = ((6, A0), (5, B), (4, A0), (6, A1))
+OWN_LATE = ((4, B), (4, A1), (1, B), (2, A0), (2, A1), (0, A0), (0, A1), (0, B))
 SUMS = (
     ("near0", 2, (6, A0), (("y6a", 0),), 0),
     ("pairb5", 1, (5, B), (("zb0", 0),), 0),
@@ -43,10 +47,10 @@
     ("last1", 2, (2, A1), (("y2b", 0),), 2),
 )
 FINAL = (
-    (A0, (0, A), 0, (("y0", 0), ("last0", 0), ("quad0", 0))),
-    (A1, (0, A), 7, (("y0", 7), ("last1", 0), ("quad1", 0))),
-    (B, (0, B), 0, (("zb1", 3), ("pairb1", 0), ("quadb", 0))),
+    (B, (0, B), (("zb1", 1), ("pairb1", 0), ("quadb", 0))),
+    (A1, (0, A1), (("y0b", 0), ("last1", 0), ("quad1", 0))),
 )
+LAST = ((A0, (0, A0), (("y0a", 0), ("last0", 0), ("quad0", 0))),)
 
 
 def fold(x):
@@ -58,7 +62,7 @@
     return total
 
 
-def deltas(me, trig, tok, acts, og, stale, messages, chunk, limit):
+def deltas(trig, tok, acts, og, stale, messages, chunk, limit):
     tokens, width = og.shape[1], og.shape[2]
     unit = chunk // 16
     pieces = [(i, m, r) for i, message in enumerate(messages) for m, r in message]
@@ -67,10 +71,13 @@
     total = sum(heights)
     n_out = len(messages)
 
-    def kernel(me_ref, trig_ref, tok_ref, acts_hbm, og_hbm, stale_hbm, *refs):
+    def kernel(trig_hbm, tok_hbm, acts_hbm, og_hbm, stale_hbm, *refs):
         outs = refs[:n_out]
-        acts_buf, og_buf, stale_buf, sem = refs[n_out:]
-        start = {m: pl.multiple_of((me_ref[0] ^ m) * chunk, chunk) for m in masks}
+        acts_buf, og_buf, stale_buf, tok_ref, trig_ref, small, sem = refs[n_out:]
+        me = lax.axis_index("dp")
+        start = {m: pl.multiple_of((me ^ m) * chunk, chunk) for m in masks}
+        tok_copy = pltpu.make_async_copy(tok_hbm, tok_ref, small.at[0])
+        trig_copy = pltpu.make_async_copy(trig_hbm, trig_ref, small.at[1])
         og_copy = pltpu.make_async_copy(og_hbm.at[0], og_buf, sem.at[0])
         act_copies, stale_copies = {}, []
         for j, m in enumerate(masks):
@@ -94,6 +101,11 @@
                 act_copies[m].start()
                 begun.add(m)
             stale_copies[j].start()
+            if j == 0:
+                tok_copy.start()
+                trig_copy.start()
+        tok_copy.wait()
+        trig_copy.wait()
         real = (tok_ref[...] != 0).astype(BF16)
         weights = {}
         at, offset, last = 0, 0, -1
@@ -109,7 +121,7 @@
             gradient = jnp.dot(part, og_buf[...], preferred_element_type=F32)
             stale_copies[j].wait()
             for b in range(0, count * unit, BLOCK):
-                flag = trig_ref[(start[m] + first * unit + b) // BLOCK].astype(F32)
+                flag = trig_ref[0, (start[m] + first * unit + b) // BLOCK].astype(F32)
                 old = stale_buf[at + b : at + b + BLOCK, :].astype(F32)
                 outs[i][offset + b : offset + b + BLOCK, :] = (flag * (gradient[b : b + BLOCK] - old)).astype(BF16)
             at += count * unit
@@ -118,19 +130,22 @@
     return pl.pallas_call(
         kernel,
         out_shape=tuple(jax.ShapeDtypeStruct((h, width), BF16) for h in heights),
-        in_specs=[SMEM, SMEM, VMEM] + [HBM] * 3,
+        in_specs=[HBM] * 5,
         out_specs=tuple(VMEM for _ in messages),
         scratch_shapes=[
             pltpu.VMEM((len(masks), tokens, chunk), BF16),
             pltpu.VMEM((tokens, width), BF16),
             pltpu.VMEM((total, width), BF16),
+            pltpu.VMEM(tok.shape, jnp.int32),
+            pltpu.SMEM(trig.shape, jnp.int32),
+            pltpu.SemaphoreType.DMA((2,)),
             pltpu.SemaphoreType.DMA((1 + len(masks) + len(pieces),)),
         ],
         cost_estimate=pl.CostEstimate(
             flops=2 * tokens * total * width, bytes_accessed=total * width * 4, transcendentals=0
         ),
         compiler_params=pltpu.CompilerParams(vmem_limit_bytes=limit),
-    )(me, trig, tok, acts, og, stale)
+    )(trig, tok, acts, og, stale)
 
 
 def add_round(parts, rows):
@@ -158,59 +173,92 @@
     )(*[x for x, _ in parts])
 
 
-def finish(prev, groups, lost, trig):
+def total_up(prev, groups, lost, trig, begun):
     arrays = {id(x): x for _, addends in groups for x, _ in addends}
     keys = list(arrays)
     flat = [x for group in lost for x in group]
-    n_arrays, n_lost = len(keys), len(flat)
+    n_arrays, n_lost, n_begun = len(keys), len(flat), len(begun)
+    lowest = min(first for (first, _), _ in groups)
+    height = sum(rows for (_, rows), _ in groups)
 
     def kernel(trig_ref, prev_ref, *refs):
         lost_refs = list(refs[n_arrays : n_arrays + n_lost])
-        agg, kept, sums, sem = refs[n_arrays + n_lost :]
+        before = refs[n_arrays + n_lost :][:n_begun]
+        kept, sums = refs[n_arrays + n_lost + n_begun :]
         total = jnp.zeros((8, 128), F32)
-        copies = []
-        for g, ((first, rows), addends) in enumerate(groups):
+        for (first, rows), addends in groups:
             for r in range(0, rows, BLOCK):
                 a = prev_ref[0, first + r : first + r + BLOCK, :]
                 for x, at in addends:
                     a = a + refs[keys.index(id(x))][at + r : at + r + BLOCK, :].astype(F32)
-                kept[0, first + r : first + r + BLOCK, :] = a
+                kept[0, first - lowest + r : first - lowest + r + BLOCK, :] = a
                 total = total + fold(a)
-            span = pl.ds(first, rows)
-            copies.append(pltpu.make_async_copy(kept.at[:, span], agg.at[:, span], sem.at[g]))
-            copies[-1].start()
-        hits = trig_ref[...].astype(F32)
         row = lax.broadcasted_iota(jnp.int32, (8, 128), 0)
-        lane = lax.broadcasted_iota(jnp.int32, (8, 128), 1)
-        stacked = jnp.where(row == 0, jnp.sum(total, axis=0, keepdims=True), jnp.where(row == 1, hits, 0.0))
+        if n_begun:
+            stacked = before[0][...]
+        else:
+            stacked = jnp.where(row == 1, trig_ref[...].astype(F32), 0.0)
+        stacked = stacked + jnp.where(row == 0, jnp.sum(total, axis=0, keepdims=True), 0.0)
         for i, group in enumerate(lost):
             tile = sum(lost_refs.pop(0)[...] for _ in group)
             stacked = jnp.where(row == 2 + i, jnp.sum(tile, axis=0, keepdims=True), stacked)
-        values = jnp.sum(stacked, axis=1, keepdims=True)
-        line = jnp.sum(jnp.where(row == lane, values, 0.0), axis=0, keepdims=True)
-        sums[...] = jnp.broadcast_to(line[None], sums.shape)
+        if sums.shape == stacked.shape:
+            sums[...] = stacked
+        else:
+            lane = lax.broadcasted_iota(jnp.int32, (8, 128), 1)
+            values = jnp.sum(stacked, axis=1, keepdims=True)
+            line = jnp.sum(jnp.where(row == lane, values, 0.0), axis=0, keepdims=True)
+            sums[...] = jnp.broadcast_to(line[None], sums.shape)
+
+    n = lax.axis_size("dp") * lax.axis_size("shard")
+    ends = n_begun or height == prev.shape[1]
+    return pl.pallas_call(
+        kernel,
+        out_shape=(
+            jax.ShapeDtypeStruct((1, height, prev.shape[2]), F32),
+            jax.ShapeDtypeStruct((n, 1, 128) if ends else (8, 128), F32),
+        ),
+        in_specs=[VMEM] * (2 + n_arrays + n_lost + n_begun),
+        out_specs=(VMEM, VMEM),
+        compiler_params=pltpu.CompilerParams(vmem_limit_bytes=12 * MIB),
+    )(trig, prev, *arrays.values(), *flat, *begun)
+
+
+def store(kept):
+    shape = (1, sum(x.shape[1] for _, x in kept), kept[0][1].shape[2])
+
+    def kernel(*refs):
+        out, sem = refs[len(kept) :]
+        copies = []
+        for i, (first, x) in enumerate(kept):
+            there = pl.ds(first, x.shape[1])
+            copies.append(pltpu.make_async_copy(refs[i], out.at[:, there], sem.at[i]))
+            copies[-1].start()
         for c in copies:
             c.wait()
 
-    n = lax.axis_size("dp") * lax.axis_size("shard")
-    whole = jax.ShapeDtypeStruct(prev.shape, F32)
-    return pl.pallas_call(
-        kernel,
-        out_shape=(whole, whole, jax.ShapeDtypeStruct((n, 1, 128), F32)),
-        in_specs=[VMEM] * (2 + n_arrays + n_lost),
-        out_specs=(HBM, VMEM, VMEM),
-        scratch_shapes=[pltpu.SemaphoreType.DMA((len(groups),))],
-        compiler_params=pltpu.CompilerParams(vmem_limit_bytes=12 * MIB),
-        name="finish",
-    )(trig, prev, *arrays.values(), *flat)
-
-
-def scale(agg, gathered):
+    return pl.pallas_call(
+        kernel,
+        out_shape=jax.ShapeDtypeStruct(shape, F32),
+        in_specs=[VMEM] * len(kept),
+        out_specs=HBM,
+        scratch_shapes=[pltpu.SemaphoreType.DMA((len(kept),))],
+        cost_estimate=pl.CostEstimate(flops=0, bytes_accessed=1 << 24, transcendentals=0),
+        compiler_params=pltpu.CompilerParams(vmem_limit_bytes=8 * MIB),
+        name="store",
+    )(*[x for _, x in kept])
+
+
+def scale(kept, gathered):
     devices = gathered.shape[0]
-    pieces = 4
-    rows = agg.shape[1] // pieces
-
-    def kernel(agg_ref, all_ref, out, hits, bad, buf, sem):
+    shape = (1, sum(x.shape[1] for _, x in kept), kept[0][1].shape[2])
+    spans = []
+    for i, (first, x) in enumerate(kept):
+        step = PIECE if x.shape[1] % PIECE == 0 else BLOCK
+        spans += [(i, r, first + r, step) for r in range(0, x.shape[1], step)]
+
+    def kernel(*refs):
+        all_ref, out, hits, bad, buf, sem = refs[len(kept) :]
         table = all_ref[:, 0, :]
         s = jnp.sum(table, axis=0, keepdims=True)
         lane = lax.broadcasted_iota(jnp.int32, (1, 128), 1)
@@ -219,10 +267,10 @@
         limit = clip_ratio * jnp.sqrt(jnp.full((1, 1), HID * COLS, F32))
         factor = jnp.minimum(1.0, limit / jnp.sqrt(square_total + epsilon))
         copies = []
-        for p in range(pieces):
-            span = pl.ds(p * rows, rows)
-            buf[0, p * rows : (p + 1) * rows, :] = agg_ref[0, p * rows : (p + 1) * rows, :] * factor
-            copies.append(pltpu.make_async_copy(buf.at[:, span], out.at[:, span], sem.at[p]))
+        for p, (i, r, first, step) in enumerate(spans):
+            there = pl.ds(first, step)
+            buf[0, first : first + step, :] = refs[i][0, r : r + step, :] * factor
+            copies.append(pltpu.make_async_copy(buf.at[:, there], out.at[:, there], sem.at[p]))
             copies[-1].start()
         most = jnp.max(table, axis=0, keepdims=True)
         hits[...] = pick(s, lane == 1)
@@ -236,13 +284,13 @@
     one = lambda t: jax.ShapeDtypeStruct((1, 1), t)
     return pl.pallas_call(
         kernel,
-        out_shape=(jax.ShapeDtypeStruct(agg.shape, F32), one(F32), one(jnp.int32)),
-        in_specs=[VMEM, VMEM],
+        out_shape=(jax.ShapeDtypeStruct(shape, F32), one(F32), one(jnp.int32)),
+        in_specs=[VMEM] * (len(kept) + 1),
         out_specs=(HBM, VMEM, VMEM),
-        scratch_shapes=[pltpu.VMEM(agg.shape, F32), pltpu.SemaphoreType.DMA((pieces,))],
+        scratch_shapes=[pltpu.VMEM(shape, F32), pltpu.SemaphoreType.DMA((len(spans),))],
         compiler_params=pltpu.CompilerParams(vmem_limit_bytes=8 * MIB),
         name="scale",
-    )(agg, gathered)
+    )(*[x for _, x in kept], gathered)
 
 
 def local(*args):
@@ -253,37 +301,46 @@
     n = lax.axis_size("dp")
     chunk = aggregate_prev.shape[1]
     unit = chunk // 16
-    me = lax.axis_index("dp").astype(jnp.int32).reshape(1)
-    args = (me, trigger[0], token_ids, hidden_acts, out_grad, stale)
+    args = (trigger, token_ids, hidden_acts, out_grad, stale)
 
     def swap(x, mask):
         return lax.ppermute(x, "dp", [(i, i ^ mask) for i in range(n)])
 
     outgoing = [[(m ^ bit, rows) for m, rows in parts] for _, bit, parts in RAW]
-    made = list(deltas(*args, outgoing[:1], chunk, 60 * 1024 * 1024))
-    made += deltas(*args, outgoing[1:], chunk, 16 * MIB)
+    made = list(deltas(*args, outgoing[:FIRST], chunk, 60 * 1024 * 1024))
+    rest = deltas(*args, outgoing[FIRST:] + [[key] for key in OWN_EARLY], chunk, 16 * MIB)
+    made += rest[: len(RAW) - FIRST]
     got = {label: swap(x, bit) for (label, bit, _), x in zip(RAW, made)}
-    own = dict(zip(OWN, deltas(*args, [[key] for key in OWN], chunk, 16 * MIB)))
+    own = dict(zip(OWN_EARLY, rest[len(RAW) - FIRST :]))
+    own.update(zip(OWN_LATE, deltas(*args, [[key] for key in OWN_LATE], chunk, 16 * MIB)))
     lost = [[] for _ in range(STAGES)]
     for label, bit, mine, others, group in SUMS:
         parts = [(own[mine], 0)] + [(got[name], k * mine[1][1] * unit) for name, k in others]
         total, energy = add_round(parts, mine[1][1] * unit)
         lost[group].append(energy)
         got[label] = swap(total, bit)
-    groups = []
-    for (first, count), mine, at, others in FINAL:
-        addends = [(own[mine], at * unit)] + [(got[name], k * unit) for name, k in others]
-        groups.append(((first * unit, count * unit), addends))
-    agg, kept, sums = finish(aggregate_prev, groups, lost, trigger)
+
+    def addends(table):
+        pieces = []
+        for (first, count), mine, others in table:
+            terms = [(own[mine], 0)] + [(got[name], k * count * unit) for name, k in others]
+            pieces.append(((first * unit, count * unit), terms))
+        return pieces
+
+    kept, sums = total_up(aggregate_prev, addends(FINAL), lost, trigger, ())
+    kept_last, sums = total_up(aggregate_prev, addends(LAST), [], trigger, (sums,))
     everyone = lax.all_to_all(sums, ("dp", "shard"), 0, 0, tiled=True)
+    kept = [(0, kept_last), (A0[1] * unit, kept)]
+    agg = store(kept)
     update, hits, bad = scale(kept, everyone)
 
     def again(state):
         mine = deltas(*args, [[(m, (0, 16))] for m in range(n)], chunk, 24 * MIB)
         came = [mine[0]] + [lax.ppermute(mine[m], "dp", [(i, i ^ m) for i in range(n)]) for m in range(1, n)]
-        new_agg, new_kept, new_sums = finish(aggregate_prev, [((0, chunk), [(x, 0) for x in came])], [], trigger)
-        new_update, _, _ = scale(new_kept, lax.all_to_all(new_sums, ("dp", "shard"), 0, 0, tiled=True))
-        return jnp.zeros((), jnp.int32), new_agg, new_update
+        whole = [((0, chunk), [(x, 0) for x in came])]
+        new_kept, new_sums = total_up(aggregate_prev, whole, [], trigger, ())
+        new_update, _, _ = scale([(0, new_kept)], lax.all_to_all(new_sums, ("dp", "shard"), 0, 0, tiled=True))
+        return jnp.zeros((), jnp.int32), new_kept, new_update
 
     _, agg, update = lax.while_loop(lambda state: state[0] > 0, again, (bad[0, 0], agg, update))
     return agg, update, hits[0, 0]

time: 83.8 us -> 81.9 us (0.977)
  blocking collectives: 11.1 us -> 0 us
  starting transfers between devices: 23.3 us -> 32.1 us
    all_to_all x1 -> x0, blocking collectives: 11.1 us -> none  [step(): everyone = lax.all_to_all(sums, ('dp', 'shard'), 0, 0, tiled=True)]
    ppermute x18 -> x19, waiting for transfers between devices: 32.5 us -> 26 us  [swap(): return lax.ppermute(x, 'dp', [(i, i ^ mask) for i in range(n)])]
    all_to_all x0 -> x1, waiting for transfers between devices: none -> 6.11 us  [step(): everyone = lax.all_to_all(sums, ('dp', 'shard'), 0, 0, tiled=True)]
    all_to_all x0 -> x1, starting transfers between devices: none -> 5.67 us  [step(): everyone = lax.all_to_all(sums, ('dp', 'shard'), 0, 0, tiled=True)]
    ppermute x18 -> x19, starting transfers between devices: 23.3 us -> 26.4 us  [swap(): return lax.ppermute(x, 'dp', [(i, i ^ mask) for i in range(n)])]
    pallas_call x2 -> x4, Pallas kernels: 3.03 us -> 3.88 us  [the longest x1 1.79 us: scale(): pl.pallas_call(kernel, out_shape=(jax.ShapeDtypeStruct(shape, F32), one(F...]
  transfers between devices with their start and end apart: 18 -> 20, of which waited for: 8 -> 11; matrix products, arithmetic and copies ran while one was open for 0% -> 0% of each run, Pallas kernels for 9% -> 13%
where the time goes in v2:
time: 81.9 us; the launch traced here: 81.7 us
  starting transfers between devices  32.1 us (39%)
  waiting for transfers between devices  32.1 us (39%)
  Pallas kernels  16 us (20%)
  between operations  0.82 us (1%)
    ppermute x19, starting transfers between devices, swap(): return lax.ppermute(x, 'dp', [(i, i ^ mask) for i in range(n)])  26.4 us
    ppermute x19, waiting for transfers between devices, swap(): return lax.ppermute(x, 'dp', [(i, i ^ mask) for i in range(n)])  26 us
    pallas_call x3, Pallas kernels, deltas(): pl.pallas_call(kernel, out_shape=tuple((jax.ShapeDtypeStruct((h, width),...  11.1 us
    all_to_all x1, waiting for transfers between devices, step(): everyone = lax.all_to_all(sums, ('dp', 'shard'), 0, 0, tiled=True)  6.11 us
    all_to_all x1, starting transfers between devices, step(): everyone = lax.all_to_all(sums, ('dp', 'shard'), 0, 0, tiled=True)  5.67 us
    pallas_call x1, Pallas kernels, scale(): pl.pallas_call(kernel, out_shape=(jax.ShapeDtypeStruct(shape, F32), one(F...  1.79 us
  transfers between devices with their start and end apart: 20, of which 11 were waited for; matrix products, arithmetic and copies ran while one was open for 0% of the time, Pallas kernels for 13%

profile of v2, /device:TPU:0, one launch (start us, length us, event | category | flops | bytes accessed | tf_op | source)
XLA Modules:
  0.0 81.7 jit_solution(2968515983414090380)
XLA Ops:
  0.7 3.0 %shard_map.88 = (bf16[96,1024]{1,0:T(8,128)(2,1)}, bf16[96,1024]{1,0:T(8,128)(2,1)}, bf16[96,1024]{1,0:T(8,128)(2,1)}) custom-call(s32[1,128]{1,0:T(1,128)} %trig_ref.3, s32[1,128]{1,0:T(1,128)} %tok_hbm.5, bf16[1,128,2048]{2,1,0:T(8,128)(2,1)} %acts_hbm.5, bf16[1,128,1024]{2,1,0:T(8,128)(2,1)} %og_hbm.5, bf16[1,2048,1024]{2,1,0:T(8,128)(2,1)} %stale_hbm.5), custom_call_target="tpu_custom_call" | custom-call | flops 75497472 | bytes 1179648 | tf_op jit(solution)/shard_map/pallas_call | solution.py:130
  3.7 3.1 %collective-permute-start.16 = (bf16[96,1024]{1,0:T(8,128)(2,1)}, bf16[96,1024]{1,0:T(8,128)(2,1)S(1)}, u32[]{:S(2)}, u32[]{:S(2)}) collective-permute-start(bf16[96,1024]{1,0:T(8,128)(2,1)} %get-tuple-element.122), channel_id=1, source_target_pairs={{0,8},{4,12},{8,0},{12,4},{16,24},{20,28},{24,16},{28,20},{1,9},{5... | collective-permute-start | bytes 589832 | tf_op jit(solution)/shard_map/ppermute | solution.py:307
  6.8 4.1 %shard_map.86 = (bf16[112,1024]{1,0:T(8,128)(2,1)S(1)}, bf16[96,1024]{1,0:T(8,128)(2,1)S(1)}, bf16[112,1024]{1,0:T(8,128)(2,1)S(1)}, bf16[96,1024]{1,0:T(8,128)(...) custom-call(s32[1,128]{1,0:T(1,128)S(1)} %copy-done.5, ...), custom_call_target="tpu_custom_call" | custom-call | flops 285212672 | bytes 4456448 | tf_op jit(solution)/shard_map/pallas_call | solution.py:130
  10.9 1.6 %collective-permute-start.23 = (bf16[112,1024]{1,0:T(8,128)(2,1)S(1)}, bf16[112,1024]{1,0:T(8,128)(2,1)S(1)}, u32[]{:S(2)}, u32[]{:S(2)}) collective-permute-start(bf16[112,1024]{1,0:T(8,128)(2,1)S(1)} %get-tuple-element.134), channel_id=1, source_target_pairs={{0,4},{4,0},{8,12},{12,8},{16,20},{20,16},{24,28},{28,24},{1,5},{5... | collective-permute-start | bytes 688136 | tf_op jit(solution)/shard_map/ppermute | solution.py:307
  12.5 0.5 collective-permute-start.11
  13.0 1.5 %collective-permute-start.10 = (bf16[96,1024]{1,0:T(8,128)(2,1)S(1)}, bf16[96,1024]{1,0:T(8,128)(2,1)S(1)}, u32[]{:S(2)}, u32[]{:S(2)}) collective-permute-start(bf16[96,1024]{1,0:T(8,128)(2,1)S(1)} %copy-done.7), channel_id=1, source_target_pairs={{0,4},{4,0},{8,12},{12,8},{16,20},{20,16},{24,28},{28,24},{1,5},{5... | collective-permute-start | bytes 589832 | tf_op jit(solution)/shard_map/ppermute | solution.py:307
  14.6 0.5 collective-permute-start.22
  15.1 0.4 collective-permute-start.14
  15.5 0.1 shard_map.92
  15.5 4.0 %collective-permute-done.23.refs_1_ = bf16[112,1024]{1,0:T(8,128)(2,1)S(1)} collective-permute-done((bf16[112,1024]{1,0:T(8,128)(2,1)S(1)}, bf16[112,1024]{1,0:T(8,128)(2,1)S(1)}, u32[]{:S(2)}, u32[]{:S(2)}) %collective-permute-start.23) | collective-permute-done | bytes 229408 | tf_op jit(solution)/shard_map/ppermute | solution.py:307
  19.5 0.1 shard_map.95
  19.6 1.6 %collective-permute-start.17 = (bf16[48,1024]{1,0:T(8,128)(2,1)S(1)}, bf16[48,1024]{1,0:T(8,128)(2,1)S(1)}, u32[]{:S(2)}, u32[]{:S(2)}) collective-permute-start(bf16[48,1024]{1,0:T(8,128)(2,1)S(1)} %get-tuple-element.124), channel_id=1, source_target_pairs={{0,4},{4,0},{8,12},{12,8},{16,20},{20,16},{24,28},{28,24},{1,5},{5... | collective-permute-start | bytes 294920 | tf_op jit(solution)/shard_map/ppermute | solution.py:307
  21.2 2.5 %collective-permute-done.11.refs_1_ = bf16[96,1024]{1,0:T(8,128)(2,1)S(1)} collective-permute-done((bf16[96,1024]{1,0:T(8,128)(2,1)S(1)}, bf16[96,1024]{1,0:T(8,128)(2,1)S(1)}, u32[]{:S(2)}, u32[]{:S(2)}) %collective-permute-start.11) | collective-permute-done | bytes 196640 | tf_op jit(solution)/shard_map/ppermute | solution.py:307
  23.7 1.5 %collective-permute-start.20 = (bf16[112,1024]{1,0:T(8,128)(2,1)S(1)}, bf16[112,1024]{1,0:T(8,128)(2,1)S(1)}, u32[]{:S(2)}, u32[]{:S(2)}) collective-permute-start(bf16[112,1024]{1,0:T(8,128)(2,1)S(1)} %get-tuple-element.129), channel_id=1, source_target_pairs={{0,4},{4,0},{8,12},{12,8},{16,20},{20,16},{24,28},{28,24},{1,5},{5... | collective-permute-start | bytes 688136 | tf_op jit(solution)/shard_map/ppermute | solution.py:307
  25.2 2.7 %collective-permute-done.10.refs_1_ = bf16[96,1024]{1,0:T(8,128)(2,1)S(1)} collective-permute-done((bf16[96,1024]{1,0:T(8,128)(2,1)S(1)}, bf16[96,1024]{1,0:T(8,128)(2,1)S(1)}, u32[]{:S(2)}, u32[]{:S(2)}) %collective-permute-start.10) | collective-permute-done | bytes 196640 | tf_op jit(solution)/shard_map/ppermute | solution.py:307
  27.9 0.3 collective-permute-start.24
  28.2 0.1 shard_map.89
  28.4 2.1 %collective-permute-start.8 = (bf16[96,1024]{1,0:T(8,128)(2,1)S(1)}, bf16[96,1024]{1,0:T(8,128)(2,1)S(1)}, u32[]{:S(2)}, u32[]{:S(2)}) collective-permute-start(bf16[96,1024]{1,0:T(8,128)(2,1)S(1)} %get-tuple-element.109), channel_id=1, source_target_pairs={{0,4},{4,0},{8,12},{12,8},{16,20},{20,16},{24,28},{28,24},{1,5},{5... | collective-permute-start | bytes 589832 | tf_op jit(solution)/shard_map/ppermute | solution.py:307
  30.4 2.4 %collective-permute-done.22.refs_1_ = bf16[112,1024]{1,0:T(8,128)(2,1)S(1)} collective-permute-done((bf16[112,1024]{1,0:T(8,128)(2,1)S(1)}, bf16[112,1024]{1,0:T(8,128)(2,1)S(1)}, u32[]{:S(2)}, u32[]{:S(2)}) %collective-permute-start.22) | collective-permute-done | bytes 229408 | tf_op jit(solution)/shard_map/ppermute | solution.py:307
  32.8 0.3 collective-permute-start.12
  33.2 1.8 %collective-permute-done.17.refs_2_ = bf16[48,1024]{1,0:T(8,128)(2,1)S(1)} collective-permute-done((bf16[48,1024]{1,0:T(8,128)(2,1)S(1)}, bf16[48,1024]{1,0:T(8,128)(2,1)S(1)}, u32[]{:S(2)}, u32[]{:S(2)}) %collective-permute-start.17) | collective-permute-done | bytes 98336 | tf_op jit(solution)/shard_map/ppermute | solution.py:307
  34.9 1.5 %collective-permute-start.19 = (bf16[112,1024]{1,0:T(8,128)(2,1)S(1)}, bf16[112,1024]{1,0:T(8,128)(2,1)S(1)}, u32[]{:S(2)}, u32[]{:S(2)}) collective-permute-start(bf16[112,1024]{1,0:T(8,128)(2,1)S(1)} %get-tuple-element.127), channel_id=1, source_target_pairs={{0,4},{4,0},{8,12},{12,8},{16,20},{20,16},{24,28},{28,24},{1,5},{5... | collective-permute-start | bytes 688136 | tf_op jit(solution)/shard_map/ppermute | solution.py:307
  36.5 4.0 %shard_map.85 = (bf16[48,1024]{1,0:T(8,128)(2,1)S(1)}, bf16[112,1024]{1,0:T(8,128)(2,1)S(1)}, bf16[48,1024]{1,0:T(8,128)(2,1)S(1)}, bf16[96,1024]{1,0:T(8,128)(2...) custom-call(s32[1,128]{1,0:T(1,128)S(1)} %copy-done.5, ...), custom_call_target="tpu_custom_call" | custom-call | flops 176160768 | bytes 2752512 | tf_op jit(solution)/shard_map/pallas_call | solution.py:130
  40.5 0.1 shard_map.91
  40.6 0.1 shard_map.93
  40.7 0.7 collective-permute-start.15
  41.4 2.6 %collective-permute-start.18 = (bf16[48,1024]{1,0:T(8,128)(2,1)S(1)}, bf16[48,1024]{1,0:T(8,128)(2,1)S(1)}, u32[]{:S(2)}, u32[]{:S(2)}) collective-permute-start(bf16[48,1024]{1,0:T(8,128)(2,1)S(1)} %get-tuple-element.125), channel_id=1, source_target_pairs={{0,16},{4,20},{8,24},{12,28},{16,0},{20,4},{24,8},{28,12},{1,17},{... | collective-permute-start | bytes 294920 | tf_op jit(solution)/shard_map/ppermute | solution.py:307
  44.0 0.1 shard_map.94
  44.1 0.2 shard_map.96
  44.3 0.9 %collective-permute-start.21 = (bf16[112,1024]{1,0:T(8,128)(2,1)S(1)}, bf16[112,1024]{1,0:T(8,128)(2,1)S(1)}, u32[]{:S(2)}, u32[]{:S(2)}) collective-permute-start(bf16[112,1024]{1,0:T(8,128)(2,1)S(1)} %get-tuple-element.130), channel_id=1, source_target_pairs={{0,8},{4,12},{8,0},{12,4},{16,24},{20,28},{24,16},{28,20},{1,9},{5... | collective-permute-start | bytes 688136 | tf_op jit(solution)/shard_map/ppermute | solution.py:307
  45.2 2.3 %collective-permute-start.25 = (bf16[112,1024]{1,0:T(8,128)(2,1)S(1)}, bf16[112,1024]{1,0:T(8,128)(2,1)S(1)}, u32[]{:S(2)}, u32[]{:S(2)}) collective-permute-start(bf16[112,1024]{1,0:T(8,128)(2,1)S(1)} %get-tuple-element.136), channel_id=1, source_target_pairs={{0,16},{4,20},{8,24},{12,28},{16,0},{20,4},{24,8},{28,12},{1,17},{... | collective-permute-start | bytes 688136 | tf_op jit(solution)/shard_map/ppermute | solution.py:307
  47.5 0.1 shard_map.87
  47.6 0.1 shard_map.90
  47.7 0.9 %collective-permute-done.19.refs_5_ = bf16[112,1024]{1,0:T(8,128)(2,1)S(1)} collective-permute-done((bf16[112,1024]{1,0:T(8,128)(2,1)S(1)}, bf16[112,1024]{1,0:T(8,128)(2,1)S(1)}, u32[]{:S(2)}, u32[]{:S(2)}) %collective-permute-start.19) | collective-permute-done | bytes 229408 | tf_op jit(solution)/shard_map/ppermute | solution.py:307
  48.6 1.5 %collective-permute-start.7 = (bf16[96,1024]{1,0:T(8,128)(2,1)S(1)}, bf16[96,1024]{1,0:T(8,128)(2,1)S(1)}, u32[]{:S(2)}, u32[]{:S(2)}) collective-permute-start(bf16[96,1024]{1,0:T(8,128)(2,1)S(1)} %get-tuple-element.107), channel_id=1, source_target_pairs={{0,4},{4,0},{8,12},{12,8},{16,20},{20,16},{24,28},{28,24},{1,5},{5... | collective-permute-start | bytes 589832 | tf_op jit(solution)/shard_map/ppermute | solution.py:307
  50.1 0.4 collective-permute-done.15.refs_2_
  50.5 0.3 collective-permute-start.9
  50.8 3.1 %collective-permute-start.13 = (bf16[96,1024]{1,0:T(8,128)(2,1)S(1)}, bf16[96,1024]{1,0:T(8,128)(2,1)S(1)}, u32[]{:S(2)}, u32[]{:S(2)}) collective-permute-start(bf16[96,1024]{1,0:T(8,128)(2,1)S(1)} %get-tuple-element.116), channel_id=1, source_target_pairs={{0,16},{4,20},{8,24},{12,28},{16,0},{20,4},{24,8},{28,12},{1,17},{... | collective-permute-start | bytes 589832 | tf_op jit(solution)/shard_map/ppermute | solution.py:307
  53.9 4.5 %collective-permute-done.21.refs_6_ = bf16[112,1024]{1,0:T(8,128)(2,1)S(1)} collective-permute-done((bf16[112,1024]{1,0:T(8,128)(2,1)S(1)}, bf16[112,1024]{1,0:T(8,128)(2,1)S(1)}, u32[]{:S(2)}, u32[]{:S(2)}) %collective-permute-start.21) | collective-permute-done | bytes 229408 | tf_op jit(solution)/shard_map/ppermute | solution.py:307
  58.4 0.3 shard_map.97
  58.7 3.5 %collective-permute-done.9.refs_2_ = bf16[96,1024]{1,0:T(8,128)(2,1)S(1)} collective-permute-done((bf16[96,1024]{1,0:T(8,128)(2,1)S(1)}, bf16[96,1024]{1,0:T(8,128)(2,1)S(1)}, u32[]{:S(2)}, u32[]{:S(2)}) %collective-permute-start.9) | collective-permute-done | bytes 196640 | tf_op jit(solution)/shard_map/ppermute | solution.py:307
  62.2 3.3 %collective-permute-done.13.refs_3_ = bf16[96,1024]{1,0:T(8,128)(2,1)S(1)} collective-permute-done((bf16[96,1024]{1,0:T(8,128)(2,1)S(1)}, bf16[96,1024]{1,0:T(8,128)(2,1)S(1)}, u32[]{:S(2)}, u32[]{:S(2)}) %collective-permute-start.13) | collective-permute-done | bytes 196640 | tf_op jit(solution)/shard_map/ppermute | solution.py:307
  65.6 0.8 %shard_map.98 = (f32[1,96,1024]{2,1,0:T(8,128)S(1)}, f32[32,1,128]{2,1,0:T(1,128)}) custom-call(s32[1,128]{1,0:T(1,128)S(1)} %copy-done.5, f32[1,256,1024]{2,1,0:T(8,128)S(1)} %copy-done.1, bf16[96,1024]{1,0:T(8,128)(2,1)S(1)} %get-tuple-element.106.refs_0_, bf16[96,1024]{1,0:T(8,128)(2,1)S(1)} %collective-permute-done.7.refs_1_, ...), custom_call_target="tpu_custom_call" | custom-call | tf_op jit(solution)/shard_map/pallas_call | solution.py:215
  66.4 5.7 %all-to-all-start.1 = ((f32[32,1,128]{2,1,0:T(1,128)}), f32[32,1,128]{2,1,0:T(1,128)S(1)}, u32[]{:S(2)}, u32[]{:S(2)}) async-start(f32[32,1,128]{2,1,0:T(1,128)} %get-tuple-element.149), calls=%async_computation.1 | async-start | bytes 32768 | tf_op jit(solution)/shard_map/all_to_all | solution.py:332
  72.1 1.0 %store.1 = f32[1,256,1024]{2,1,0:T(8,128)} custom-call(f32[1,96,1024]{2,1,0:T(8,128)S(1)} %get-tuple-element.147.refs_0_, f32[1,160,1024]{2,1,0:T(8,128)S(1)} %get-tuple-element.148.refs_1_), custom_call_target="tpu_custom_call" | custom-call | bytes 16777216 | tf_op jit(solution)/shard_map/store/pallas_call | solution.py:240
  73.1 6.1 %all-to-all-done.1.refs_2_ = f32[32,1,128]{2,1,0:T(1,128)S(1)} async-done(((f32[32,1,128]{2,1,0:T(1,128)}), f32[32,1,128]{2,1,0:T(1,128)S(1)}, u32[]{:S(2)}, u32[]{:S(2)}) %all-to-all-start.1) | async-done | bytes 16416 | tf_op jit(solution)/shard_map/all_to_all | solution.py:332
  79.2 1.8 %scale.3 = (f32[1,256,1024]{2,1,0:T(8,128)}, f32[1,1]{1,0:T(1,128)}, s32[1,1]{1,0:T(1,128)}) custom-call(f32[1,96,1024]{2,1,0:T(8,128)S(1)} %get-tuple-element.147.refs_0_, f32[1,160,1024]{2,1,0:T(8,128)S(1)} %get-tuple-element.148.refs_1_, f32[32,1,128]{2,1,0:T(1,128)S(1)} %all-to-all-done.1.refs_2_), custom_call_target="tpu_custom_call" | custom-call | tf_op jit(solution)/shard_map/scale/pallas_call | solution.py:285
  81.0 0.7 while.11
  (25 shorter events, 0.1 us)
Async XLA Ops:
  0.6 6.2 %copy-start.6 = (s32[1,128]{1,0:T(1,128)S(1)}, s32[1,128]{1,0:T(1,128)}, u32[]{:S(2)}) copy-start(s32[1,128]{1,0:T(1,128)} %tok_hbm.5) | copy-start | bytes 1540
  0.6 6.1 %copy-start.5 = (s32[1,128]{1,0:T(1,128)S(1)}, s32[1,128]{1,0:T(1,128)}, u32[]{:S(2)}) copy-start(s32[1,128]{1,0:T(1,128)} %trig_ref.3) | copy-start | bytes 1540
  0.7 6.1 %copy-start.3 = (bf16[1,128,2048]{2,1,0:T(8,128)(2,1)S(1)}, bf16[1,128,2048]{2,1,0:T(8,128)(2,1)}, u32[]{:S(2)}) copy-start(bf16[1,128,2048]{2,1,0:T(8,128)(2,1)} %acts_hbm.5) | copy-start | bytes 1572868
  0.7 6.1 %copy-start.4 = (bf16[1,128,1024]{2,1,0:T(8,128)(2,1)S(1)}, bf16[1,128,1024]{2,1,0:T(8,128)(2,1)}, u32[]{:S(2)}) copy-start(bf16[1,128,1024]{2,1,0:T(8,128)(2,1)} %og_hbm.5) | copy-start | bytes 786436
  3.6 8.9 %copy-start.8 = (bf16[96,1024]{1,0:T(8,128)(2,1)S(1)}, bf16[96,1024]{1,0:T(8,128)(2,1)}, u32[]{:S(2)}) copy-start(bf16[96,1024]{1,0:T(8,128)(2,1)} %get-tuple-element.114) | copy-start | bytes 589828
  3.6 9.4 %copy-start.7 = (bf16[96,1024]{1,0:T(8,128)(2,1)S(1)}, bf16[96,1024]{1,0:T(8,128)(2,1)}, u32[]{:S(2)}) copy-start(bf16[96,1024]{1,0:T(8,128)(2,1)} %get-tuple-element.112) | copy-start | bytes 589828
  3.7 32.8 %copy-start = (bf16[1,2048,1024]{2,1,0:T(8,128)(2,1)S(1)}, bf16[1,2048,1024]{2,1,0:T(8,128)(2,1)}, u32[]{:S(2)}) copy-start(bf16[1,2048,1024]{2,1,0:T(8,128)(2,1)} %stale_hbm.5) | copy-start | bytes 12582916
  3.7 11.4 %collective-permute-start.16 = (bf16[96,1024]{1,0:T(8,128)(2,1)}, bf16[96,1024]{1,0:T(8,128)(2,1)S(1)}, u32[]{:S(2)}, u32[]{:S(2)}) collective-permute-start(bf16[96,1024]{1,0:T(8,128)(2,1)} %get-tuple-element.122), channel_id=1, source_target_pairs={{0,8},{4,12},{8,0},{12,4},{16,24},{20,28},{24,16},{28,20},{1,9},{5... | collective-permute-start | bytes 589832 | tf_op jit(solution)/shard_map/ppermute | solution.py:307
  10.9 8.5 %collective-permute-start.23 = (bf16[112,1024]{1,0:T(8,128)(2,1)S(1)}, bf16[112,1024]{1,0:T(8,128)(2,1)S(1)}, u32[]{:S(2)}, u32[]{:S(2)}) collective-permute-start(bf16[112,1024]{1,0:T(8,128)(2,1)S(1)} %get-tuple-element.134), channel_id=1, source_target_pairs={{0,4},{4,0},{8,12},{12,8},{16,20},{20,16},{24,28},{28,24},{1,5},{5... | collective-permute-start | bytes 688136 | tf_op jit(solution)/shard_map/ppermute | solution.py:307
  12.5 11.2 %collective-permute-start.11 = (bf16[96,1024]{1,0:T(8,128)(2,1)S(1)}, bf16[96,1024]{1,0:T(8,128)(2,1)S(1)}, u32[]{:S(2)}, u32[]{:S(2)}) collective-permute-start(bf16[96,1024]{1,0:T(8,128)(2,1)S(1)} %copy-done.8), channel_id=1, source_target_pairs={{0,4},{4,0},{8,12},{12,8},{16,20},{20,16},{24,28},{28,24},{1,5},{5... | collective-permute-start | bytes 589832 | tf_op jit(solution)/shard_map/ppermute | solution.py:307
  13.0 14.9 %collective-permute-start.10 = (bf16[96,1024]{1,0:T(8,128)(2,1)S(1)}, bf16[96,1024]{1,0:T(8,128)(2,1)S(1)}, u32[]{:S(2)}, u32[]{:S(2)}) collective-permute-start(bf16[96,1024]{1,0:T(8,128)(2,1)S(1)} %copy-done.7), channel_id=1, source_target_pairs={{0,4},{4,0},{8,12},{12,8},{16,20},{20,16},{24,28},{28,24},{1,5},{5... | collective-permute-start | bytes 589832 | tf_op jit(solution)/shard_map/ppermute | solution.py:307
  14.6 18.3 %collective-permute-start.22 = (bf16[112,1024]{1,0:T(8,128)(2,1)S(1)}, bf16[112,1024]{1,0:T(8,128)(2,1)S(1)}, u32[]{:S(2)}, u32[]{:S(2)}) collective-permute-start(bf16[112,1024]{1,0:T(8,128)(2,1)S(1)} %get-tuple-element.132), channel_id=1, source_target_pairs={{0,4},{4,0},{8,12},{12,8},{16,20},{20,16},{24,28},{28,24},{1,5},{5... | collective-permute-start | bytes 688136 | tf_op jit(solution)/shard_map/ppermute | solution.py:307
  15.1 13.3 %collective-permute-start.14 = (bf16[96,1024]{1,0:T(8,128)(2,1)S(1)}, bf16[96,1024]{1,0:T(8,128)(2,1)S(1)}, u32[]{:S(2)}, u32[]{:S(2)}) collective-permute-start(bf16[96,1024]{1,0:T(8,128)(2,1)S(1)} %get-tuple-element.118), channel_id=1, source_target_pairs={{0,8},{4,12},{8,0},{12,4},{16,24},{20,28},{24,16},{28,20},{1,9},{5... | collective-permute-start | bytes 589832 | tf_op jit(solution)/shard_map/ppermute | solution.py:307
  19.6 38.8 %copy-start.1 = (f32[1,256,1024]{2,1,0:T(8,128)S(1)}, f32[1,256,1024]{2,1,0:T(8,128)}, u32[]{:S(2)}) copy-start(f32[1,256,1024]{2,1,0:T(8,128)} %prev_ref.3) | copy-start | bytes 3145732
  19.6 15.3 %collective-permute-start.17 = (bf16[48,1024]{1,0:T(8,128)(2,1)S(1)}, bf16[48,1024]{1,0:T(8,128)(2,1)S(1)}, u32[]{:S(2)}, u32[]{:S(2)}) collective-permute-start(bf16[48,1024]{1,0:T(8,128)(2,1)S(1)} %get-tuple-element.124), channel_id=1, source_target_pairs={{0,4},{4,0},{8,12},{12,8},{16,20},{20,16},{24,28},{28,24},{1,5},{5... | collective-permute-start | bytes 294920 | tf_op jit(solution)/shard_map/ppermute | solution.py:307
  23.7 17.0 %collective-permute-start.20 = (bf16[112,1024]{1,0:T(8,128)(2,1)S(1)}, bf16[112,1024]{1,0:T(8,128)(2,1)S(1)}, u32[]{:S(2)}, u32[]{:S(2)}) collective-permute-start(bf16[112,1024]{1,0:T(8,128)(2,1)S(1)} %get-tuple-element.129), channel_id=1, source_target_pairs={{0,4},{4,0},{8,12},{12,8},{16,20},{20,16},{24,28},{28,24},{1,5},{5... | collective-permute-start | bytes 688136 | tf_op jit(solution)/shard_map/ppermute | solution.py:307
  27.9 13.5 %collective-permute-start.24 = (bf16[112,1024]{1,0:T(8,128)(2,1)S(1)}, bf16[112,1024]{1,0:T(8,128)(2,1)S(1)}, u32[]{:S(2)}, u32[]{:S(2)}) collective-permute-start(bf16[112,1024]{1,0:T(8,128)(2,1)S(1)} %get-tuple-element.135), channel_id=1, source_target_pairs={{0,8},{4,12},{8,0},{12,4},{16,24},{20,28},{24,16},{28,20},{1,9},{5... | collective-permute-start | bytes 688136 | tf_op jit(solution)/shard_map/ppermute | solution.py:307
  28.4 15.9 %collective-permute-start.8 = (bf16[96,1024]{1,0:T(8,128)(2,1)S(1)}, bf16[96,1024]{1,0:T(8,128)(2,1)S(1)}, u32[]{:S(2)}, u32[]{:S(2)}) collective-permute-start(bf16[96,1024]{1,0:T(8,128)(2,1)S(1)} %get-tuple-element.109), channel_id=1, source_target_pairs={{0,4},{4,0},{8,12},{12,8},{16,20},{20,16},{24,28},{28,24},{1,5},{5... | collective-permute-start | bytes 589832 | tf_op jit(solution)/shard_map/ppermute | solution.py:307
  32.8 12.3 %collective-permute-start.12 = (bf16[96,1024]{1,0:T(8,128)(2,1)S(1)}, bf16[96,1024]{1,0:T(8,128)(2,1)S(1)}, u32[]{:S(2)}, u32[]{:S(2)}) collective-permute-start(bf16[96,1024]{1,0:T(8,128)(2,1)S(1)} %get-tuple-element.115), channel_id=1, source_target_pairs={{0,8},{4,12},{8,0},{12,4},{16,24},{20,28},{24,16},{28,20},{1,9},{5... | collective-permute-start | bytes 589832 | tf_op jit(solution)/shard_map/ppermute | solution.py:307
  34.9 13.7 %collective-permute-start.19 = (bf16[112,1024]{1,0:T(8,128)(2,1)S(1)}, bf16[112,1024]{1,0:T(8,128)(2,1)S(1)}, u32[]{:S(2)}, u32[]{:S(2)}) collective-permute-start(bf16[112,1024]{1,0:T(8,128)(2,1)S(1)} %get-tuple-element.127), channel_id=1, source_target_pairs={{0,4},{4,0},{8,12},{12,8},{16,20},{20,16},{24,28},{28,24},{1,5},{5... | collective-permute-start | bytes 688136 | tf_op jit(solution)/shard_map/ppermute | solution.py:307
  40.7 9.8 %collective-permute-start.15 = (bf16[48,1024]{1,0:T(8,128)(2,1)S(1)}, bf16[48,1024]{1,0:T(8,128)(2,1)S(1)}, u32[]{:S(2)}, u32[]{:S(2)}) collective-permute-start(bf16[48,1024]{1,0:T(8,128)(2,1)S(1)} %get-tuple-element.120), channel_id=1, source_target_pairs={{0,4},{4,0},{8,12},{12,8},{16,20},{20,16},{24,28},{28,24},{1,5},{5... | collective-permute-start | bytes 294920 | tf_op jit(solution)/shard_map/ppermute | solution.py:307
  41.4 9.5 %collective-permute-start.18 = (bf16[48,1024]{1,0:T(8,128)(2,1)S(1)}, bf16[48,1024]{1,0:T(8,128)(2,1)S(1)}, u32[]{:S(2)}, u32[]{:S(2)}) collective-permute-start(bf16[48,1024]{1,0:T(8,128)(2,1)S(1)} %get-tuple-element.125), channel_id=1, source_target_pairs={{0,16},{4,20},{8,24},{12,28},{16,0},{20,4},{24,8},{28,12},{1,17},{... | collective-permute-start | bytes 294920 | tf_op jit(solution)/shard_map/ppermute | solution.py:307
  44.3 14.2 %collective-permute-start.21 = (bf16[112,1024]{1,0:T(8,128)(2,1)S(1)}, bf16[112,1024]{1,0:T(8,128)(2,1)S(1)}, u32[]{:S(2)}, u32[]{:S(2)}) collective-permute-start(bf16[112,1024]{1,0:T(8,128)(2,1)S(1)} %get-tuple-element.130), channel_id=1, source_target_pairs={{0,8},{4,12},{8,0},{12,4},{16,24},{20,28},{24,16},{28,20},{1,9},{5... | collective-permute-start | bytes 688136 | tf_op jit(solution)/shard_map/ppermute | solution.py:307
  45.2 13.3 %collective-permute-start.25 = (bf16[112,1024]{1,0:T(8,128)(2,1)S(1)}, bf16[112,1024]{1,0:T(8,128)(2,1)S(1)}, u32[]{:S(2)}, u32[]{:S(2)}) collective-permute-start(bf16[112,1024]{1,0:T(8,128)(2,1)S(1)} %get-tuple-element.136), channel_id=1, source_target_pairs={{0,16},{4,20},{8,24},{12,28},{16,0},{20,4},{24,8},{28,12},{1,17},{... | collective-permute-start | bytes 688136 | tf_op jit(solution)/shard_map/ppermute | solution.py:307
  48.6 10.1 %collective-permute-start.7 = (bf16[96,1024]{1,0:T(8,128)(2,1)S(1)}, bf16[96,1024]{1,0:T(8,128)(2,1)S(1)}, u32[]{:S(2)}, u32[]{:S(2)}) collective-permute-start(bf16[96,1024]{1,0:T(8,128)(2,1)S(1)} %get-tuple-element.107), channel_id=1, source_target_pairs={{0,4},{4,0},{8,12},{12,8},{16,20},{20,16},{24,28},{28,24},{1,5},{5... | collective-permute-start | bytes 589832 | tf_op jit(solution)/shard_map/ppermute | solution.py:307
  50.5 11.8 %collective-permute-start.9 = (bf16[96,1024]{1,0:T(8,128)(2,1)S(1)}, bf16[96,1024]{1,0:T(8,128)(2,1)S(1)}, u32[]{:S(2)}, u32[]{:S(2)}) collective-permute-start(bf16[96,1024]{1,0:T(8,128)(2,1)S(1)} %get-tuple-element.110), channel_id=1, source_target_pairs={{0,8},{4,12},{8,0},{12,4},{16,24},{20,28},{24,16},{28,20},{1,9},{5... | collective-permute-start | bytes 589832 | tf_op jit(solution)/shard_map/ppermute | solution.py:307
  50.8 14.7 %collective-permute-start.13 = (bf16[96,1024]{1,0:T(8,128)(2,1)S(1)}, bf16[96,1024]{1,0:T(8,128)(2,1)S(1)}, u32[]{:S(2)}, u32[]{:S(2)}) collective-permute-start(bf16[96,1024]{1,0:T(8,128)(2,1)S(1)} %get-tuple-element.116), channel_id=1, source_target_pairs={{0,16},{4,20},{8,24},{12,28},{16,0},{20,4},{24,8},{28,12},{1,17},{... | collective-permute-start | bytes 589832 | tf_op jit(solution)/shard_map/ppermute | solution.py:307
  66.4 12.8 %all-to-all-start.1 = ((f32[32,1,128]{2,1,0:T(1,128)}), f32[32,1,128]{2,1,0:T(1,128)S(1)}, u32[]{:S(2)}, u32[]{:S(2)}) async-start(f32[32,1,128]{2,1,0:T(1,128)} %get-tuple-element.149), calls=%async_computation.1 | async-start | bytes 32768 | tf_op jit(solution)/shard_map/all_to_all | solution.py:332

commit v3 on v2

--- a/solution.py
+++ b/solution.py
@@ -19,7 +19,7 @@
 SMEM = pl.BlockSpec(memory_space=pltpu.SMEM)
 HBM = pl.BlockSpec(memory_space=pltpu.HBM)
 
-A0, A1, B = (0, 6), (6, 7), (13, 3)
+A0, A1, B = (0, 6), (6, 6), (12, 4)
 RAW = (
     ("y6a", 1, ((6, A0),)),
     ("zb0", 2, ((5, B), (4, B))),
@@ -62,70 +62,65 @@
     return total
 
 
-def deltas(trig, tok, acts, og, stale, messages, chunk, limit):
+def plan(messages, chunk):
+    unit = chunk // 16
+    pieces, heights = [], []
+    for i, message in enumerate(messages):
+        at = 0
+        for mask, (first, count) in message:
+            pieces.append((i, at, mask, first * unit, count * unit))
+            at += count * unit
+        heights.append(at)
+    return pieces, list(dict.fromkeys(p[2] for p in pieces)), heights
+
+
+def piece_rows(weights, og, old, trig_ref, block, out):
+    gradient = jnp.dot(weights, og, preferred_element_type=F32)
+    for b in range(0, gradient.shape[0], BLOCK):
+        flag = trig_ref[0, block + b // BLOCK].astype(F32)
+        out[b : b + BLOCK, :] = (flag * (gradient[b : b + BLOCK] - old(b).astype(F32))).astype(BF16)
+
+
+def deltas_first(trig, tok, acts, og, stale, messages, chunk):
     tokens, width = og.shape[1], og.shape[2]
-    unit = chunk // 16
-    pieces = [(i, m, r) for i, message in enumerate(messages) for m, r in message]
-    masks = list(dict.fromkeys(m for _, m, _ in pieces))
-    heights = [sum(r[1] for _, r in message) * unit for message in messages]
-    total = sum(heights)
-    n_out = len(messages)
+    pieces, masks, heights = plan(messages, chunk)
+    total, n_out = sum(heights), len(messages)
 
     def kernel(trig_hbm, tok_hbm, acts_hbm, og_hbm, stale_hbm, *refs):
         outs = refs[:n_out]
-        acts_buf, og_buf, stale_buf, tok_ref, trig_ref, small, sem = refs[n_out:]
+        acts_buf, og_buf, stale_buf, tok_ref, trig_ref, sem = refs[n_out : n_out + 6]
         me = lax.axis_index("dp")
         start = {m: pl.multiple_of((me ^ m) * chunk, chunk) for m in masks}
-        tok_copy = pltpu.make_async_copy(tok_hbm, tok_ref, small.at[0])
-        trig_copy = pltpu.make_async_copy(trig_hbm, trig_ref, small.at[1])
-        og_copy = pltpu.make_async_copy(og_hbm.at[0], og_buf, sem.at[0])
-        act_copies, stale_copies = {}, []
-        for j, m in enumerate(masks):
-            act_copies[m] = pltpu.make_async_copy(
-                acts_hbm.at[0, :, pl.ds(start[m], chunk)], acts_buf.at[j], sem.at[1 + j]
-            )
-        at = 0
-        for j, (_, m, (first, count)) in enumerate(pieces):
-            rows = pl.ds(pl.multiple_of(start[m] + first * unit, unit), count * unit)
-            stale_copies.append(
-                pltpu.make_async_copy(
-                    stale_hbm.at[0, rows, :], stale_buf.at[pl.ds(at, count * unit), :], sem.at[1 + len(masks) + j]
-                )
-            )
-            at += count * unit
-        act_copies[masks[0]].start()
-        og_copy.start()
-        begun = {masks[0]}
-        for j, (_, m, _) in enumerate(pieces):
-            if m not in begun:
-                act_copies[m].start()
-                begun.add(m)
-            stale_copies[j].start()
-            if j == 0:
-                tok_copy.start()
-                trig_copy.start()
+        sems = iter(range(3 + len(masks) + len(pieces)))
+        begin = lambda source, target: pltpu.make_async_copy(source, target, sem.at[next(sems)])
+        acts_of = lambda j: begin(acts_hbm.at[0, :, pl.ds(start[masks[j]], chunk)], acts_buf.at[j])
+        first_acts, og_copy = acts_of(0), begin(og_hbm.at[0], og_buf)
+        tok_copy, trig_copy = begin(tok_hbm, tok_ref), begin(trig_hbm, trig_ref)
+        stale_copies, at = [], 0
+        for _, _, m, first, rows in pieces:
+            source = stale_hbm.at[0, pl.ds(pl.multiple_of(start[m] + first, BLOCK), rows), :]
+            stale_copies.append(begin(source, stale_buf.at[pl.ds(at, rows), :]))
+            at += rows
+        act_copies = [first_acts] + [acts_of(j) for j in range(1, len(masks))]
+        for copy in [first_acts, og_copy, stale_copies[0], tok_copy, trig_copy] + act_copies[1:] + stale_copies[1:]:
+            copy.start()
         tok_copy.wait()
         trig_copy.wait()
         real = (tok_ref[...] != 0).astype(BF16)
-        weights = {}
-        at, offset, last = 0, 0, -1
-        for j, (i, m, (first, count)) in enumerate(pieces):
-            offset = 0 if i != last else offset
-            last = i
+        weights, at = {}, 0
+        for j, (i, offset, m, first, rows) in enumerate(pieces):
             if m not in weights:
-                act_copies[m].wait()
+                act_copies[masks.index(m)].wait()
                 weights[m] = acts_buf[masks.index(m)].T * real
             if j == 0:
                 og_copy.wait()
-            part = weights[m][first * unit : (first + count) * unit]
-            gradient = jnp.dot(part, og_buf[...], preferred_element_type=F32)
             stale_copies[j].wait()
-            for b in range(0, count * unit, BLOCK):
-                flag = trig_ref[0, (start[m] + first * unit + b) // BLOCK].astype(F32)
-                old = stale_buf[at + b : at + b + BLOCK, :].astype(F32)
-                outs[i][offset + b : offset + b + BLOCK, :] = (flag * (gradient[b : b + BLOCK] - old)).astype(BF16)
-            at += count * unit
-            offset += count * unit
+            old = lambda b, at=at: stale_buf[at + b : at + b + BLOCK, :]
+            block = (start[m] + first) // BLOCK
+            piece_rows(
+                weights[m][first : first + rows], og_buf[...], old, trig_ref, block, outs[i].at[pl.ds(offset, rows), :]
+            )
+            at += rows
 
     return pl.pallas_call(
         kernel,
@@ -138,13 +133,49 @@
             pltpu.VMEM((total, width), BF16),
             pltpu.VMEM(tok.shape, jnp.int32),
             pltpu.SMEM(trig.shape, jnp.int32),
-            pltpu.SemaphoreType.DMA((2,)),
-            pltpu.SemaphoreType.DMA((1 + len(masks) + len(pieces),)),
+            pltpu.SemaphoreType.DMA((4 + len(masks) + len(pieces),)),
         ],
         cost_estimate=pl.CostEstimate(
             flops=2 * tokens * total * width, bytes_accessed=total * width * 4, transcendentals=0
         ),
-        compiler_params=pltpu.CompilerParams(vmem_limit_bytes=limit),
+        compiler_params=pltpu.CompilerParams(vmem_limit_bytes=16 * MIB),
+    )(trig, tok, acts, og, stale)
+
+
+def deltas(trig, tok, acts, og, stale, messages, chunk):
+    tokens, width = og.shape[1], og.shape[2]
+    pieces, masks, heights = plan(messages, chunk)
+
+    def kernel(trig_hbm, tok_ref, acts_ref, og_ref, stale_ref, *refs):
+        outs, (trig_ref, sem) = refs[:-2], refs[-2:]
+        trig_copy = pltpu.make_async_copy(trig_hbm, trig_ref, sem.at[0])
+        trig_copy.start()
+        me = lax.axis_index("dp")
+        start = {m: pl.multiple_of((me ^ m) * chunk, chunk) for m in masks}
+        real = (tok_ref[...] != 0).astype(BF16)
+        weights = {}
+        for j, (i, offset, m, first, rows) in enumerate(pieces):
+            if m not in weights:
+                weights[m] = acts_ref[0, :, pl.ds(start[m], chunk)].T * real
+            if j == 0:
+                trig_copy.wait()
+            old = lambda b, m=m, first=first: stale_ref[0, pl.ds(pl.multiple_of(start[m] + first + b, BLOCK), BLOCK), :]
+            block = (start[m] + first) // BLOCK
+            piece_rows(
+                weights[m][first : first + rows], og_ref[0], old, trig_ref, block, outs[i].at[pl.ds(offset, rows), :]
+            )
+
+    total = sum(heights)
+    return pl.pallas_call(
+        kernel,
+        out_shape=tuple(jax.ShapeDtypeStruct((h, width), BF16) for h in heights),
+        in_specs=[HBM] + [VMEM] * 4,
+        out_specs=tuple(VMEM for _ in messages),
+        scratch_shapes=[pltpu.SMEM(trig.shape, jnp.int32), pltpu.SemaphoreType.DMA((1,))],
+        cost_estimate=pl.CostEstimate(
+            flops=2 * tokens * total * width, bytes_accessed=total * width * 4, transcendentals=0
+        ),
+        compiler_params=pltpu.CompilerParams(vmem_limit_bytes=16 * MIB),
     )(trig, tok, acts, og, stale)
 
 
@@ -258,7 +289,7 @@
         spans += [(i, r, first + r, step) for r in range(0, x.shape[1], step)]
 
     def kernel(*refs):
-        all_ref, out, hits, bad, buf, sem = refs[len(kept) :]
+        all_ref, out, hits_out, bad_out, buf, hits, bad, sem = refs[len(kept) :]
         table = all_ref[:, 0, :]
         s = jnp.sum(table, axis=0, keepdims=True)
         lane = lax.broadcasted_iota(jnp.int32, (1, 128), 1)
@@ -273,11 +304,16 @@
             copies.append(pltpu.make_async_copy(buf.at[:, there], out.at[:, there], sem.at[p]))
             copies[-1].start()
         most = jnp.max(table, axis=0, keepdims=True)
+        n = len(spans)
         hits[...] = pick(s, lane == 1)
         roundings = (lane >= 2) & (lane < 2 + STAGES)
         room = (ROUNDING * ROUNDING / STAGES) * square_total
         over = (pick(s, roundings) > room) | (devices * pick(most, roundings) > 2.0 * room)
         bad[...] = over.astype(jnp.int32)
+        copies.append(pltpu.make_async_copy(hits, hits_out, sem.at[n]))
+        copies.append(pltpu.make_async_copy(bad, bad_out, sem.at[n + 1]))
+        copies[n].start()
+        copies[n + 1].start()
         for c in copies:
             c.wait()
 
@@ -286,8 +322,13 @@
         kernel,
         out_shape=(jax.ShapeDtypeStruct(shape, F32), one(F32), one(jnp.int32)),
         in_specs=[VMEM] * (len(kept) + 1),
-        out_specs=(HBM, VMEM, VMEM),
-        scratch_shapes=[pltpu.VMEM(shape, F32), pltpu.SemaphoreType.DMA((len(spans),))],
+        out_specs=(HBM, HBM, HBM),
+        scratch_shapes=[
+            pltpu.VMEM(shape, F32),
+            pltpu.VMEM((1, 1), F32),
+            pltpu.VMEM((1, 1), jnp.int32),
+            pltpu.SemaphoreType.DMA((len(spans) + 2,)),
+        ],
         compiler_params=pltpu.CompilerParams(vmem_limit_bytes=8 * MIB),
         name="scale",
     )(*[x for _, x in kept], gathered)
@@ -307,12 +348,12 @@
         return lax.ppermute(x, "dp", [(i, i ^ mask) for i in range(n)])
 
     outgoing = [[(m ^ bit, rows) for m, rows in parts] for _, bit, parts in RAW]
-    made = list(deltas(*args, outgoing[:FIRST], chunk, 60 * 1024 * 1024))
-    rest = deltas(*args, outgoing[FIRST:] + [[key] for key in OWN_EARLY], chunk, 16 * MIB)
+    made = list(deltas_first(*args, outgoing[:FIRST], chunk))
+    rest = deltas(*args, outgoing[FIRST:] + [[key] for key in OWN_EARLY], chunk)
     made += rest[: len(RAW) - FIRST]
     got = {label: swap(x, bit) for (label, bit, _), x in zip(RAW, made)}
     own = dict(zip(OWN_EARLY, rest[len(RAW) - FIRST :]))
-    own.update(zip(OWN_LATE, deltas(*args, [[key] for key in OWN_LATE], chunk, 16 * MIB)))
+    own.update(zip(OWN_LATE, deltas(*args, [[key] for key in OWN_LATE], chunk)))
     lost = [[] for _ in range(STAGES)]
     for label, bit, mine, others, group in SUMS:
         parts = [(own[mine], 0)] + [(got[name], k * mine[1][1] * unit) for name, k in others]
@@ -335,7 +376,7 @@
     update, hits, bad = scale(kept, everyone)
 
     def again(state):
-        mine = deltas(*args, [[(m, (0, 16))] for m in range(n)], chunk, 24 * MIB)
+        mine = deltas(*args, [[(m, (0, 16))] for m in range(n)], chunk)
         came = [mine[0]] + [lax.ppermute(mine[m], "dp", [(i, i ^ m) for i in range(n)]) for m in range(1, n)]
         whole = [((0, chunk), [(x, 0) for x in came])]
         new_kept, new_sums = total_up(aggregate_prev, whole, [], trigger, ())

time: 81.9 us -> 78.2 us (0.955)
  starting transfers between devices: 32.1 us -> 36.9 us
  waiting for transfers between devices: 32.1 us -> 27.9 us
  Pallas kernels: 16 us -> 11.8 us
    pallas_call x3 -> x2, Pallas kernels: 11.1 us -> 5.53 us  [deltas(): pl.pallas_call(kernel, out_shape=tuple((jax.ShapeDtypeStruct((h, width),...]
    ppermute x19, starting transfers between devices: 26.4 us -> 31.2 us  [swap(): return lax.ppermute(x, 'dp', [(i, i ^ mask) for i in range(n)])]
    ppermute x19, waiting for transfers between devices: 26 us -> 21.8 us  [swap(): return lax.ppermute(x, 'dp', [(i, i ^ mask) for i in range(n)])]
    pallas_call x0 -> x1, Pallas kernels: none -> 1.99 us  [deltas_first(): pl.pallas_call(kernel, out_shape=tuple((jax.ShapeDtypeStruct((h, width),...]
  transfers between devices with their start and end apart: 20 -> 20, of which waited for: 11 -> 7; matrix products, arithmetic and copies ran while one was open for 0% -> 0% of each run, Pallas kernels for 13% -> 7%
where the time goes in v3:
time: 78.2 us; the launch traced here: 78 us
  starting transfers between devices  36.9 us (47%)
  waiting for transfers between devices  27.9 us (36%)
  Pallas kernels  11.8 us (15%)
  between operations  0.84 us (1%)
    ppermute x19, starting transfers between devices, swap(): return lax.ppermute(x, 'dp', [(i, i ^ mask) for i in range(n)])  31.2 us
    ppermute x19, waiting for transfers between devices, swap(): return lax.ppermute(x, 'dp', [(i, i ^ mask) for i in range(n)])  21.8 us
    all_to_all x1, waiting for transfers between devices, step(): everyone = lax.all_to_all(sums, ('dp', 'shard'), 0, 0, tiled=True)  6.11 us
    all_to_all x1, starting transfers between devices, step(): everyone = lax.all_to_all(sums, ('dp', 'shard'), 0, 0, tiled=True)  5.64 us
    pallas_call x2, Pallas kernels, deltas(): pl.pallas_call(kernel, out_shape=tuple((jax.ShapeDtypeStruct((h, width),...  5.53 us
    pallas_call x1, Pallas kernels, deltas_first(): pl.pallas_call(kernel, out_shape=tuple((jax.ShapeDtypeStruct((h, width),...  1.99 us
  transfers between devices with their start and end apart: 20, of which 7 were waited for; matrix products, arithmetic and copies ran while one was open for 0% of the time, Pallas kernels for 7%

profile of v3, /device:TPU:0, one launch (start us, length us, event | category | flops | bytes accessed | tf_op | source)
XLA Modules:
  0.0 78.0 jit_solution(6774689540590856542)
XLA Ops:
  0.7 0.0 copy-start
  0.7 4.3 %shard_map.86 = (bf16[96,1024]{1,0:T(8,128)(2,1)S(1)}, bf16[128,1024]{1,0:T(8,128)(2,1)S(1)}, bf16[96,1024]{1,0:T(8,128)(2,1)S(1)}, bf16[96,1024]{1,0:T(8,128)(2...) custom-call(s32[1,128]{1,0:T(1,128)} %trig_ref.3, ...), custom_call_target="tpu_custom_call" | custom-call | flops 276824064 | bytes 4325376 | tf_op jit(solution)/shard_map/pallas_call | solution.py:169
  5.0 3.0 %collective-permute-start.23 = (bf16[96,1024]{1,0:T(8,128)(2,1)S(1)}, bf16[96,1024]{1,0:T(8,128)(2,1)S(1)}, u32[]{:S(2)}, u32[]{:S(2)}) collective-permute-start(bf16[96,1024]{1,0:T(8,128)(2,1)S(1)} %get-tuple-element.134), channel_id=1, source_target_pairs={{0,4},{4,0},{8,12},{12,8},{16,20},{20,16},{24,28},{28,24},{1,5},{5... | collective-permute-start | bytes 589832 | tf_op jit(solution)/shard_map/ppermute | solution.py:348
  8.1 0.1 collective-permute-start.22
  8.2 2.0 %shard_map.88 = (bf16[96,1024]{1,0:T(8,128)(2,1)S(1)}, bf16[128,1024]{1,0:T(8,128)(2,1)S(1)}, bf16[96,1024]{1,0:T(8,128)(2,1)S(1)}) custom-call(s32[1,128]{1,0:T(1,128)S(1)} %copy-done.5, s32[1,128]{1,0:T(1,128)S(1)} %copy-done.6, bf16[1,128,2048]{2,1,0:T(8,128)(2,1)S(1)} %copy-done.3, bf16[1,128,1024]{2,1,0:T(8,128)(2,1)S(1)} %copy-done.4, ...), custom_call_target="tpu_custom_call" | custom-call | flops 83886080 | bytes 1310720 | tf_op jit(solution)/shard_map/pallas_call | solution.py:125
  10.2 2.0 %collective-permute-start.11 = (bf16[96,1024]{1,0:T(8,128)(2,1)S(1)}, bf16[96,1024]{1,0:T(8,128)(2,1)S(1)}, u32[]{:S(2)}, u32[]{:S(2)}) collective-permute-start(bf16[96,1024]{1,0:T(8,128)(2,1)S(1)} %get-tuple-element.114), channel_id=1, source_target_pairs={{0,4},{4,0},{8,12},{12,8},{16,20},{20,16},{24,28},{28,24},{1,5},{5... | collective-permute-start | bytes 589832 | tf_op jit(solution)/shard_map/ppermute | solution.py:348
  12.2 0.1 collective-permute-start.10
  12.3 2.0 %collective-permute-start.16 = (bf16[128,1024]{1,0:T(8,128)(2,1)S(1)}, bf16[128,1024]{1,0:T(8,128)(2,1)S(1)}, u32[]{:S(2)}, u32[]{:S(2)}) collective-permute-start(bf16[128,1024]{1,0:T(8,128)(2,1)S(1)} %get-tuple-element.122), channel_id=1, source_target_pairs={{0,8},{4,12},{8,0},{12,4},{16,24},{20,28},{24,16},{28,20},{1,9},{5... | collective-permute-start | bytes 786440 | tf_op jit(solution)/shard_map/ppermute | solution.py:348
  14.3 1.6 %collective-permute-start.14 = (bf16[128,1024]{1,0:T(8,128)(2,1)S(1)}, bf16[128,1024]{1,0:T(8,128)(2,1)S(1)}, u32[]{:S(2)}, u32[]{:S(2)}) collective-permute-start(bf16[128,1024]{1,0:T(8,128)(2,1)S(1)} %get-tuple-element.118), channel_id=1, source_target_pairs={{0,8},{4,12},{8,0},{12,4},{16,24},{20,28},{24,16},{28,20},{1,9},{5... | collective-permute-start | bytes 786440 | tf_op jit(solution)/shard_map/ppermute | solution.py:348
  15.9 2.1 %collective-permute-done.22.refs_1_ = bf16[96,1024]{1,0:T(8,128)(2,1)S(1)} collective-permute-done((bf16[96,1024]{1,0:T(8,128)(2,1)S(1)}, bf16[96,1024]{1,0:T(8,128)(2,1)S(1)}, u32[]{:S(2)}, u32[]{:S(2)}) %collective-permute-start.22) | collective-permute-done | bytes 196640 | tf_op jit(solution)/shard_map/ppermute | solution.py:348
  18.1 2.0 %collective-permute-start.20 = (bf16[96,1024]{1,0:T(8,128)(2,1)S(1)}, bf16[96,1024]{1,0:T(8,128)(2,1)S(1)}, u32[]{:S(2)}, u32[]{:S(2)}) collective-permute-start(bf16[96,1024]{1,0:T(8,128)(2,1)S(1)} %get-tuple-element.129), channel_id=1, source_target_pairs={{0,4},{4,0},{8,12},{12,8},{16,20},{20,16},{24,28},{28,24},{1,5},{5... | collective-permute-start | bytes 589832 | tf_op jit(solution)/shard_map/ppermute | solution.py:348
  20.1 0.1 shard_map.95
  20.2 2.1 %collective-permute-done.11.refs_1_ = bf16[96,1024]{1,0:T(8,128)(2,1)S(1)} collective-permute-done((bf16[96,1024]{1,0:T(8,128)(2,1)S(1)}, bf16[96,1024]{1,0:T(8,128)(2,1)S(1)}, u32[]{:S(2)}, u32[]{:S(2)}) %collective-permute-start.11) | collective-permute-done | bytes 196640 | tf_op jit(solution)/shard_map/ppermute | solution.py:348
  22.3 2.0 %collective-permute-start.8 = (bf16[96,1024]{1,0:T(8,128)(2,1)S(1)}, bf16[96,1024]{1,0:T(8,128)(2,1)S(1)}, u32[]{:S(2)}, u32[]{:S(2)}) collective-permute-start(bf16[96,1024]{1,0:T(8,128)(2,1)S(1)} %get-tuple-element.109), channel_id=1, source_target_pairs={{0,4},{4,0},{8,12},{12,8},{16,20},{20,16},{24,28},{28,24},{1,5},{5... | collective-permute-start | bytes 589832 | tf_op jit(solution)/shard_map/ppermute | solution.py:348
  24.3 2.2 %collective-permute-done.10.refs_1_ = bf16[96,1024]{1,0:T(8,128)(2,1)S(1)} collective-permute-done((bf16[96,1024]{1,0:T(8,128)(2,1)S(1)}, bf16[96,1024]{1,0:T(8,128)(2,1)S(1)}, u32[]{:S(2)}, u32[]{:S(2)}) %collective-permute-start.10) | collective-permute-done | bytes 196640 | tf_op jit(solution)/shard_map/ppermute | solution.py:348
  26.5 2.1 %collective-permute-start.24 = (bf16[96,1024]{1,0:T(8,128)(2,1)S(1)}, bf16[96,1024]{1,0:T(8,128)(2,1)S(1)}, u32[]{:S(2)}, u32[]{:S(2)}) collective-permute-start(bf16[96,1024]{1,0:T(8,128)(2,1)S(1)} %get-tuple-element.135), channel_id=1, source_target_pairs={{0,8},{4,12},{8,0},{12,4},{16,24},{20,28},{24,16},{28,20},{1,9},{5... | collective-permute-start | bytes 589832 | tf_op jit(solution)/shard_map/ppermute | solution.py:348
  28.6 0.1 shard_map.89
  28.7 0.0 copy-start.1
  28.7 2.0 %collective-permute-done.20.refs_1_ = bf16[96,1024]{1,0:T(8,128)(2,1)S(1)} collective-permute-done((bf16[96,1024]{1,0:T(8,128)(2,1)S(1)}, bf16[96,1024]{1,0:T(8,128)(2,1)S(1)}, u32[]{:S(2)}, u32[]{:S(2)}) %collective-permute-start.20) | collective-permute-done | bytes 196640 | tf_op jit(solution)/shard_map/ppermute | solution.py:348
  30.7 2.1 %collective-permute-start.12 = (bf16[96,1024]{1,0:T(8,128)(2,1)S(1)}, bf16[96,1024]{1,0:T(8,128)(2,1)S(1)}, u32[]{:S(2)}, u32[]{:S(2)}) collective-permute-start(bf16[96,1024]{1,0:T(8,128)(2,1)S(1)} %get-tuple-element.115), channel_id=1, source_target_pairs={{0,8},{4,12},{8,0},{12,4},{16,24},{20,28},{24,16},{28,20},{1,9},{5... | collective-permute-start | bytes 589832 | tf_op jit(solution)/shard_map/ppermute | solution.py:348
  32.8 0.0 collective-permute-done.16.refs_1_
  32.8 1.5 %collective-permute-start.19 = (bf16[96,1024]{1,0:T(8,128)(2,1)S(1)}, bf16[96,1024]{1,0:T(8,128)(2,1)S(1)}, u32[]{:S(2)}, u32[]{:S(2)}) collective-permute-start(bf16[96,1024]{1,0:T(8,128)(2,1)S(1)} %get-tuple-element.127), channel_id=1, source_target_pairs={{0,4},{4,0},{8,12},{12,8},{16,20},{20,16},{24,28},{28,24},{1,5},{5... | collective-permute-start | bytes 589832 | tf_op jit(solution)/shard_map/ppermute | solution.py:348
  34.3 1.2 %shard_map.85 = (bf16[64,1024]{1,0:T(8,128)(2,1)S(1)}, bf16[96,1024]{1,0:T(8,128)(2,1)S(1)}, bf16[64,1024]{1,0:T(8,128)(2,1)S(1)}, bf16[96,1024]{1,0:T(8,128)(2,...) custom-call(s32[1,128]{1,0:T(1,128)S(1)} %copy-done.5, ...), custom_call_target="tpu_custom_call" | custom-call | flops 176160768 | bytes 2752512 | tf_op jit(solution)/shard_map/pallas_call | solution.py:169
  35.5 0.1 shard_map.94
  35.6 0.5 collective-permute-start.21
  36.1 0.1 shard_map.92
  36.2 0.1 shard_map.91
  36.3 0.6 collective-permute-start.17
  36.9 0.0 collective-permute-done.24.refs_2_
  36.9 1.5 %collective-permute-start.15 = (bf16[64,1024]{1,0:T(8,128)(2,1)S(1)}, bf16[64,1024]{1,0:T(8,128)(2,1)S(1)}, u32[]{:S(2)}, u32[]{:S(2)}) collective-permute-start(bf16[64,1024]{1,0:T(8,128)(2,1)S(1)} %get-tuple-element.120), channel_id=1, source_target_pairs={{0,4},{4,0},{8,12},{12,8},{16,20},{20,16},{24,28},{28,24},{1,5},{5... | collective-permute-start | bytes 393224 | tf_op jit(solution)/shard_map/ppermute | solution.py:348
  38.4 0.1 shard_map.96
  38.5 2.7 %collective-permute-start.25 = (bf16[96,1024]{1,0:T(8,128)(2,1)S(1)}, bf16[96,1024]{1,0:T(8,128)(2,1)S(1)}, u32[]{:S(2)}, u32[]{:S(2)}) collective-permute-start(bf16[96,1024]{1,0:T(8,128)(2,1)S(1)} %get-tuple-element.136), channel_id=1, source_target_pairs={{0,16},{4,20},{8,24},{12,28},{16,0},{20,4},{24,8},{28,12},{1,17},{... | collective-permute-start | bytes 589832 | tf_op jit(solution)/shard_map/ppermute | solution.py:348
  41.2 0.1 shard_map.87
  41.3 0.1 shard_map.90
  41.4 2.0 %collective-permute-start.7 = (bf16[96,1024]{1,0:T(8,128)(2,1)S(1)}, bf16[96,1024]{1,0:T(8,128)(2,1)S(1)}, u32[]{:S(2)}, u32[]{:S(2)}) collective-permute-start(bf16[96,1024]{1,0:T(8,128)(2,1)S(1)} %get-tuple-element.107), channel_id=1, source_target_pairs={{0,4},{4,0},{8,12},{12,8},{16,20},{20,16},{24,28},{28,24},{1,5},{5... | collective-permute-start | bytes 589832 | tf_op jit(solution)/shard_map/ppermute | solution.py:348
  43.4 2.4 %collective-permute-start.9 = (bf16[96,1024]{1,0:T(8,128)(2,1)S(1)}, bf16[96,1024]{1,0:T(8,128)(2,1)S(1)}, u32[]{:S(2)}, u32[]{:S(2)}) collective-permute-start(bf16[96,1024]{1,0:T(8,128)(2,1)S(1)} %get-tuple-element.110), channel_id=1, source_target_pairs={{0,8},{4,12},{8,0},{12,4},{16,24},{20,28},{24,16},{28,20},{1,9},{5... | collective-permute-start | bytes 589832 | tf_op jit(solution)/shard_map/ppermute | solution.py:348
  45.8 0.1 collective-permute-done.15.refs_2_
  46.0 2.8 %collective-permute-start.13 = (bf16[96,1024]{1,0:T(8,128)(2,1)S(1)}, bf16[96,1024]{1,0:T(8,128)(2,1)S(1)}, u32[]{:S(2)}, u32[]{:S(2)}) collective-permute-start(bf16[96,1024]{1,0:T(8,128)(2,1)S(1)} %get-tuple-element.116), channel_id=1, source_target_pairs={{0,16},{4,20},{8,24},{12,28},{16,0},{20,4},{24,8},{28,12},{1,17},{... | collective-permute-start | bytes 589832 | tf_op jit(solution)/shard_map/ppermute | solution.py:348
  48.8 0.1 shard_map.93
  48.9 0.2 collective-permute-start.18
  49.1 13.2 %collective-permute-done.18.refs_3_ = bf16[64,1024]{1,0:T(8,128)(2,1)S(1)} collective-permute-done((bf16[64,1024]{1,0:T(8,128)(2,1)S(1)}, bf16[64,1024]{1,0:T(8,128)(2,1)S(1)}, u32[]{:S(2)}, u32[]{:S(2)}) %collective-permute-start.18) | collective-permute-done | bytes 131104 | tf_op jit(solution)/shard_map/ppermute | solution.py:348
  62.3 0.2 shard_map.97
  62.6 0.8 %shard_map.98 = (f32[1,96,1024]{2,1,0:T(8,128)S(1)}, f32[32,1,128]{2,1,0:T(1,128)}) custom-call(s32[1,128]{1,0:T(1,128)S(1)} %copy-done.5, f32[1,256,1024]{2,1,0:T(8,128)S(1)} %copy-done.1, bf16[96,1024]{1,0:T(8,128)(2,1)S(1)} %get-tuple-element.106.refs_0_, bf16[96,1024]{1,0:T(8,128)(2,1)S(1)} %collective-permute-done.7.refs_1_, ...), custom_call_target="tpu_custom_call" | custom-call | tf_op jit(solution)/shard_map/pallas_call | solution.py:246
  63.4 5.6 %all-to-all-start.1 = ((f32[32,1,128]{2,1,0:T(1,128)}), f32[32,1,128]{2,1,0:T(1,128)S(1)}, u32[]{:S(2)}, u32[]{:S(2)}) async-start(f32[32,1,128]{2,1,0:T(1,128)} %get-tuple-element.149), calls=%async_computation.1 | async-start | bytes 32768 | tf_op jit(solution)/shard_map/all_to_all | solution.py:373
  69.1 1.0 %store.1 = f32[1,256,1024]{2,1,0:T(8,128)} custom-call(f32[1,96,1024]{2,1,0:T(8,128)S(1)} %get-tuple-element.147.refs_0_, f32[1,160,1024]{2,1,0:T(8,128)S(1)} %get-tuple-element.148.refs_1_), custom_call_target="tpu_custom_call" | custom-call | bytes 16777216 | tf_op jit(solution)/shard_map/store/pallas_call | solution.py:271
  70.0 6.1 %all-to-all-done.1.refs_2_ = f32[32,1,128]{2,1,0:T(1,128)S(1)} async-done(((f32[32,1,128]{2,1,0:T(1,128)}), f32[32,1,128]{2,1,0:T(1,128)S(1)}, u32[]{:S(2)}, u32[]{:S(2)}) %all-to-all-start.1) | async-done | bytes 16416 | tf_op jit(solution)/shard_map/all_to_all | solution.py:373
  76.2 1.2 %scale.3 = (f32[1,256,1024]{2,1,0:T(8,128)}, f32[1,1]{1,0:T(1,128)}, s32[1,1]{1,0:T(1,128)}) custom-call(f32[1,96,1024]{2,1,0:T(8,128)S(1)} %get-tuple-element.147.refs_0_, f32[1,160,1024]{2,1,0:T(8,128)S(1)} %get-tuple-element.148.refs_1_, f32[32,1,128]{2,1,0:T(1,128)S(1)} %all-to-all-done.1.refs_2_), custom_call_target="tpu_custom_call" | custom-call | tf_op jit(solution)/shard_map/scale/pallas_call | solution.py:321
  77.4 0.6 while.11
  (21 shorter events, 0.0 us)
Async XLA Ops:
  0.6 7.5 %copy-start.6 = (s32[1,128]{1,0:T(1,128)S(1)}, s32[1,128]{1,0:T(1,128)}, u32[]{:S(2)}) copy-start(s32[1,128]{1,0:T(1,128)} %tok_hbm.1) | copy-start | bytes 1540
  0.6 7.5 %copy-start.5 = (s32[1,128]{1,0:T(1,128)S(1)}, s32[1,128]{1,0:T(1,128)}, u32[]{:S(2)}) copy-start(s32[1,128]{1,0:T(1,128)} %trig_ref.3) | copy-start | bytes 1540
  0.7 7.5 %copy-start = (bf16[1,2048,1024]{2,1,0:T(8,128)(2,1)S(1)}, bf16[1,2048,1024]{2,1,0:T(8,128)(2,1)}, u32[]{:S(2)}) copy-start(bf16[1,2048,1024]{2,1,0:T(8,128)(2,1)} %stale_hbm.1) | copy-start | bytes 12582916
  0.7 7.5 %copy-start.3 = (bf16[1,128,2048]{2,1,0:T(8,128)(2,1)S(1)}, bf16[1,128,2048]{2,1,0:T(8,128)(2,1)}, u32[]{:S(2)}) copy-start(bf16[1,128,2048]{2,1,0:T(8,128)(2,1)} %acts_hbm.1) | copy-start | bytes 1572868
  0.7 7.5 %copy-start.4 = (bf16[1,128,1024]{2,1,0:T(8,128)(2,1)S(1)}, bf16[1,128,1024]{2,1,0:T(8,128)(2,1)}, u32[]{:S(2)}) copy-start(bf16[1,128,1024]{2,1,0:T(8,128)(2,1)} %og_hbm.1) | copy-start | bytes 786436
  5.0 9.3 %collective-permute-start.23 = (bf16[96,1024]{1,0:T(8,128)(2,1)S(1)}, bf16[96,1024]{1,0:T(8,128)(2,1)S(1)}, u32[]{:S(2)}, u32[]{:S(2)}) collective-permute-start(bf16[96,1024]{1,0:T(8,128)(2,1)S(1)} %get-tuple-element.134), channel_id=1, source_target_pairs={{0,4},{4,0},{8,12},{12,8},{16,20},{20,16},{24,28},{28,24},{1,5},{5... | collective-permute-start | bytes 589832 | tf_op jit(solution)/shard_map/ppermute | solution.py:348
  8.1 10.0 %collective-permute-start.22 = (bf16[96,1024]{1,0:T(8,128)(2,1)S(1)}, bf16[96,1024]{1,0:T(8,128)(2,1)S(1)}, u32[]{:S(2)}, u32[]{:S(2)}) collective-permute-start(bf16[96,1024]{1,0:T(8,128)(2,1)S(1)} %get-tuple-element.132), channel_id=1, source_target_pairs={{0,4},{4,0},{8,12},{12,8},{16,20},{20,16},{24,28},{28,24},{1,5},{5... | collective-permute-start | bytes 589832 | tf_op jit(solution)/shard_map/ppermute | solution.py:348
  10.2 12.1 %collective-permute-start.11 = (bf16[96,1024]{1,0:T(8,128)(2,1)S(1)}, bf16[96,1024]{1,0:T(8,128)(2,1)S(1)}, u32[]{:S(2)}, u32[]{:S(2)}) collective-permute-start(bf16[96,1024]{1,0:T(8,128)(2,1)S(1)} %get-tuple-element.114), channel_id=1, source_target_pairs={{0,4},{4,0},{8,12},{12,8},{16,20},{20,16},{24,28},{28,24},{1,5},{5... | collective-permute-start | bytes 589832 | tf_op jit(solution)/shard_map/ppermute | solution.py:348
  12.2 14.3 %collective-permute-start.10 = (bf16[96,1024]{1,0:T(8,128)(2,1)S(1)}, bf16[96,1024]{1,0:T(8,128)(2,1)S(1)}, u32[]{:S(2)}, u32[]{:S(2)}) collective-permute-start(bf16[96,1024]{1,0:T(8,128)(2,1)S(1)} %get-tuple-element.112), channel_id=1, source_target_pairs={{0,4},{4,0},{8,12},{12,8},{16,20},{20,16},{24,28},{28,24},{1,5},{5... | collective-permute-start | bytes 589832 | tf_op jit(solution)/shard_map/ppermute | solution.py:348
  12.3 20.5 %collective-permute-start.16 = (bf16[128,1024]{1,0:T(8,128)(2,1)S(1)}, bf16[128,1024]{1,0:T(8,128)(2,1)S(1)}, u32[]{:S(2)}, u32[]{:S(2)}) collective-permute-start(bf16[128,1024]{1,0:T(8,128)(2,1)S(1)} %get-tuple-element.122), channel_id=1, source_target_pairs={{0,8},{4,12},{8,0},{12,4},{16,24},{20,28},{24,16},{28,20},{1,9},{5... | collective-permute-start | bytes 786440 | tf_op jit(solution)/shard_map/ppermute | solution.py:348
  14.3 21.3 %collective-permute-start.14 = (bf16[128,1024]{1,0:T(8,128)(2,1)S(1)}, bf16[128,1024]{1,0:T(8,128)(2,1)S(1)}, u32[]{:S(2)}, u32[]{:S(2)}) collective-permute-start(bf16[128,1024]{1,0:T(8,128)(2,1)S(1)} %get-tuple-element.118), channel_id=1, source_target_pairs={{0,8},{4,12},{8,0},{12,4},{16,24},{20,28},{24,16},{28,20},{1,9},{5... | collective-permute-start | bytes 786440 | tf_op jit(solution)/shard_map/ppermute | solution.py:348
  18.1 12.6 %collective-permute-start.20 = (bf16[96,1024]{1,0:T(8,128)(2,1)S(1)}, bf16[96,1024]{1,0:T(8,128)(2,1)S(1)}, u32[]{:S(2)}, u32[]{:S(2)}) collective-permute-start(bf16[96,1024]{1,0:T(8,128)(2,1)S(1)} %get-tuple-element.129), channel_id=1, source_target_pairs={{0,4},{4,0},{8,12},{12,8},{16,20},{20,16},{24,28},{28,24},{1,5},{5... | collective-permute-start | bytes 589832 | tf_op jit(solution)/shard_map/ppermute | solution.py:348
  22.3 14.0 %collective-permute-start.8 = (bf16[96,1024]{1,0:T(8,128)(2,1)S(1)}, bf16[96,1024]{1,0:T(8,128)(2,1)S(1)}, u32[]{:S(2)}, u32[]{:S(2)}) collective-permute-start(bf16[96,1024]{1,0:T(8,128)(2,1)S(1)} %get-tuple-element.109), channel_id=1, source_target_pairs={{0,4},{4,0},{8,12},{12,8},{16,20},{20,16},{24,28},{28,24},{1,5},{5... | collective-permute-start | bytes 589832 | tf_op jit(solution)/shard_map/ppermute | solution.py:348
  26.5 10.4 %collective-permute-start.24 = (bf16[96,1024]{1,0:T(8,128)(2,1)S(1)}, bf16[96,1024]{1,0:T(8,128)(2,1)S(1)}, u32[]{:S(2)}, u32[]{:S(2)}) collective-permute-start(bf16[96,1024]{1,0:T(8,128)(2,1)S(1)} %get-tuple-element.135), channel_id=1, source_target_pairs={{0,8},{4,12},{8,0},{12,4},{16,24},{20,28},{24,16},{28,20},{1,9},{5... | collective-permute-start | bytes 589832 | tf_op jit(solution)/shard_map/ppermute | solution.py:348
  28.7 33.6 %copy-start.1 = (f32[1,256,1024]{2,1,0:T(8,128)S(1)}, f32[1,256,1024]{2,1,0:T(8,128)}, u32[]{:S(2)}) copy-start(f32[1,256,1024]{2,1,0:T(8,128)} %prev_ref.3) | copy-start | bytes 3145732
  30.7 7.8 %collective-permute-start.12 = (bf16[96,1024]{1,0:T(8,128)(2,1)S(1)}, bf16[96,1024]{1,0:T(8,128)(2,1)S(1)}, u32[]{:S(2)}, u32[]{:S(2)}) collective-permute-start(bf16[96,1024]{1,0:T(8,128)(2,1)S(1)} %get-tuple-element.115), channel_id=1, source_target_pairs={{0,8},{4,12},{8,0},{12,4},{16,24},{20,28},{24,16},{28,20},{1,9},{5... | collective-permute-start | bytes 589832 | tf_op jit(solution)/shard_map/ppermute | solution.py:348
  32.8 8.7 %collective-permute-start.19 = (bf16[96,1024]{1,0:T(8,128)(2,1)S(1)}, bf16[96,1024]{1,0:T(8,128)(2,1)S(1)}, u32[]{:S(2)}, u32[]{:S(2)}) collective-permute-start(bf16[96,1024]{1,0:T(8,128)(2,1)S(1)} %get-tuple-element.127), channel_id=1, source_target_pairs={{0,4},{4,0},{8,12},{12,8},{16,20},{20,16},{24,28},{28,24},{1,5},{5... | collective-permute-start | bytes 589832 | tf_op jit(solution)/shard_map/ppermute | solution.py:348
  35.6 13.2 %collective-permute-start.21 = (bf16[96,1024]{1,0:T(8,128)(2,1)S(1)}, bf16[96,1024]{1,0:T(8,128)(2,1)S(1)}, u32[]{:S(2)}, u32[]{:S(2)}) collective-permute-start(bf16[96,1024]{1,0:T(8,128)(2,1)S(1)} %get-tuple-element.130), channel_id=1, source_target_pairs={{0,8},{4,12},{8,0},{12,4},{16,24},{20,28},{24,16},{28,20},{1,9},{5... | collective-permute-start | bytes 589832 | tf_op jit(solution)/shard_map/ppermute | solution.py:348
  36.3 7.1 %collective-permute-start.17 = (bf16[64,1024]{1,0:T(8,128)(2,1)S(1)}, bf16[64,1024]{1,0:T(8,128)(2,1)S(1)}, u32[]{:S(2)}, u32[]{:S(2)}) collective-permute-start(bf16[64,1024]{1,0:T(8,128)(2,1)S(1)} %get-tuple-element.124), channel_id=1, source_target_pairs={{0,4},{4,0},{8,12},{12,8},{16,20},{20,16},{24,28},{28,24},{1,5},{5... | collective-permute-start | bytes 393224 | tf_op jit(solution)/shard_map/ppermute | solution.py:348
  36.9 9.1 %collective-permute-start.15 = (bf16[64,1024]{1,0:T(8,128)(2,1)S(1)}, bf16[64,1024]{1,0:T(8,128)(2,1)S(1)}, u32[]{:S(2)}, u32[]{:S(2)}) collective-permute-start(bf16[64,1024]{1,0:T(8,128)(2,1)S(1)} %get-tuple-element.120), channel_id=1, source_target_pairs={{0,4},{4,0},{8,12},{12,8},{16,20},{20,16},{24,28},{28,24},{1,5},{5... | collective-permute-start | bytes 393224 | tf_op jit(solution)/shard_map/ppermute | solution.py:348
  38.5 23.7 %collective-permute-start.25 = (bf16[96,1024]{1,0:T(8,128)(2,1)S(1)}, bf16[96,1024]{1,0:T(8,128)(2,1)S(1)}, u32[]{:S(2)}, u32[]{:S(2)}) collective-permute-start(bf16[96,1024]{1,0:T(8,128)(2,1)S(1)} %get-tuple-element.136), channel_id=1, source_target_pairs={{0,16},{4,20},{8,24},{12,28},{16,0},{20,4},{24,8},{28,12},{1,17},{... | collective-permute-start | bytes 589832 | tf_op jit(solution)/shard_map/ppermute | solution.py:348
  41.4 21.1 %collective-permute-start.7 = (bf16[96,1024]{1,0:T(8,128)(2,1)S(1)}, bf16[96,1024]{1,0:T(8,128)(2,1)S(1)}, u32[]{:S(2)}, u32[]{:S(2)}) collective-permute-start(bf16[96,1024]{1,0:T(8,128)(2,1)S(1)} %get-tuple-element.107), channel_id=1, source_target_pairs={{0,4},{4,0},{8,12},{12,8},{16,20},{20,16},{24,28},{28,24},{1,5},{5... | collective-permute-start | bytes 589832 | tf_op jit(solution)/shard_map/ppermute | solution.py:348
  43.4 19.1 %collective-permute-start.9 = (bf16[96,1024]{1,0:T(8,128)(2,1)S(1)}, bf16[96,1024]{1,0:T(8,128)(2,1)S(1)}, u32[]{:S(2)}, u32[]{:S(2)}) collective-permute-start(bf16[96,1024]{1,0:T(8,128)(2,1)S(1)} %get-tuple-element.110), channel_id=1, source_target_pairs={{0,8},{4,12},{8,0},{12,4},{16,24},{20,28},{24,16},{28,20},{1,9},{5... | collective-permute-start | bytes 589832 | tf_op jit(solution)/shard_map/ppermute | solution.py:348
  46.0 16.6 %collective-permute-start.13 = (bf16[96,1024]{1,0:T(8,128)(2,1)S(1)}, bf16[96,1024]{1,0:T(8,128)(2,1)S(1)}, u32[]{:S(2)}, u32[]{:S(2)}) collective-permute-start(bf16[96,1024]{1,0:T(8,128)(2,1)S(1)} %get-tuple-element.116), channel_id=1, source_target_pairs={{0,16},{4,20},{8,24},{12,28},{16,0},{20,4},{24,8},{28,12},{1,17},{... | collective-permute-start | bytes 589832 | tf_op jit(solution)/shard_map/ppermute | solution.py:348
  48.9 13.4 %collective-permute-start.18 = (bf16[64,1024]{1,0:T(8,128)(2,1)S(1)}, bf16[64,1024]{1,0:T(8,128)(2,1)S(1)}, u32[]{:S(2)}, u32[]{:S(2)}) collective-permute-start(bf16[64,1024]{1,0:T(8,128)(2,1)S(1)} %get-tuple-element.125), channel_id=1, source_target_pairs={{0,16},{4,20},{8,24},{12,28},{16,0},{20,4},{24,8},{28,12},{1,17},{... | collective-permute-start | bytes 393224 | tf_op jit(solution)/shard_map/ppermute | solution.py:348
  63.4 12.7 %all-to-all-start.1 = ((f32[32,1,128]{2,1,0:T(1,128)}), f32[32,1,128]{2,1,0:T(1,128)S(1)}, u32[]{:S(2)}, u32[]{:S(2)}) async-start(f32[32,1,128]{2,1,0:T(1,128)} %get-tuple-element.149), calls=%async_computation.1 | async-start | bytes 32768 | tf_op jit(solution)/shard_map/all_to_all | solution.py:373

commit v4 on v3

--- a/solution.py
+++ b/solution.py
@@ -13,6 +13,7 @@
 MIB = 1 << 20
 PIECE = 64
 STAGES = 3
+KINDS = 6
 ROUNDING = 4.8e-4
 F32, BF16 = jnp.float32, jnp.bfloat16
 VMEM = pl.BlockSpec(memory_space=pltpu.VMEM)
@@ -32,16 +33,16 @@
     ("y0b", 1, ((0, A1),)),
     ("y0a", 1, ((0, A0),)),
 )
-FIRST = 3
+FIRST = 2
 OWN_EARLY = ((6, A0), (5, B), (4, A0), (6, A1))
 OWN_LATE = ((4, B), (4, A1), (1, B), (2, A0), (2, A1), (0, A0), (0, A1), (0, B))
 SUMS = (
     ("near0", 2, (6, A0), (("y6a", 0),), 0),
-    ("pairb5", 1, (5, B), (("zb0", 0),), 0),
+    ("pairb5", 1, (5, B), (("zb0", 0),), 3),
     ("quad0", 4, (4, A0), (("y4a", 0), ("near0", 0)), 1),
     ("near1", 2, (6, A1), (("y6b", 0),), 0),
-    ("pairb1", 1, (1, B), (("zb1", 0),), 2),
-    ("quadb", 4, (4, B), (("zb0", 1), ("pairb5", 0)), 1),
+    ("pairb1", 1, (1, B), (("zb1", 0),), 5),
+    ("quadb", 4, (4, B), (("zb0", 1), ("pairb5", 0)), 4),
     ("quad1", 4, (4, A1), (("y4b", 0), ("near1", 0)), 1),
     ("last0", 2, (2, A0), (("y2a", 0),), 2),
     ("last1", 2, (2, A1), (("y2b", 0),), 2),
@@ -306,7 +307,7 @@
         most = jnp.max(table, axis=0, keepdims=True)
         n = len(spans)
         hits[...] = pick(s, lane == 1)
-        roundings = (lane >= 2) & (lane < 2 + STAGES)
+        roundings = (lane >= 2) & (lane < 2 + KINDS)
         room = (ROUNDING * ROUNDING / STAGES) * square_total
         over = (pick(s, roundings) > room) | (devices * pick(most, roundings) > 2.0 * room)
         bad[...] = over.astype(jnp.int32)
@@ -354,7 +355,7 @@
     got = {label: swap(x, bit) for (label, bit, _), x in zip(RAW, made)}
     own = dict(zip(OWN_EARLY, rest[len(RAW) - FIRST :]))
     own.update(zip(OWN_LATE, deltas(*args, [[key] for key in OWN_LATE], chunk)))
-    lost = [[] for _ in range(STAGES)]
+    lost = [[] for _ in range(KINDS)]
     for label, bit, mine, others, group in SUMS:
         parts = [(own[mine], 0)] + [(got[name], k * mine[1][1] * unit) for name, k in others]
         total, energy = add_round(parts, mine[1][1] * unit)

time: 78.2 us -> 78.3 us (level)
  transfers between devices with their start and end apart: 20 -> 20, of which waited for: 7 -> 7; matrix products, arithmetic and copies ran while one was open for 0% -> 0% of each run, Pallas kernels for 7% -> 6%
where the time goes in v4:
time: 78.3 us; the launch traced here: 78.1 us
  starting transfers between devices  37.2 us (48%)
  waiting for transfers between devices  27.9 us (36%)
  Pallas kernels  11.4 us (15%)
  between operations  0.84 us (1%)
    ppermute x19, starting transfers between devices, swap(): return lax.ppermute(x, 'dp', [(i, i ^ mask) for i in range(n)])  31.6 us
    ppermute x19, waiting for transfers between devices, swap(): return lax.ppermute(x, 'dp', [(i, i ^ mask) for i in range(n)])  21.8 us
    all_to_all x1, waiting for transfers between devices, step(): everyone = lax.all_to_all(sums, ('dp', 'shard'), 0, 0, tiled=True)  6.11 us
    all_to_all x1, starting transfers between devices, step(): everyone = lax.all_to_all(sums, ('dp', 'shard'), 0, 0, tiled=True)  5.64 us
    pallas_call x2, Pallas kernels, deltas(): pl.pallas_call(kernel, out_shape=tuple((jax.ShapeDtypeStruct((h, width),...  5.57 us
    pallas_call x1, Pallas kernels, deltas_first(): pl.pallas_call(kernel, out_shape=tuple((jax.ShapeDtypeStruct((h, width),...  1.62 us
  transfers between devices with their start and end apart: 20, of which 7 were waited for; matrix products, arithmetic and copies ran while one was open for 0% of the time, Pallas kernels for 6%

profile of v4, /device:TPU:0, one launch (start us, length us, event | category | flops | bytes accessed | tf_op | source)
XLA Modules:
  0.0 78.1 jit_solution(4988631591631283355)
XLA Ops:
  0.7 0.0 copy-start
  0.7 4.4 %shard_map.86 = (bf16[96,1024]{1,0:T(8,128)(2,1)S(1)}, bf16[96,1024]{1,0:T(8,128)(2,1)S(1)}, bf16[128,1024]{1,0:T(8,128)(2,1)S(1)}, bf16[96,1024]{1,0:T(8,128)(2...) custom-call(s32[1,128]{1,0:T(1,128)} %trig_ref.3, ...), custom_call_target="tpu_custom_call" | custom-call | flops 301989888 | bytes 4718592 | tf_op jit(solution)/shard_map/pallas_call | solution.py:170
  5.1 3.1 %collective-permute-start.23 = (bf16[96,1024]{1,0:T(8,128)(2,1)S(1)}, bf16[96,1024]{1,0:T(8,128)(2,1)S(1)}, u32[]{:S(2)}, u32[]{:S(2)}) collective-permute-start(bf16[96,1024]{1,0:T(8,128)(2,1)S(1)} %get-tuple-element.134), channel_id=1, source_target_pairs={{0,4},{4,0},{8,12},{12,8},{16,20},{20,16},{24,28},{28,24},{1,5},{5... | collective-permute-start | bytes 589832 | tf_op jit(solution)/shard_map/ppermute | solution.py:349
  8.1 0.1 collective-permute-start.22
  8.2 1.6 %shard_map.88 = (bf16[96,1024]{1,0:T(8,128)(2,1)S(1)}, bf16[128,1024]{1,0:T(8,128)(2,1)S(1)}) custom-call(s32[1,128]{1,0:T(1,128)S(1)} %copy-done.5, s32[1,128]{1,0:T(1,128)S(1)} %copy-done.6, bf16[1,128,2048]{2,1,0:T(8,128)(2,1)S(1)} %copy-done.3, bf16[1,128,1024]{2,1,0:T(8,128)(2,1)S(1)} %copy-done.4, bf16[1,2048,1024]{2,1,0:T(8,128)(2,1)S(1)} %copy-done), custom_call_target="tpu_custom_call" | custom-call | flops 58720256 | bytes 917504 | tf_op jit(solution)/shard_map/pallas_call | solution.py:126
  9.9 2.0 %collective-permute-start.11 = (bf16[96,1024]{1,0:T(8,128)(2,1)S(1)}, bf16[96,1024]{1,0:T(8,128)(2,1)S(1)}, u32[]{:S(2)}, u32[]{:S(2)}) collective-permute-start(bf16[96,1024]{1,0:T(8,128)(2,1)S(1)} %get-tuple-element.114), channel_id=1, source_target_pairs={{0,4},{4,0},{8,12},{12,8},{16,20},{20,16},{24,28},{28,24},{1,5},{5... | collective-permute-start | bytes 589832 | tf_op jit(solution)/shard_map/ppermute | solution.py:349
  11.9 0.1 collective-permute-start.10
  12.0 2.0 %collective-permute-start.16 = (bf16[128,1024]{1,0:T(8,128)(2,1)S(1)}, bf16[128,1024]{1,0:T(8,128)(2,1)S(1)}, u32[]{:S(2)}, u32[]{:S(2)}) collective-permute-start(bf16[128,1024]{1,0:T(8,128)(2,1)S(1)} %get-tuple-element.122), channel_id=1, source_target_pairs={{0,8},{4,12},{8,0},{12,4},{16,24},{20,28},{24,16},{28,20},{1,9},{5... | collective-permute-start | bytes 786440 | tf_op jit(solution)/shard_map/ppermute | solution.py:349
  14.0 0.0 collective-permute-done.23.refs_1_
  14.0 2.0 %collective-permute-start.14 = (bf16[128,1024]{1,0:T(8,128)(2,1)S(1)}, bf16[128,1024]{1,0:T(8,128)(2,1)S(1)}, u32[]{:S(2)}, u32[]{:S(2)}) collective-permute-start(bf16[128,1024]{1,0:T(8,128)(2,1)S(1)} %get-tuple-element.118), channel_id=1, source_target_pairs={{0,8},{4,12},{8,0},{12,4},{16,24},{20,28},{24,16},{28,20},{1,9},{5... | collective-permute-start | bytes 786440 | tf_op jit(solution)/shard_map/ppermute | solution.py:349
  16.0 2.1 %collective-permute-done.22.refs_1_ = bf16[96,1024]{1,0:T(8,128)(2,1)S(1)} collective-permute-done((bf16[96,1024]{1,0:T(8,128)(2,1)S(1)}, bf16[96,1024]{1,0:T(8,128)(2,1)S(1)}, u32[]{:S(2)}, u32[]{:S(2)}) %collective-permute-start.22) | collective-permute-done | bytes 196640 | tf_op jit(solution)/shard_map/ppermute | solution.py:349
  18.1 2.0 %collective-permute-start.20 = (bf16[96,1024]{1,0:T(8,128)(2,1)S(1)}, bf16[96,1024]{1,0:T(8,128)(2,1)S(1)}, u32[]{:S(2)}, u32[]{:S(2)}) collective-permute-start(bf16[96,1024]{1,0:T(8,128)(2,1)S(1)} %get-tuple-element.129), channel_id=1, source_target_pairs={{0,4},{4,0},{8,12},{12,8},{16,20},{20,16},{24,28},{28,24},{1,5},{5... | collective-permute-start | bytes 589832 | tf_op jit(solution)/shard_map/ppermute | solution.py:349
  20.1 0.1 shard_map.95
  20.2 2.1 %collective-permute-done.11.refs_1_ = bf16[96,1024]{1,0:T(8,128)(2,1)S(1)} collective-permute-done((bf16[96,1024]{1,0:T(8,128)(2,1)S(1)}, bf16[96,1024]{1,0:T(8,128)(2,1)S(1)}, u32[]{:S(2)}, u32[]{:S(2)}) %collective-permute-start.11) | collective-permute-done | bytes 196640 | tf_op jit(solution)/shard_map/ppermute | solution.py:349
  22.3 2.0 %collective-permute-start.8 = (bf16[96,1024]{1,0:T(8,128)(2,1)S(1)}, bf16[96,1024]{1,0:T(8,128)(2,1)S(1)}, u32[]{:S(2)}, u32[]{:S(2)}) collective-permute-start(bf16[96,1024]{1,0:T(8,128)(2,1)S(1)} %get-tuple-element.109), channel_id=1, source_target_pairs={{0,4},{4,0},{8,12},{12,8},{16,20},{20,16},{24,28},{28,24},{1,5},{5... | collective-permute-start | bytes 589832 | tf_op jit(solution)/shard_map/ppermute | solution.py:349
  24.3 2.2 %collective-permute-done.10.refs_1_ = bf16[96,1024]{1,0:T(8,128)(2,1)S(1)} collective-permute-done((bf16[96,1024]{1,0:T(8,128)(2,1)S(1)}, bf16[96,1024]{1,0:T(8,128)(2,1)S(1)}, u32[]{:S(2)}, u32[]{:S(2)}) %collective-permute-start.10) | collective-permute-done | bytes 196640 | tf_op jit(solution)/shard_map/ppermute | solution.py:349
  26.5 2.1 %collective-permute-start.24 = (bf16[96,1024]{1,0:T(8,128)(2,1)S(1)}, bf16[96,1024]{1,0:T(8,128)(2,1)S(1)}, u32[]{:S(2)}, u32[]{:S(2)}) collective-permute-start(bf16[96,1024]{1,0:T(8,128)(2,1)S(1)} %get-tuple-element.135), channel_id=1, source_target_pairs={{0,8},{4,12},{8,0},{12,4},{16,24},{20,28},{24,16},{28,20},{1,9},{5... | collective-permute-start | bytes 589832 | tf_op jit(solution)/shard_map/ppermute | solution.py:349
  28.6 0.1 shard_map.89
  28.7 0.0 copy-start.1
  28.7 2.0 %collective-permute-done.20.refs_1_ = bf16[96,1024]{1,0:T(8,128)(2,1)S(1)} collective-permute-done((bf16[96,1024]{1,0:T(8,128)(2,1)S(1)}, bf16[96,1024]{1,0:T(8,128)(2,1)S(1)}, u32[]{:S(2)}, u32[]{:S(2)}) %collective-permute-start.20) | collective-permute-done | bytes 196640 | tf_op jit(solution)/shard_map/ppermute | solution.py:349
  30.7 2.1 %collective-permute-start.12 = (bf16[96,1024]{1,0:T(8,128)(2,1)S(1)}, bf16[96,1024]{1,0:T(8,128)(2,1)S(1)}, u32[]{:S(2)}, u32[]{:S(2)}) collective-permute-start(bf16[96,1024]{1,0:T(8,128)(2,1)S(1)} %get-tuple-element.115), channel_id=1, source_target_pairs={{0,8},{4,12},{8,0},{12,4},{16,24},{20,28},{24,16},{28,20},{1,9},{5... | collective-permute-start | bytes 589832 | tf_op jit(solution)/shard_map/ppermute | solution.py:349
  32.8 0.0 collective-permute-done.16.refs_1_
  32.8 1.5 %collective-permute-start.19 = (bf16[96,1024]{1,0:T(8,128)(2,1)S(1)}, bf16[96,1024]{1,0:T(8,128)(2,1)S(1)}, u32[]{:S(2)}, u32[]{:S(2)}) collective-permute-start(bf16[96,1024]{1,0:T(8,128)(2,1)S(1)} %get-tuple-element.127), channel_id=1, source_target_pairs={{0,4},{4,0},{8,12},{12,8},{16,20},{20,16},{24,28},{28,24},{1,5},{5... | collective-permute-start | bytes 589832 | tf_op jit(solution)/shard_map/ppermute | solution.py:349
  34.3 1.2 %shard_map.85 = (bf16[64,1024]{1,0:T(8,128)(2,1)S(1)}, bf16[96,1024]{1,0:T(8,128)(2,1)S(1)}, bf16[64,1024]{1,0:T(8,128)(2,1)S(1)}, bf16[96,1024]{1,0:T(8,128)(2,...) custom-call(s32[1,128]{1,0:T(1,128)S(1)} %copy-done.5, ...), custom_call_target="tpu_custom_call" | custom-call | flops 176160768 | bytes 2752512 | tf_op jit(solution)/shard_map/pallas_call | solution.py:170
  35.5 0.1 shard_map.94
  35.7 0.5 collective-permute-start.21
  36.2 0.1 shard_map.92
  36.3 0.1 shard_map.91
  36.3 0.6 collective-permute-start.17
  37.0 1.5 %collective-permute-start.15 = (bf16[64,1024]{1,0:T(8,128)(2,1)S(1)}, bf16[64,1024]{1,0:T(8,128)(2,1)S(1)}, u32[]{:S(2)}, u32[]{:S(2)}) collective-permute-start(bf16[64,1024]{1,0:T(8,128)(2,1)S(1)} %get-tuple-element.120), channel_id=1, source_target_pairs={{0,4},{4,0},{8,12},{12,8},{16,20},{20,16},{24,28},{28,24},{1,5},{5... | collective-permute-start | bytes 393224 | tf_op jit(solution)/shard_map/ppermute | solution.py:349
  38.4 0.1 shard_map.96
  38.6 2.7 %collective-permute-start.25 = (bf16[96,1024]{1,0:T(8,128)(2,1)S(1)}, bf16[96,1024]{1,0:T(8,128)(2,1)S(1)}, u32[]{:S(2)}, u32[]{:S(2)}) collective-permute-start(bf16[96,1024]{1,0:T(8,128)(2,1)S(1)} %get-tuple-element.136), channel_id=1, source_target_pairs={{0,16},{4,20},{8,24},{12,28},{16,0},{20,4},{24,8},{28,12},{1,17},{... | collective-permute-start | bytes 589832 | tf_op jit(solution)/shard_map/ppermute | solution.py:349
  41.2 0.1 shard_map.87
  41.3 0.1 shard_map.90
  41.5 2.0 %collective-permute-start.7 = (bf16[96,1024]{1,0:T(8,128)(2,1)S(1)}, bf16[96,1024]{1,0:T(8,128)(2,1)S(1)}, u32[]{:S(2)}, u32[]{:S(2)}) collective-permute-start(bf16[96,1024]{1,0:T(8,128)(2,1)S(1)} %get-tuple-element.107), channel_id=1, source_target_pairs={{0,4},{4,0},{8,12},{12,8},{16,20},{20,16},{24,28},{28,24},{1,5},{5... | collective-permute-start | bytes 589832 | tf_op jit(solution)/shard_map/ppermute | solution.py:349
  43.5 2.4 %collective-permute-start.9 = (bf16[96,1024]{1,0:T(8,128)(2,1)S(1)}, bf16[96,1024]{1,0:T(8,128)(2,1)S(1)}, u32[]{:S(2)}, u32[]{:S(2)}) collective-permute-start(bf16[96,1024]{1,0:T(8,128)(2,1)S(1)} %get-tuple-element.110), channel_id=1, source_target_pairs={{0,8},{4,12},{8,0},{12,4},{16,24},{20,28},{24,16},{28,20},{1,9},{5... | collective-permute-start | bytes 589832 | tf_op jit(solution)/shard_map/ppermute | solution.py:349
  45.9 0.2 collective-permute-done.15.refs_2_
  46.0 2.8 %collective-permute-start.13 = (bf16[96,1024]{1,0:T(8,128)(2,1)S(1)}, bf16[96,1024]{1,0:T(8,128)(2,1)S(1)}, u32[]{:S(2)}, u32[]{:S(2)}) collective-permute-start(bf16[96,1024]{1,0:T(8,128)(2,1)S(1)} %get-tuple-element.116), channel_id=1, source_target_pairs={{0,16},{4,20},{8,24},{12,28},{16,0},{20,4},{24,8},{28,12},{1,17},{... | collective-permute-start | bytes 589832 | tf_op jit(solution)/shard_map/ppermute | solution.py:349
  48.8 0.1 shard_map.93
  48.9 0.2 collective-permute-start.18
  49.1 13.2 %collective-permute-done.18.refs_3_ = bf16[64,1024]{1,0:T(8,128)(2,1)S(1)} collective-permute-done((bf16[64,1024]{1,0:T(8,128)(2,1)S(1)}, bf16[64,1024]{1,0:T(8,128)(2,1)S(1)}, u32[]{:S(2)}, u32[]{:S(2)}) %collective-permute-start.18) | collective-permute-done | bytes 131104 | tf_op jit(solution)/shard_map/ppermute | solution.py:349
  62.3 0.3 shard_map.97
  62.6 0.8 %shard_map.98 = (f32[1,96,1024]{2,1,0:T(8,128)S(1)}, f32[32,1,128]{2,1,0:T(1,128)}) custom-call(s32[1,128]{1,0:T(1,128)S(1)} %copy-done.5, f32[1,256,1024]{2,1,0:T(8,128)S(1)} %copy-done.1, bf16[96,1024]{1,0:T(8,128)(2,1)S(1)} %get-tuple-element.106.refs_0_, bf16[96,1024]{1,0:T(8,128)(2,1)S(1)} %collective-permute-done.7.refs_1_, ...), custom_call_target="tpu_custom_call" | custom-call | tf_op jit(solution)/shard_map/pallas_call | solution.py:247
  63.4 5.6 %all-to-all-start.1 = ((f32[32,1,128]{2,1,0:T(1,128)}), f32[32,1,128]{2,1,0:T(1,128)S(1)}, u32[]{:S(2)}, u32[]{:S(2)}) async-start(f32[32,1,128]{2,1,0:T(1,128)} %get-tuple-element.149), calls=%async_computation.1 | async-start | bytes 32768 | tf_op jit(solution)/shard_map/all_to_all | solution.py:374
  69.1 1.0 %store.1 = f32[1,256,1024]{2,1,0:T(8,128)} custom-call(f32[1,96,1024]{2,1,0:T(8,128)S(1)} %get-tuple-element.147.refs_0_, f32[1,160,1024]{2,1,0:T(8,128)S(1)} %get-tuple-element.148.refs_1_), custom_call_target="tpu_custom_call" | custom-call | bytes 16777216 | tf_op jit(solution)/shard_map/store/pallas_call | solution.py:272
  70.1 6.1 %all-to-all-done.1.refs_2_ = f32[32,1,128]{2,1,0:T(1,128)S(1)} async-done(((f32[32,1,128]{2,1,0:T(1,128)}), f32[32,1,128]{2,1,0:T(1,128)S(1)}, u32[]{:S(2)}, u32[]{:S(2)}) %all-to-all-start.1) | async-done | bytes 16416 | tf_op jit(solution)/shard_map/all_to_all | solution.py:374
  76.2 1.2 %scale.3 = (f32[1,256,1024]{2,1,0:T(8,128)}, f32[1,1]{1,0:T(1,128)}, s32[1,1]{1,0:T(1,128)}) custom-call(f32[1,96,1024]{2,1,0:T(8,128)S(1)} %get-tuple-element.147.refs_0_, f32[1,160,1024]{2,1,0:T(8,128)S(1)} %get-tuple-element.148.refs_1_, f32[32,1,128]{2,1,0:T(1,128)S(1)} %all-to-all-done.1.refs_2_), custom_call_target="tpu_custom_call" | custom-call | tf_op jit(solution)/shard_map/scale/pallas_call | solution.py:322
  77.4 0.6 while.11
  (21 shorter events, 0.1 us)
Async XLA Ops:
  0.6 7.6 %copy-start.6 = (s32[1,128]{1,0:T(1,128)S(1)}, s32[1,128]{1,0:T(1,128)}, u32[]{:S(2)}) copy-start(s32[1,128]{1,0:T(1,128)} %tok_hbm.1) | copy-start | bytes 1540
  0.6 7.6 %copy-start.5 = (s32[1,128]{1,0:T(1,128)S(1)}, s32[1,128]{1,0:T(1,128)}, u32[]{:S(2)}) copy-start(s32[1,128]{1,0:T(1,128)} %trig_ref.3) | copy-start | bytes 1540
  0.7 7.6 %copy-start = (bf16[1,2048,1024]{2,1,0:T(8,128)(2,1)S(1)}, bf16[1,2048,1024]{2,1,0:T(8,128)(2,1)}, u32[]{:S(2)}) copy-start(bf16[1,2048,1024]{2,1,0:T(8,128)(2,1)} %stale_hbm.1) | copy-start | bytes 12582916
  0.7 7.6 %copy-start.3 = (bf16[1,128,2048]{2,1,0:T(8,128)(2,1)S(1)}, bf16[1,128,2048]{2,1,0:T(8,128)(2,1)}, u32[]{:S(2)}) copy-start(bf16[1,128,2048]{2,1,0:T(8,128)(2,1)} %acts_hbm.1) | copy-start | bytes 1572868
  0.7 7.6 %copy-start.4 = (bf16[1,128,1024]{2,1,0:T(8,128)(2,1)S(1)}, bf16[1,128,1024]{2,1,0:T(8,128)(2,1)}, u32[]{:S(2)}) copy-start(bf16[1,128,1024]{2,1,0:T(8,128)(2,1)} %og_hbm.1) | copy-start | bytes 786436
  5.1 8.9 %collective-permute-start.23 = (bf16[96,1024]{1,0:T(8,128)(2,1)S(1)}, bf16[96,1024]{1,0:T(8,128)(2,1)S(1)}, u32[]{:S(2)}, u32[]{:S(2)}) collective-permute-start(bf16[96,1024]{1,0:T(8,128)(2,1)S(1)} %get-tuple-element.134), channel_id=1, source_target_pairs={{0,4},{4,0},{8,12},{12,8},{16,20},{20,16},{24,28},{28,24},{1,5},{5... | collective-permute-start | bytes 589832 | tf_op jit(solution)/shard_map/ppermute | solution.py:349
  8.1 10.0 %collective-permute-start.22 = (bf16[96,1024]{1,0:T(8,128)(2,1)S(1)}, bf16[96,1024]{1,0:T(8,128)(2,1)S(1)}, u32[]{:S(2)}, u32[]{:S(2)}) collective-permute-start(bf16[96,1024]{1,0:T(8,128)(2,1)S(1)} %get-tuple-element.132), channel_id=1, source_target_pairs={{0,4},{4,0},{8,12},{12,8},{16,20},{20,16},{24,28},{28,24},{1,5},{5... | collective-permute-start | bytes 589832 | tf_op jit(solution)/shard_map/ppermute | solution.py:349
  9.9 12.4 %collective-permute-start.11 = (bf16[96,1024]{1,0:T(8,128)(2,1)S(1)}, bf16[96,1024]{1,0:T(8,128)(2,1)S(1)}, u32[]{:S(2)}, u32[]{:S(2)}) collective-permute-start(bf16[96,1024]{1,0:T(8,128)(2,1)S(1)} %get-tuple-element.114), channel_id=1, source_target_pairs={{0,4},{4,0},{8,12},{12,8},{16,20},{20,16},{24,28},{28,24},{1,5},{5... | collective-permute-start | bytes 589832 | tf_op jit(solution)/shard_map/ppermute | solution.py:349
  11.9 14.7 %collective-permute-start.10 = (bf16[96,1024]{1,0:T(8,128)(2,1)S(1)}, bf16[96,1024]{1,0:T(8,128)(2,1)S(1)}, u32[]{:S(2)}, u32[]{:S(2)}) collective-permute-start(bf16[96,1024]{1,0:T(8,128)(2,1)S(1)} %get-tuple-element.112), channel_id=1, source_target_pairs={{0,4},{4,0},{8,12},{12,8},{16,20},{20,16},{24,28},{28,24},{1,5},{5... | collective-permute-start | bytes 589832 | tf_op jit(solution)/shard_map/ppermute | solution.py:349
  12.0 20.9 %collective-permute-start.16 = (bf16[128,1024]{1,0:T(8,128)(2,1)S(1)}, bf16[128,1024]{1,0:T(8,128)(2,1)S(1)}, u32[]{:S(2)}, u32[]{:S(2)}) collective-permute-start(bf16[128,1024]{1,0:T(8,128)(2,1)S(1)} %get-tuple-element.122), channel_id=1, source_target_pairs={{0,8},{4,12},{8,0},{12,4},{16,24},{20,28},{24,16},{28,20},{1,9},{5... | collective-permute-start | bytes 786440 | tf_op jit(solution)/shard_map/ppermute | solution.py:349
  14.0 21.7 %collective-permute-start.14 = (bf16[128,1024]{1,0:T(8,128)(2,1)S(1)}, bf16[128,1024]{1,0:T(8,128)(2,1)S(1)}, u32[]{:S(2)}, u32[]{:S(2)}) collective-permute-start(bf16[128,1024]{1,0:T(8,128)(2,1)S(1)} %get-tuple-element.118), channel_id=1, source_target_pairs={{0,8},{4,12},{8,0},{12,4},{16,24},{20,28},{24,16},{28,20},{1,9},{5... | collective-permute-start | bytes 786440 | tf_op jit(solution)/shard_map/ppermute | solution.py:349
  18.1 12.6 %collective-permute-start.20 = (bf16[96,1024]{1,0:T(8,128)(2,1)S(1)}, bf16[96,1024]{1,0:T(8,128)(2,1)S(1)}, u32[]{:S(2)}, u32[]{:S(2)}) collective-permute-start(bf16[96,1024]{1,0:T(8,128)(2,1)S(1)} %get-tuple-element.129), channel_id=1, source_target_pairs={{0,4},{4,0},{8,12},{12,8},{16,20},{20,16},{24,28},{28,24},{1,5},{5... | collective-permute-start | bytes 589832 | tf_op jit(solution)/shard_map/ppermute | solution.py:349
  22.3 14.0 %collective-permute-start.8 = (bf16[96,1024]{1,0:T(8,128)(2,1)S(1)}, bf16[96,1024]{1,0:T(8,128)(2,1)S(1)}, u32[]{:S(2)}, u32[]{:S(2)}) collective-permute-start(bf16[96,1024]{1,0:T(8,128)(2,1)S(1)} %get-tuple-element.109), channel_id=1, source_target_pairs={{0,4},{4,0},{8,12},{12,8},{16,20},{20,16},{24,28},{28,24},{1,5},{5... | collective-permute-start | bytes 589832 | tf_op jit(solution)/shard_map/ppermute | solution.py:349
  26.5 10.4 %collective-permute-start.24 = (bf16[96,1024]{1,0:T(8,128)(2,1)S(1)}, bf16[96,1024]{1,0:T(8,128)(2,1)S(1)}, u32[]{:S(2)}, u32[]{:S(2)}) collective-permute-start(bf16[96,1024]{1,0:T(8,128)(2,1)S(1)} %get-tuple-element.135), channel_id=1, source_target_pairs={{0,8},{4,12},{8,0},{12,4},{16,24},{20,28},{24,16},{28,20},{1,9},{5... | collective-permute-start | bytes 589832 | tf_op jit(solution)/shard_map/ppermute | solution.py:349
  28.7 33.6 %copy-start.1 = (f32[1,256,1024]{2,1,0:T(8,128)S(1)}, f32[1,256,1024]{2,1,0:T(8,128)}, u32[]{:S(2)}) copy-start(f32[1,256,1024]{2,1,0:T(8,128)} %prev_ref.3) | copy-start | bytes 3145732
  30.7 7.8 %collective-permute-start.12 = (bf16[96,1024]{1,0:T(8,128)(2,1)S(1)}, bf16[96,1024]{1,0:T(8,128)(2,1)S(1)}, u32[]{:S(2)}, u32[]{:S(2)}) collective-permute-start(bf16[96,1024]{1,0:T(8,128)(2,1)S(1)} %get-tuple-element.115), channel_id=1, source_target_pairs={{0,8},{4,12},{8,0},{12,4},{16,24},{20,28},{24,16},{28,20},{1,9},{5... | collective-permute-start | bytes 589832 | tf_op jit(solution)/shard_map/ppermute | solution.py:349
  32.8 8.7 %collective-permute-start.19 = (bf16[96,1024]{1,0:T(8,128)(2,1)S(1)}, bf16[96,1024]{1,0:T(8,128)(2,1)S(1)}, u32[]{:S(2)}, u32[]{:S(2)}) collective-permute-start(bf16[96,1024]{1,0:T(8,128)(2,1)S(1)} %get-tuple-element.127), channel_id=1, source_target_pairs={{0,4},{4,0},{8,12},{12,8},{16,20},{20,16},{24,28},{28,24},{1,5},{5... | collective-permute-start | bytes 589832 | tf_op jit(solution)/shard_map/ppermute | solution.py:349
  35.7 13.3 %collective-permute-start.21 = (bf16[96,1024]{1,0:T(8,128)(2,1)S(1)}, bf16[96,1024]{1,0:T(8,128)(2,1)S(1)}, u32[]{:S(2)}, u32[]{:S(2)}) collective-permute-start(bf16[96,1024]{1,0:T(8,128)(2,1)S(1)} %get-tuple-element.130), channel_id=1, source_target_pairs={{0,8},{4,12},{8,0},{12,4},{16,24},{20,28},{24,16},{28,20},{1,9},{5... | collective-permute-start | bytes 589832 | tf_op jit(solution)/shard_map/ppermute | solution.py:349
  36.3 7.1 %collective-permute-start.17 = (bf16[64,1024]{1,0:T(8,128)(2,1)S(1)}, bf16[64,1024]{1,0:T(8,128)(2,1)S(1)}, u32[]{:S(2)}, u32[]{:S(2)}) collective-permute-start(bf16[64,1024]{1,0:T(8,128)(2,1)S(1)} %get-tuple-element.124), channel_id=1, source_target_pairs={{0,4},{4,0},{8,12},{12,8},{16,20},{20,16},{24,28},{28,24},{1,5},{5... | collective-permute-start | bytes 393224 | tf_op jit(solution)/shard_map/ppermute | solution.py:349
  37.0 9.1 %collective-permute-start.15 = (bf16[64,1024]{1,0:T(8,128)(2,1)S(1)}, bf16[64,1024]{1,0:T(8,128)(2,1)S(1)}, u32[]{:S(2)}, u32[]{:S(2)}) collective-permute-start(bf16[64,1024]{1,0:T(8,128)(2,1)S(1)} %get-tuple-element.120), channel_id=1, source_target_pairs={{0,4},{4,0},{8,12},{12,8},{16,20},{20,16},{24,28},{28,24},{1,5},{5... | collective-permute-start | bytes 393224 | tf_op jit(solution)/shard_map/ppermute | solution.py:349
  38.6 23.7 %collective-permute-start.25 = (bf16[96,1024]{1,0:T(8,128)(2,1)S(1)}, bf16[96,1024]{1,0:T(8,128)(2,1)S(1)}, u32[]{:S(2)}, u32[]{:S(2)}) collective-permute-start(bf16[96,1024]{1,0:T(8,128)(2,1)S(1)} %get-tuple-element.136), channel_id=1, source_target_pairs={{0,16},{4,20},{8,24},{12,28},{16,0},{20,4},{24,8},{28,12},{1,17},{... | collective-permute-start | bytes 589832 | tf_op jit(solution)/shard_map/ppermute | solution.py:349
  41.5 21.1 %collective-permute-start.7 = (bf16[96,1024]{1,0:T(8,128)(2,1)S(1)}, bf16[96,1024]{1,0:T(8,128)(2,1)S(1)}, u32[]{:S(2)}, u32[]{:S(2)}) collective-permute-start(bf16[96,1024]{1,0:T(8,128)(2,1)S(1)} %get-tuple-element.107), channel_id=1, source_target_pairs={{0,4},{4,0},{8,12},{12,8},{16,20},{20,16},{24,28},{28,24},{1,5},{5... | collective-permute-start | bytes 589832 | tf_op jit(solution)/shard_map/ppermute | solution.py:349
  43.5 19.1 %collective-permute-start.9 = (bf16[96,1024]{1,0:T(8,128)(2,1)S(1)}, bf16[96,1024]{1,0:T(8,128)(2,1)S(1)}, u32[]{:S(2)}, u32[]{:S(2)}) collective-permute-start(bf16[96,1024]{1,0:T(8,128)(2,1)S(1)} %get-tuple-element.110), channel_id=1, source_target_pairs={{0,8},{4,12},{8,0},{12,4},{16,24},{20,28},{24,16},{28,20},{1,9},{5... | collective-permute-start | bytes 589832 | tf_op jit(solution)/shard_map/ppermute | solution.py:349
  46.0 16.5 %collective-permute-start.13 = (bf16[96,1024]{1,0:T(8,128)(2,1)S(1)}, bf16[96,1024]{1,0:T(8,128)(2,1)S(1)}, u32[]{:S(2)}, u32[]{:S(2)}) collective-permute-start(bf16[96,1024]{1,0:T(8,128)(2,1)S(1)} %get-tuple-element.116), channel_id=1, source_target_pairs={{0,16},{4,20},{8,24},{12,28},{16,0},{20,4},{24,8},{28,12},{1,17},{... | collective-permute-start | bytes 589832 | tf_op jit(solution)/shard_map/ppermute | solution.py:349
  48.9 13.4 %collective-permute-start.18 = (bf16[64,1024]{1,0:T(8,128)(2,1)S(1)}, bf16[64,1024]{1,0:T(8,128)(2,1)S(1)}, u32[]{:S(2)}, u32[]{:S(2)}) collective-permute-start(bf16[64,1024]{1,0:T(8,128)(2,1)S(1)} %get-tuple-element.125), channel_id=1, source_target_pairs={{0,16},{4,20},{8,24},{12,28},{16,0},{20,4},{24,8},{28,12},{1,17},{... | collective-permute-start | bytes 393224 | tf_op jit(solution)/shard_map/ppermute | solution.py:349
  63.4 12.8 %all-to-all-start.1 = ((f32[32,1,128]{2,1,0:T(1,128)}), f32[32,1,128]{2,1,0:T(1,128)S(1)}, u32[]{:S(2)}, u32[]{:S(2)}) async-start(f32[32,1,128]{2,1,0:T(1,128)} %get-tuple-element.149), calls=%async_computation.1 | async-start | bytes 32768 | tf_op jit(solution)/shard_map/all_to_all | solution.py:374

commit v5 on v4

--- a/solution.py
+++ b/solution.py
@@ -11,7 +11,7 @@
 clip_ratio = 0.25
 epsilon = 1e-06
 MIB = 1 << 20
-PIECE = 64
+PIECE = 32
 STAGES = 3
 KINDS = 6
 ROUNDING = 4.8e-4
@@ -20,7 +20,7 @@
 SMEM = pl.BlockSpec(memory_space=pltpu.SMEM)
 HBM = pl.BlockSpec(memory_space=pltpu.HBM)
 
-A0, A1, B = (0, 6), (6, 6), (12, 4)
+A0, A1, B = (6, 6), (0, 6), (12, 4)
 RAW = (
     ("y6a", 1, ((6, A0),)),
     ("zb0", 2, ((5, B), (4, B))),
@@ -49,9 +49,9 @@
 )
 FINAL = (
     (B, (0, B), (("zb1", 1), ("pairb1", 0), ("quadb", 0))),
-    (A1, (0, A1), (("y0b", 0), ("last1", 0), ("quad1", 0))),
+    (A0, (0, A0), (("y0a", 0), ("last0", 0), ("quad0", 0))),
 )
-LAST = ((A0, (0, A0), (("y0a", 0), ("last0", 0), ("quad0", 0))),)
+LAST = ((A1, (0, A1), (("y0b", 0), ("last1", 0), ("quad1", 0))),)
 
 
 def fold(x):
@@ -372,7 +372,7 @@
     kept, sums = total_up(aggregate_prev, addends(FINAL), lost, trigger, ())
     kept_last, sums = total_up(aggregate_prev, addends(LAST), [], trigger, (sums,))
     everyone = lax.all_to_all(sums, ("dp", "shard"), 0, 0, tiled=True)
-    kept = [(0, kept_last), (A0[1] * unit, kept)]
+    kept = [(0, kept_last), (A1[1] * unit, kept)]
     agg = store(kept)
     update, hits, bad = scale(kept, everyone)
 

time: 78.3 us -> 78.2 us (level)
  no operation moved by 1% of the time
where the time goes in v5:
time: 78.2 us; the launch traced here: 78 us
  starting transfers between devices  37.2 us (48%)
  waiting for transfers between devices  27.9 us (36%)
  Pallas kernels  11.4 us (15%)
  between operations  0.84 us (1%)
    ppermute x19, starting transfers between devices, swap(): return lax.ppermute(x, 'dp', [(i, i ^ mask) for i in range(n)])  31.6 us
    ppermute x19, waiting for transfers between devices, swap(): return lax.ppermute(x, 'dp', [(i, i ^ mask) for i in range(n)])  21.8 us
    all_to_all x1, waiting for transfers between devices, step(): everyone = lax.all_to_all(sums, ('dp', 'shard'), 0, 0, tiled=True)  6.11 us
    all_to_all x1, starting transfers between devices, step(): everyone = lax.all_to_all(sums, ('dp', 'shard'), 0, 0, tiled=True)  5.67 us
    pallas_call x2, Pallas kernels, deltas(): pl.pallas_call(kernel, out_shape=tuple((jax.ShapeDtypeStruct((h, width),...  5.58 us
    pallas_call x1, Pallas kernels, deltas_first(): pl.pallas_call(kernel, out_shape=tuple((jax.ShapeDtypeStruct((h, width),...  1.62 us
  transfers between devices with their start and end apart: 20, of which 7 were waited for; matrix products, arithmetic and copies ran while one was open for 0% of the time, Pallas kernels for 6%

profile of v5, /device:TPU:0, one launch (start us, length us, event | category | flops | bytes accessed | tf_op | source)
XLA Modules:
  0.0 78.0 jit_solution(9843283405755820681)
XLA Ops:
  0.7 0.0 copy-start
  0.7 4.4 %shard_map.86 = (bf16[96,1024]{1,0:T(8,128)(2,1)S(1)}, bf16[96,1024]{1,0:T(8,128)(2,1)S(1)}, bf16[128,1024]{1,0:T(8,128)(2,1)S(1)}, bf16[96,1024]{1,0:T(8,128)(2...) custom-call(s32[1,128]{1,0:T(1,128)} %trig_ref.3, ...), custom_call_target="tpu_custom_call" | custom-call | flops 301989888 | bytes 4718592 | tf_op jit(solution)/shard_map/pallas_call | solution.py:170
  5.1 3.1 %collective-permute-start.11 = (bf16[96,1024]{1,0:T(8,128)(2,1)S(1)}, bf16[96,1024]{1,0:T(8,128)(2,1)S(1)}, u32[]{:S(2)}, u32[]{:S(2)}) collective-permute-start(bf16[96,1024]{1,0:T(8,128)(2,1)S(1)} %get-tuple-element.114), channel_id=1, source_target_pairs={{0,4},{4,0},{8,12},{12,8},{16,20},{20,16},{24,28},{28,24},{1,5},{5... | collective-permute-start | bytes 589832 | tf_op jit(solution)/shard_map/ppermute | solution.py:349
  8.2 1.6 %shard_map.91 = (bf16[96,1024]{1,0:T(8,128)(2,1)S(1)}, bf16[128,1024]{1,0:T(8,128)(2,1)S(1)}) custom-call(s32[1,128]{1,0:T(1,128)S(1)} %copy-done.5, s32[1,128]{1,0:T(1,128)S(1)} %copy-done.6, bf16[1,128,2048]{2,1,0:T(8,128)(2,1)S(1)} %copy-done.3, bf16[1,128,1024]{2,1,0:T(8,128)(2,1)S(1)} %copy-done.4, bf16[1,2048,1024]{2,1,0:T(8,128)(2,1)S(1)} %copy-done), custom_call_target="tpu_custom_call" | custom-call | flops 58720256 | bytes 917504 | tf_op jit(solution)/shard_map/pallas_call | solution.py:126
  9.8 0.1 collective-permute-start.23
  9.9 2.0 %collective-permute-start.10 = (bf16[96,1024]{1,0:T(8,128)(2,1)S(1)}, bf16[96,1024]{1,0:T(8,128)(2,1)S(1)}, u32[]{:S(2)}, u32[]{:S(2)}) collective-permute-start(bf16[96,1024]{1,0:T(8,128)(2,1)S(1)} %get-tuple-element.112), channel_id=1, source_target_pairs={{0,4},{4,0},{8,12},{12,8},{16,20},{20,16},{24,28},{28,24},{1,5},{5... | collective-permute-start | bytes 589832 | tf_op jit(solution)/shard_map/ppermute | solution.py:349
  11.9 0.1 collective-permute-start.22
  12.0 2.0 %collective-permute-start.16 = (bf16[128,1024]{1,0:T(8,128)(2,1)S(1)}, bf16[128,1024]{1,0:T(8,128)(2,1)S(1)}, u32[]{:S(2)}, u32[]{:S(2)}) collective-permute-start(bf16[128,1024]{1,0:T(8,128)(2,1)S(1)} %get-tuple-element.122), channel_id=1, source_target_pairs={{0,8},{4,12},{8,0},{12,4},{16,24},{20,28},{24,16},{28,20},{1,9},{5... | collective-permute-start | bytes 786440 | tf_op jit(solution)/shard_map/ppermute | solution.py:349
  14.0 2.0 %collective-permute-start.14 = (bf16[128,1024]{1,0:T(8,128)(2,1)S(1)}, bf16[128,1024]{1,0:T(8,128)(2,1)S(1)}, u32[]{:S(2)}, u32[]{:S(2)}) collective-permute-start(bf16[128,1024]{1,0:T(8,128)(2,1)S(1)} %get-tuple-element.118), channel_id=1, source_target_pairs={{0,8},{4,12},{8,0},{12,4},{16,24},{20,28},{24,16},{28,20},{1,9},{5... | collective-permute-start | bytes 786440 | tf_op jit(solution)/shard_map/ppermute | solution.py:349
  16.0 2.1 %collective-permute-done.23.refs_1_ = bf16[96,1024]{1,0:T(8,128)(2,1)S(1)} collective-permute-done((bf16[96,1024]{1,0:T(8,128)(2,1)S(1)}, bf16[96,1024]{1,0:T(8,128)(2,1)S(1)}, u32[]{:S(2)}, u32[]{:S(2)}) %collective-permute-start.23) | collective-permute-done | bytes 196640 | tf_op jit(solution)/shard_map/ppermute | solution.py:349
  18.1 2.0 %collective-permute-start.20 = (bf16[96,1024]{1,0:T(8,128)(2,1)S(1)}, bf16[96,1024]{1,0:T(8,128)(2,1)S(1)}, u32[]{:S(2)}, u32[]{:S(2)}) collective-permute-start(bf16[96,1024]{1,0:T(8,128)(2,1)S(1)} %get-tuple-element.129), channel_id=1, source_target_pairs={{0,4},{4,0},{8,12},{12,8},{16,20},{20,16},{24,28},{28,24},{1,5},{5... | collective-permute-start | bytes 589832 | tf_op jit(solution)/shard_map/ppermute | solution.py:349
  20.1 0.1 shard_map.95
  20.2 2.1 %collective-permute-done.10.refs_1_ = bf16[96,1024]{1,0:T(8,128)(2,1)S(1)} collective-permute-done((bf16[96,1024]{1,0:T(8,128)(2,1)S(1)}, bf16[96,1024]{1,0:T(8,128)(2,1)S(1)}, u32[]{:S(2)}, u32[]{:S(2)}) %collective-permute-start.10) | collective-permute-done | bytes 196640 | tf_op jit(solution)/shard_map/ppermute | solution.py:349
  22.3 2.0 %collective-permute-start.8 = (bf16[96,1024]{1,0:T(8,128)(2,1)S(1)}, bf16[96,1024]{1,0:T(8,128)(2,1)S(1)}, u32[]{:S(2)}, u32[]{:S(2)}) collective-permute-start(bf16[96,1024]{1,0:T(8,128)(2,1)S(1)} %get-tuple-element.109), channel_id=1, source_target_pairs={{0,4},{4,0},{8,12},{12,8},{16,20},{20,16},{24,28},{28,24},{1,5},{5... | collective-permute-start | bytes 589832 | tf_op jit(solution)/shard_map/ppermute | solution.py:349
  24.3 2.2 %collective-permute-done.22.refs_1_ = bf16[96,1024]{1,0:T(8,128)(2,1)S(1)} collective-permute-done((bf16[96,1024]{1,0:T(8,128)(2,1)S(1)}, bf16[96,1024]{1,0:T(8,128)(2,1)S(1)}, u32[]{:S(2)}, u32[]{:S(2)}) %collective-permute-start.22) | collective-permute-done | bytes 196640 | tf_op jit(solution)/shard_map/ppermute | solution.py:349
  26.5 2.1 %collective-permute-start.24 = (bf16[96,1024]{1,0:T(8,128)(2,1)S(1)}, bf16[96,1024]{1,0:T(8,128)(2,1)S(1)}, u32[]{:S(2)}, u32[]{:S(2)}) collective-permute-start(bf16[96,1024]{1,0:T(8,128)(2,1)S(1)} %get-tuple-element.135), channel_id=1, source_target_pairs={{0,8},{4,12},{8,0},{12,4},{16,24},{20,28},{24,16},{28,20},{1,9},{5... | collective-permute-start | bytes 589832 | tf_op jit(solution)/shard_map/ppermute | solution.py:349
  28.6 0.1 shard_map.88
  28.7 0.0 copy-start.1
  28.7 2.0 %collective-permute-done.20.refs_1_ = bf16[96,1024]{1,0:T(8,128)(2,1)S(1)} collective-permute-done((bf16[96,1024]{1,0:T(8,128)(2,1)S(1)}, bf16[96,1024]{1,0:T(8,128)(2,1)S(1)}, u32[]{:S(2)}, u32[]{:S(2)}) %collective-permute-start.20) | collective-permute-done | bytes 196640 | tf_op jit(solution)/shard_map/ppermute | solution.py:349
  30.8 2.1 %collective-permute-start.12 = (bf16[96,1024]{1,0:T(8,128)(2,1)S(1)}, bf16[96,1024]{1,0:T(8,128)(2,1)S(1)}, u32[]{:S(2)}, u32[]{:S(2)}) collective-permute-start(bf16[96,1024]{1,0:T(8,128)(2,1)S(1)} %get-tuple-element.115), channel_id=1, source_target_pairs={{0,8},{4,12},{8,0},{12,4},{16,24},{20,28},{24,16},{28,20},{1,9},{5... | collective-permute-start | bytes 589832 | tf_op jit(solution)/shard_map/ppermute | solution.py:349
  32.8 0.0 collective-permute-done.16.refs_1_
  32.8 1.5 %collective-permute-start.19 = (bf16[96,1024]{1,0:T(8,128)(2,1)S(1)}, bf16[96,1024]{1,0:T(8,128)(2,1)S(1)}, u32[]{:S(2)}, u32[]{:S(2)}) collective-permute-start(bf16[96,1024]{1,0:T(8,128)(2,1)S(1)} %get-tuple-element.127), channel_id=1, source_target_pairs={{0,4},{4,0},{8,12},{12,8},{16,20},{20,16},{24,28},{28,24},{1,5},{5... | collective-permute-start | bytes 589832 | tf_op jit(solution)/shard_map/ppermute | solution.py:349
  34.3 1.2 %shard_map.85 = (bf16[64,1024]{1,0:T(8,128)(2,1)S(1)}, bf16[96,1024]{1,0:T(8,128)(2,1)S(1)}, bf16[64,1024]{1,0:T(8,128)(2,1)S(1)}, bf16[96,1024]{1,0:T(8,128)(2,...) custom-call(s32[1,128]{1,0:T(1,128)S(1)} %copy-done.5, ...), custom_call_target="tpu_custom_call" | custom-call | flops 176160768 | bytes 2752512 | tf_op jit(solution)/shard_map/pallas_call | solution.py:170
  35.5 0.1 shard_map.94
  35.7 0.0 collective-permute-done.14.refs_1_
  35.7 0.5 collective-permute-start.21
  36.2 0.1 shard_map.92
  36.3 0.1 shard_map.90
  36.4 0.6 collective-permute-start.17
  37.0 1.5 %collective-permute-start.15 = (bf16[64,1024]{1,0:T(8,128)(2,1)S(1)}, bf16[64,1024]{1,0:T(8,128)(2,1)S(1)}, u32[]{:S(2)}, u32[]{:S(2)}) collective-permute-start(bf16[64,1024]{1,0:T(8,128)(2,1)S(1)} %get-tuple-element.120), channel_id=1, source_target_pairs={{0,4},{4,0},{8,12},{12,8},{16,20},{20,16},{24,28},{28,24},{1,5},{5... | collective-permute-start | bytes 393224 | tf_op jit(solution)/shard_map/ppermute | solution.py:349
  38.5 0.1 shard_map.96
  38.6 2.6 %collective-permute-start.25 = (bf16[96,1024]{1,0:T(8,128)(2,1)S(1)}, bf16[96,1024]{1,0:T(8,128)(2,1)S(1)}, u32[]{:S(2)}, u32[]{:S(2)}) collective-permute-start(bf16[96,1024]{1,0:T(8,128)(2,1)S(1)} %get-tuple-element.136), channel_id=1, source_target_pairs={{0,16},{4,20},{8,24},{12,28},{16,0},{20,4},{24,8},{28,12},{1,17},{... | collective-permute-start | bytes 589832 | tf_op jit(solution)/shard_map/ppermute | solution.py:349
  41.3 0.1 shard_map.87
  41.4 0.1 shard_map.89
  41.5 1.9 %collective-permute-start.7 = (bf16[96,1024]{1,0:T(8,128)(2,1)S(1)}, bf16[96,1024]{1,0:T(8,128)(2,1)S(1)}, u32[]{:S(2)}, u32[]{:S(2)}) collective-permute-start(bf16[96,1024]{1,0:T(8,128)(2,1)S(1)} %get-tuple-element.107), channel_id=1, source_target_pairs={{0,4},{4,0},{8,12},{12,8},{16,20},{20,16},{24,28},{28,24},{1,5},{5... | collective-permute-start | bytes 589832 | tf_op jit(solution)/shard_map/ppermute | solution.py:349
  43.5 2.4 %collective-permute-start.9 = (bf16[96,1024]{1,0:T(8,128)(2,1)S(1)}, bf16[96,1024]{1,0:T(8,128)(2,1)S(1)}, u32[]{:S(2)}, u32[]{:S(2)}) collective-permute-start(bf16[96,1024]{1,0:T(8,128)(2,1)S(1)} %get-tuple-element.110), channel_id=1, source_target_pairs={{0,8},{4,12},{8,0},{12,4},{16,24},{20,28},{24,16},{28,20},{1,9},{5... | collective-permute-start | bytes 589832 | tf_op jit(solution)/shard_map/ppermute | solution.py:349
  45.9 0.2 collective-permute-done.15.refs_2_
  46.0 2.8 %collective-permute-start.13 = (bf16[96,1024]{1,0:T(8,128)(2,1)S(1)}, bf16[96,1024]{1,0:T(8,128)(2,1)S(1)}, u32[]{:S(2)}, u32[]{:S(2)}) collective-permute-start(bf16[96,1024]{1,0:T(8,128)(2,1)S(1)} %get-tuple-element.116), channel_id=1, source_target_pairs={{0,16},{4,20},{8,24},{12,28},{16,0},{20,4},{24,8},{28,12},{1,17},{... | collective-permute-start | bytes 589832 | tf_op jit(solution)/shard_map/ppermute | solution.py:349
  48.8 0.1 shard_map.93
  48.9 0.2 collective-permute-start.18
  49.1 13.2 %collective-permute-done.18.refs_3_ = bf16[64,1024]{1,0:T(8,128)(2,1)S(1)} collective-permute-done((bf16[64,1024]{1,0:T(8,128)(2,1)S(1)}, bf16[64,1024]{1,0:T(8,128)(2,1)S(1)}, u32[]{:S(2)}, u32[]{:S(2)}) %collective-permute-start.18) | collective-permute-done | bytes 131104 | tf_op jit(solution)/shard_map/ppermute | solution.py:349
  62.3 0.2 shard_map.97
  62.6 0.8 %shard_map.98 = (f32[1,96,1024]{2,1,0:T(8,128)S(1)}, f32[32,1,128]{2,1,0:T(1,128)}) custom-call(s32[1,128]{1,0:T(1,128)S(1)} %copy-done.5, f32[1,256,1024]{2,1,0:T(8,128)S(1)} %copy-done.1, bf16[96,1024]{1,0:T(8,128)(2,1)S(1)} %get-tuple-element.106.refs_0_, bf16[96,1024]{1,0:T(8,128)(2,1)S(1)} %collective-permute-done.7.refs_1_, ...), custom_call_target="tpu_custom_call" | custom-call | tf_op jit(solution)/shard_map/pallas_call | solution.py:247
  63.4 5.7 %all-to-all-start.1 = ((f32[32,1,128]{2,1,0:T(1,128)}), f32[32,1,128]{2,1,0:T(1,128)S(1)}, u32[]{:S(2)}, u32[]{:S(2)}) async-start(f32[32,1,128]{2,1,0:T(1,128)} %get-tuple-element.149), calls=%async_computation.1 | async-start | bytes 32768 | tf_op jit(solution)/shard_map/all_to_all | solution.py:374
  69.1 1.0 %store.1 = f32[1,256,1024]{2,1,0:T(8,128)} custom-call(f32[1,96,1024]{2,1,0:T(8,128)S(1)} %get-tuple-element.147.refs_0_, f32[1,160,1024]{2,1,0:T(8,128)S(1)} %get-tuple-element.148.refs_1_), custom_call_target="tpu_custom_call" | custom-call | bytes 16777216 | tf_op jit(solution)/shard_map/store/pallas_call | solution.py:272
  70.1 6.1 %all-to-all-done.1.refs_2_ = f32[32,1,128]{2,1,0:T(1,128)S(1)} async-done(((f32[32,1,128]{2,1,0:T(1,128)}), f32[32,1,128]{2,1,0:T(1,128)S(1)}, u32[]{:S(2)}, u32[]{:S(2)}) %all-to-all-start.1) | async-done | bytes 16416 | tf_op jit(solution)/shard_map/all_to_all | solution.py:374
  76.2 1.2 %scale.3 = (f32[1,256,1024]{2,1,0:T(8,128)}, f32[1,1]{1,0:T(1,128)}, s32[1,1]{1,0:T(1,128)}) custom-call(f32[1,96,1024]{2,1,0:T(8,128)S(1)} %get-tuple-element.147.refs_0_, f32[1,160,1024]{2,1,0:T(8,128)S(1)} %get-tuple-element.148.refs_1_, f32[32,1,128]{2,1,0:T(1,128)S(1)} %all-to-all-done.1.refs_2_), custom_call_target="tpu_custom_call" | custom-call | tf_op jit(solution)/shard_map/scale/pallas_call | solution.py:322
  77.4 0.6 while.11
  (21 shorter events, 0.0 us)
Async XLA Ops:
  0.6 7.5 %copy-start.6 = (s32[1,128]{1,0:T(1,128)S(1)}, s32[1,128]{1,0:T(1,128)}, u32[]{:S(2)}) copy-start(s32[1,128]{1,0:T(1,128)} %tok_hbm.1) | copy-start | bytes 1540
  0.6 7.5 %copy-start.5 = (s32[1,128]{1,0:T(1,128)S(1)}, s32[1,128]{1,0:T(1,128)}, u32[]{:S(2)}) copy-start(s32[1,128]{1,0:T(1,128)} %trig_ref.3) | copy-start | bytes 1540
  0.7 7.5 %copy-start = (bf16[1,2048,1024]{2,1,0:T(8,128)(2,1)S(1)}, bf16[1,2048,1024]{2,1,0:T(8,128)(2,1)}, u32[]{:S(2)}) copy-start(bf16[1,2048,1024]{2,1,0:T(8,128)(2,1)} %stale_hbm.1) | copy-start | bytes 12582916
  0.7 7.5 %copy-start.3 = (bf16[1,128,2048]{2,1,0:T(8,128)(2,1)S(1)}, bf16[1,128,2048]{2,1,0:T(8,128)(2,1)}, u32[]{:S(2)}) copy-start(bf16[1,128,2048]{2,1,0:T(8,128)(2,1)} %acts_hbm.1) | copy-start | bytes 1572868
  0.7 7.5 %copy-start.4 = (bf16[1,128,1024]{2,1,0:T(8,128)(2,1)S(1)}, bf16[1,128,1024]{2,1,0:T(8,128)(2,1)}, u32[]{:S(2)}) copy-start(bf16[1,128,1024]{2,1,0:T(8,128)(2,1)} %og_hbm.1) | copy-start | bytes 786436
  5.1 8.9 %collective-permute-start.11 = (bf16[96,1024]{1,0:T(8,128)(2,1)S(1)}, bf16[96,1024]{1,0:T(8,128)(2,1)S(1)}, u32[]{:S(2)}, u32[]{:S(2)}) collective-permute-start(bf16[96,1024]{1,0:T(8,128)(2,1)S(1)} %get-tuple-element.114), channel_id=1, source_target_pairs={{0,4},{4,0},{8,12},{12,8},{16,20},{20,16},{24,28},{28,24},{1,5},{5... | collective-permute-start | bytes 589832 | tf_op jit(solution)/shard_map/ppermute | solution.py:349
  9.8 8.3 %collective-permute-start.23 = (bf16[96,1024]{1,0:T(8,128)(2,1)S(1)}, bf16[96,1024]{1,0:T(8,128)(2,1)S(1)}, u32[]{:S(2)}, u32[]{:S(2)}) collective-permute-start(bf16[96,1024]{1,0:T(8,128)(2,1)S(1)} %get-tuple-element.134), channel_id=1, source_target_pairs={{0,4},{4,0},{8,12},{12,8},{16,20},{20,16},{24,28},{28,24},{1,5},{5... | collective-permute-start | bytes 589832 | tf_op jit(solution)/shard_map/ppermute | solution.py:349
  9.9 12.4 %collective-permute-start.10 = (bf16[96,1024]{1,0:T(8,128)(2,1)S(1)}, bf16[96,1024]{1,0:T(8,128)(2,1)S(1)}, u32[]{:S(2)}, u32[]{:S(2)}) collective-permute-start(bf16[96,1024]{1,0:T(8,128)(2,1)S(1)} %get-tuple-element.112), channel_id=1, source_target_pairs={{0,4},{4,0},{8,12},{12,8},{16,20},{20,16},{24,28},{28,24},{1,5},{5... | collective-permute-start | bytes 589832 | tf_op jit(solution)/shard_map/ppermute | solution.py:349
  11.9 14.7 %collective-permute-start.22 = (bf16[96,1024]{1,0:T(8,128)(2,1)S(1)}, bf16[96,1024]{1,0:T(8,128)(2,1)S(1)}, u32[]{:S(2)}, u32[]{:S(2)}) collective-permute-start(bf16[96,1024]{1,0:T(8,128)(2,1)S(1)} %get-tuple-element.132), channel_id=1, source_target_pairs={{0,4},{4,0},{8,12},{12,8},{16,20},{20,16},{24,28},{28,24},{1,5},{5... | collective-permute-start | bytes 589832 | tf_op jit(solution)/shard_map/ppermute | solution.py:349
  12.0 20.9 %collective-permute-start.16 = (bf16[128,1024]{1,0:T(8,128)(2,1)S(1)}, bf16[128,1024]{1,0:T(8,128)(2,1)S(1)}, u32[]{:S(2)}, u32[]{:S(2)}) collective-permute-start(bf16[128,1024]{1,0:T(8,128)(2,1)S(1)} %get-tuple-element.122), channel_id=1, source_target_pairs={{0,8},{4,12},{8,0},{12,4},{16,24},{20,28},{24,16},{28,20},{1,9},{5... | collective-permute-start | bytes 786440 | tf_op jit(solution)/shard_map/ppermute | solution.py:349
  14.0 21.7 %collective-permute-start.14 = (bf16[128,1024]{1,0:T(8,128)(2,1)S(1)}, bf16[128,1024]{1,0:T(8,128)(2,1)S(1)}, u32[]{:S(2)}, u32[]{:S(2)}) collective-permute-start(bf16[128,1024]{1,0:T(8,128)(2,1)S(1)} %get-tuple-element.118), channel_id=1, source_target_pairs={{0,8},{4,12},{8,0},{12,4},{16,24},{20,28},{24,16},{28,20},{1,9},{5... | collective-permute-start | bytes 786440 | tf_op jit(solution)/shard_map/ppermute | solution.py:349
  18.1 12.6 %collective-permute-start.20 = (bf16[96,1024]{1,0:T(8,128)(2,1)S(1)}, bf16[96,1024]{1,0:T(8,128)(2,1)S(1)}, u32[]{:S(2)}, u32[]{:S(2)}) collective-permute-start(bf16[96,1024]{1,0:T(8,128)(2,1)S(1)} %get-tuple-element.129), channel_id=1, source_target_pairs={{0,4},{4,0},{8,12},{12,8},{16,20},{20,16},{24,28},{28,24},{1,5},{5... | collective-permute-start | bytes 589832 | tf_op jit(solution)/shard_map/ppermute | solution.py:349
  22.3 14.0 %collective-permute-start.8 = (bf16[96,1024]{1,0:T(8,128)(2,1)S(1)}, bf16[96,1024]{1,0:T(8,128)(2,1)S(1)}, u32[]{:S(2)}, u32[]{:S(2)}) collective-permute-start(bf16[96,1024]{1,0:T(8,128)(2,1)S(1)} %get-tuple-element.109), channel_id=1, source_target_pairs={{0,4},{4,0},{8,12},{12,8},{16,20},{20,16},{24,28},{28,24},{1,5},{5... | collective-permute-start | bytes 589832 | tf_op jit(solution)/shard_map/ppermute | solution.py:349
  26.5 10.4 %collective-permute-start.24 = (bf16[96,1024]{1,0:T(8,128)(2,1)S(1)}, bf16[96,1024]{1,0:T(8,128)(2,1)S(1)}, u32[]{:S(2)}, u32[]{:S(2)}) collective-permute-start(bf16[96,1024]{1,0:T(8,128)(2,1)S(1)} %get-tuple-element.135), channel_id=1, source_target_pairs={{0,8},{4,12},{8,0},{12,4},{16,24},{20,28},{24,16},{28,20},{1,9},{5... | collective-permute-start | bytes 589832 | tf_op jit(solution)/shard_map/ppermute | solution.py:349
  28.7 33.6 %copy-start.1 = (f32[1,256,1024]{2,1,0:T(8,128)S(1)}, f32[1,256,1024]{2,1,0:T(8,128)}, u32[]{:S(2)}) copy-start(f32[1,256,1024]{2,1,0:T(8,128)} %prev_ref.3) | copy-start | bytes 3145732
  30.8 7.8 %collective-permute-start.12 = (bf16[96,1024]{1,0:T(8,128)(2,1)S(1)}, bf16[96,1024]{1,0:T(8,128)(2,1)S(1)}, u32[]{:S(2)}, u32[]{:S(2)}) collective-permute-start(bf16[96,1024]{1,0:T(8,128)(2,1)S(1)} %get-tuple-element.115), channel_id=1, source_target_pairs={{0,8},{4,12},{8,0},{12,4},{16,24},{20,28},{24,16},{28,20},{1,9},{5... | collective-permute-start | bytes 589832 | tf_op jit(solution)/shard_map/ppermute | solution.py:349
  32.8 8.7 %collective-permute-start.19 = (bf16[96,1024]{1,0:T(8,128)(2,1)S(1)}, bf16[96,1024]{1,0:T(8,128)(2,1)S(1)}, u32[]{:S(2)}, u32[]{:S(2)}) collective-permute-start(bf16[96,1024]{1,0:T(8,128)(2,1)S(1)} %get-tuple-element.127), channel_id=1, source_target_pairs={{0,4},{4,0},{8,12},{12,8},{16,20},{20,16},{24,28},{28,24},{1,5},{5... | collective-permute-start | bytes 589832 | tf_op jit(solution)/shard_map/ppermute | solution.py:349
  35.7 13.2 %collective-permute-start.21 = (bf16[96,1024]{1,0:T(8,128)(2,1)S(1)}, bf16[96,1024]{1,0:T(8,128)(2,1)S(1)}, u32[]{:S(2)}, u32[]{:S(2)}) collective-permute-start(bf16[96,1024]{1,0:T(8,128)(2,1)S(1)} %get-tuple-element.130), channel_id=1, source_target_pairs={{0,8},{4,12},{8,0},{12,4},{16,24},{20,28},{24,16},{28,20},{1,9},{5... | collective-permute-start | bytes 589832 | tf_op jit(solution)/shard_map/ppermute | solution.py:349
  36.4 7.1 %collective-permute-start.17 = (bf16[64,1024]{1,0:T(8,128)(2,1)S(1)}, bf16[64,1024]{1,0:T(8,128)(2,1)S(1)}, u32[]{:S(2)}, u32[]{:S(2)}) collective-permute-start(bf16[64,1024]{1,0:T(8,128)(2,1)S(1)} %get-tuple-element.124), channel_id=1, source_target_pairs={{0,4},{4,0},{8,12},{12,8},{16,20},{20,16},{24,28},{28,24},{1,5},{5... | collective-permute-start | bytes 393224 | tf_op jit(solution)/shard_map/ppermute | solution.py:349
  37.0 9.1 %collective-permute-start.15 = (bf16[64,1024]{1,0:T(8,128)(2,1)S(1)}, bf16[64,1024]{1,0:T(8,128)(2,1)S(1)}, u32[]{:S(2)}, u32[]{:S(2)}) collective-permute-start(bf16[64,1024]{1,0:T(8,128)(2,1)S(1)} %get-tuple-element.120), channel_id=1, source_target_pairs={{0,4},{4,0},{8,12},{12,8},{16,20},{20,16},{24,28},{28,24},{1,5},{5... | collective-permute-start | bytes 393224 | tf_op jit(solution)/shard_map/ppermute | solution.py:349
  38.6 23.7 %collective-permute-start.25 = (bf16[96,1024]{1,0:T(8,128)(2,1)S(1)}, bf16[96,1024]{1,0:T(8,128)(2,1)S(1)}, u32[]{:S(2)}, u32[]{:S(2)}) collective-permute-start(bf16[96,1024]{1,0:T(8,128)(2,1)S(1)} %get-tuple-element.136), channel_id=1, source_target_pairs={{0,16},{4,20},{8,24},{12,28},{16,0},{20,4},{24,8},{28,12},{1,17},{... | collective-permute-start | bytes 589832 | tf_op jit(solution)/shard_map/ppermute | solution.py:349
  41.5 21.1 %collective-permute-start.7 = (bf16[96,1024]{1,0:T(8,128)(2,1)S(1)}, bf16[96,1024]{1,0:T(8,128)(2,1)S(1)}, u32[]{:S(2)}, u32[]{:S(2)}) collective-permute-start(bf16[96,1024]{1,0:T(8,128)(2,1)S(1)} %get-tuple-element.107), channel_id=1, source_target_pairs={{0,4},{4,0},{8,12},{12,8},{16,20},{20,16},{24,28},{28,24},{1,5},{5... | collective-permute-start | bytes 589832 | tf_op jit(solution)/shard_map/ppermute | solution.py:349
  43.5 19.1 %collective-permute-start.9 = (bf16[96,1024]{1,0:T(8,128)(2,1)S(1)}, bf16[96,1024]{1,0:T(8,128)(2,1)S(1)}, u32[]{:S(2)}, u32[]{:S(2)}) collective-permute-start(bf16[96,1024]{1,0:T(8,128)(2,1)S(1)} %get-tuple-element.110), channel_id=1, source_target_pairs={{0,8},{4,12},{8,0},{12,4},{16,24},{20,28},{24,16},{28,20},{1,9},{5... | collective-permute-start | bytes 589832 | tf_op jit(solution)/shard_map/ppermute | solution.py:349
  46.0 16.6 %collective-permute-start.13 = (bf16[96,1024]{1,0:T(8,128)(2,1)S(1)}, bf16[96,1024]{1,0:T(8,128)(2,1)S(1)}, u32[]{:S(2)}, u32[]{:S(2)}) collective-permute-start(bf16[96,1024]{1,0:T(8,128)(2,1)S(1)} %get-tuple-element.116), channel_id=1, source_target_pairs={{0,16},{4,20},{8,24},{12,28},{16,0},{20,4},{24,8},{28,12},{1,17},{... | collective-permute-start | bytes 589832 | tf_op jit(solution)/shard_map/ppermute | solution.py:349
  48.9 13.4 %collective-permute-start.18 = (bf16[64,1024]{1,0:T(8,128)(2,1)S(1)}, bf16[64,1024]{1,0:T(8,128)(2,1)S(1)}, u32[]{:S(2)}, u32[]{:S(2)}) collective-permute-start(bf16[64,1024]{1,0:T(8,128)(2,1)S(1)} %get-tuple-element.125), channel_id=1, source_target_pairs={{0,16},{4,20},{8,24},{12,28},{16,0},{20,4},{24,8},{28,12},{1,17},{... | collective-permute-start | bytes 393224 | tf_op jit(solution)/shard_map/ppermute | solution.py:349
  63.4 12.8 %all-to-all-start.1 = ((f32[32,1,128]{2,1,0:T(1,128)}), f32[32,1,128]{2,1,0:T(1,128)S(1)}, u32[]{:S(2)}, u32[]{:S(2)}) async-start(f32[32,1,128]{2,1,0:T(1,128)} %get-tuple-element.149), calls=%async_computation.1 | async-start | bytes 32768 | tf_op jit(solution)/shard_map/all_to_all | solution.py:374
